TPU v7x, 1024 devices: a whole 4x8x16 slice. The times are simulated.
1024 devices in a mesh: grid: 16 (over z), space: 32 (over x, y), spec: 2 (over core).
Axes of the slice: x: 4, y: 8, z: 16, core: 2. Of those that a mesh axis runs over, the one named last changes fastest.
Arguments:
- spectrum: float32 [16, 32, 36, 64, 128], P('grid', None, None, ('space', 'spec')), may hold values from 0.05 to 1
- land_sea: int32 [16, 64, 128], P('grid'), may hold values 0 or 1
- west_index: int32 [16, 64], P('grid'), may hold values from 0 to 63, each once within a row
- east_index: int32 [16, 64], P('grid'), may hold values from 0 to 63, each once within a row
- current_u: float32 [16, 64, 64, 128], P('grid', None, ('space', 'spec')), may hold values from -0.3 to 0.3
- current_v: float32 [16, 64, 64, 128], P('grid', None, ('space', 'spec')), may hold values from -0.3 to 0.3
- transfer: bfloat16 [1152, 1152], replicated, may hold values from -0.1875 to 0.1875
- wind_rate: float32 [36], replicated, may hold values from 0.1 to 1
- dissipation: float32 [36], replicated, may hold values from 0.5 to 4
Outputs:
- waves: float32 [16, 32, 36, 64, 128], P('grid', 'space', 'spec')
- stokes: float32 [16, 128, 64, 128], P('grid', None, ('space', 'spec'))
Inputs may be any that keep to these rules, and one draw needn't show every extreme that they name: `land_sea`: 1 marks a sea cell, 0 a land cell. `west_index`: row g lists, for each row of grid g, the row of grid g - 1 whose easternmost cell borders it; each row of the array is a permutation of the 64 rows. `east_index`: row g lists, for each row of grid g, the row of grid g + 1 whose westernmost cell borders it; each row of the array is a permutation of the 64 rows.
All inputs are finite; a program needn't handle non-finite values. No bound on the sum of `land_sea` on one device may be relied on, other than what follows from the above.
Results may differ from a plain program's by a relative error of at most 0.00082.
Values sent between devices are 32-bit elements; how exact they have to be, the bound alone decides.
No kernel may reach another device: no remote copies, remote signals or barrier semaphores. Data moves between devices by JAX's collectives and lax.ppermute only.
A program may use at most 64 MiB of HBM per device.

v0:
```python
import math

import jax
import jax.numpy as jnp
from jax import lax
from jax.sharding import PartitionSpec as P

sigma_base = 0.2199
gravity = 9.81
growth = 1.1
courant_scale = 3.0
time_step = 0.5
stokes_gain = 2.0
highest = lax.Precision.HIGHEST


def shifted(block, axis, distance):
    devices = range(lax.axis_size(axis))
    route = [(i - distance, i) for i in devices if i - distance in devices]
    return lax.ppermute(block, axis, route)


def tables(freq_count, directions, levels):
    freq_steps = jnp.arange(freq_count).astype(jnp.float32)
    radian_freq = sigma_base * growth**freq_steps
    wavenum = radian_freq * radian_freq / gravity
    speeds = courant_scale * growth ** (-freq_steps)
    angles = 2.0 * jnp.pi * jnp.arange(directions).astype(jnp.float32) / directions
    depths = -(jnp.arange(levels).astype(jnp.float32) + 0.5)
    decays = jnp.exp(2.0 * wavenum[:, None] * depths[None, :])
    current_weight = decays / jnp.sum(decays, axis=1, keepdims=True)
    drifts = (radian_freq * wavenum)[:, None] * decays
    drifts = drifts / jnp.sum(drifts, axis=0, keepdims=True)
    return (speeds, angles, current_weight, drifts)


def sweep_matrix(courant, length):
    forward = jnp.maximum(courant, 0.0)[..., None, None]
    backward = jnp.maximum(-courant, 0.0)[..., None, None]
    places = jnp.arange(length)
    offset = (places[:, None] - places[None, :]).astype(courant.dtype)
    lower_part = jnp.where(
        offset >= 0, (forward / (1.0 + forward)) ** jnp.maximum(offset, 0.0) / (1.0 + forward), 0.0
    )
    upper_part = jnp.where(
        offset <= 0,
        (backward / (1.0 + backward)) ** jnp.maximum(-offset, 0.0) / (1.0 + backward),
        0.0,
    )
    return lower_part + upper_part - jnp.eye(length, dtype=courant.dtype)


def sources(spectra, sea_points, transfer, wind_gain, damping):
    rounded = spectra.astype(jnp.bfloat16)
    redist = jnp.dot(transfer, rounded, preferred_element_type=jnp.float32)
    energy = jnp.mean(spectra * spectra, axis=0, keepdims=True)
    spectra = (
        sea_points
        * (spectra * (1.0 + time_step * wind_gain) + time_step * redist)
        / (1.0 + time_step * damping * energy)
    )
    return spectra


def propagate(
    wave_field, ghost_west, ghost_east, flow_field, sea_cells, sweep_cols, sweep_rows, courant_x
):
    flow_x = flow_field[0][None]
    flow_y = flow_field[1][None]
    west_cells = jnp.concatenate([ghost_west[..., None], wave_field[..., :-1]], axis=-1)
    east_cells = jnp.concatenate([wave_field[..., 1:], ghost_east[..., None]], axis=-1)
    blank_row = jnp.zeros_like(wave_field[..., :1, :])
    north_cells = jnp.concatenate([blank_row, wave_field[..., :-1, :]], axis=-2)
    south_cells = jnp.concatenate([wave_field[..., 1:, :], blank_row], axis=-2)
    moved = (
        wave_field
        - jnp.maximum(flow_x, 0.0) * (wave_field - west_cells)
        - jnp.maximum(-flow_x, 0.0) * (wave_field - east_cells)
        - jnp.maximum(flow_y, 0.0) * (wave_field - north_cells)
        - jnp.maximum(-flow_y, 0.0) * (wave_field - south_cells)
    )
    inflow_west = jnp.maximum(courant_x, 0.0)[..., None] * ghost_west
    inflow_east = jnp.maximum(-courant_x, 0.0)[..., None] * ghost_east
    moved = moved.at[..., 0].add(inflow_west).at[..., -1].add(inflow_east)
    swept = jnp.einsum("abij,abyj->abyi", sweep_cols, moved, precision=highest)
    swept = jnp.einsum("abij,abjx->abix", sweep_rows, swept, precision=highest)
    return sea_cells * swept


def neighbour(column, offset_by):
    return shifted(column, "grid", offset_by)


def to_cells(payload):
    return lax.all_to_all(payload, ("space", "spec"), split_axis=0, concat_axis=2, tiled=True)


def propagate_local(
    wave_field, west_order, east_order, flow_field, sea_cells, sweep_cols, sweep_rows, courant_x
):
    raw_west = neighbour(wave_field[..., -1], 1)
    raw_east = neighbour(wave_field[..., 0], -1)
    ghost_west = jnp.take(raw_west, west_order, axis=2)
    ghost_east = jnp.take(raw_east, east_order, axis=2)
    return propagate(
        wave_field, ghost_west, ghost_east, flow_field, sea_cells, sweep_cols, sweep_rows, courant_x
    )


def shards(
    spectrum,
    land_sea,
    west_index,
    east_index,
    current_u,
    current_v,
    transfer,
    wind_rate,
    dissipation,
):
    ranks = lax.axis_size("space")
    cores = lax.axis_size("spec")
    directions = spectrum.shape[1]
    freq_count = spectrum.shape[2]
    rows_local = spectrum.shape[3]
    columns = spectrum.shape[4]
    levels = current_u.shape[1]
    total_rows = land_sea.shape[1]
    dir_local = directions // ranks
    freq_local = freq_count // cores
    components = directions * freq_count
    points = rows_local * columns
    groups = ranks * cores
    space_rank = lax.axis_index("space")
    core_rank = lax.axis_index("spec")
    block_rank = space_rank * cores + core_rank
    speeds, angles, current_weight, drifts = tables(freq_count, directions, levels)
    own_freqs = core_rank * freq_local + jnp.arange(freq_local)
    own_dirs = space_rank * dir_local + jnp.arange(dir_local)
    own_speeds = courant_scale * growth ** (-own_freqs.astype(jnp.float32))
    own_angles = 2.0 * jnp.pi * own_dirs.astype(jnp.float32) / directions
    courant_x = own_speeds[None, :] * jnp.cos(own_angles)[:, None]
    courant_y = own_speeds[None, :] * jnp.sin(own_angles)[:, None]
    sweep_cols = sweep_matrix(courant_x, columns)
    sweep_rows = sweep_matrix(courant_y, total_rows)

    def to_blocks(spectra):
        shaped = spectra.reshape(ranks, dir_local, cores, freq_local, points)
        return shaped.transpose(0, 2, 1, 3, 4).reshape(groups, dir_local * freq_local, points)

    wind_gain = (0.5 * (1.0 + jnp.cos(angles))[:, None] * wind_rate[None, :]).reshape(components, 1)
    damping = jnp.broadcast_to(dissipation[None, :], (directions, freq_count)).reshape(
        components, 1
    )
    drift_x = (
        drifts.T[:, None, :]
        * (jnp.cos(angles) * stokes_gain / math.sqrt(directions))[None, :, None]
    )
    drift_y = (
        drifts.T[:, None, :]
        * (jnp.sin(angles) * stokes_gain / math.sqrt(directions))[None, :, None]
    )
    stokes_table = jnp.concatenate([drift_x, drift_y], 0).reshape(2 * levels, components)
    sea_cells = land_sea[0].astype(jnp.float32)
    sea_points = lax.dynamic_slice_in_dim(sea_cells, block_rank * rows_local, rows_local, 0)
    flow_points = jnp.stack(
        [
            jnp.dot(current_weight, current_u[0].reshape(levels, points), precision=highest),
            jnp.dot(current_weight, current_v[0].reshape(levels, points), precision=highest),
        ]
    )
    spectra = spectrum[0].reshape(components, points)
    spectra = sources(spectra, sea_points, transfer, wind_gain, damping)
    arrived = to_cells(to_blocks(spectra))
    gathered = lax.all_gather(
        flow_points.reshape(2 * freq_count, points), ("space", "spec"), axis=1, tiled=True
    )
    flow_cells = lax.dynamic_slice_in_dim(
        gathered.reshape(2, freq_count, total_rows * columns), core_rank * freq_local, freq_local, 1
    )
    flow_cells = flow_cells.reshape(2, freq_local, total_rows, columns)
    wave_field = arrived.reshape(dir_local, freq_local, total_rows, columns)
    wave_field = propagate_local(
        wave_field,
        west_index[0],
        east_index[0],
        flow_cells,
        sea_cells,
        sweep_cols,
        sweep_rows,
        courant_x,
    )
    shaped = wave_field.reshape(dir_local * freq_local, groups, points)
    returned = lax.all_to_all(shaped, ("space", "spec"), split_axis=1, concat_axis=0, tiled=True)
    shaped = returned.reshape(ranks, cores, dir_local, freq_local, points)
    spectra = sources(
        shaped.transpose(0, 2, 1, 3, 4).reshape(components, points),
        sea_points,
        transfer,
        wind_gain,
        damping,
    )
    stokes = jnp.dot(stokes_table, spectra, precision=highest)
    arrived = to_cells(to_blocks(spectra))
    wave_field = arrived.reshape(dir_local, freq_local, total_rows, columns)
    wave_field = propagate_local(
        wave_field,
        west_index[0],
        east_index[0],
        flow_cells,
        sea_cells,
        sweep_cols,
        sweep_rows,
        courant_x,
    )
    return (wave_field[None], stokes.reshape(1, 2 * levels, rows_local, columns))


def solution(mesh):
    placed = (
        P("grid", None, None, ("space", "spec"), None),
        P("grid", None, None),
        P("grid", None),
        P("grid", None),
        P("grid", None, ("space", "spec"), None),
        P("grid", None, ("space", "spec"), None),
        P(),
        P(),
        P(),
    )
    return jax.shard_map(
        shards,
        mesh=mesh,
        in_specs=placed,
        out_specs=(
            P("grid", "space", "spec", None, None),
            P("grid", None, ("space", "spec"), None),
        ),
        check_vma=False,
    )
```

profile of v0, /device:TPU:192, one launch (start us, length us, event | category | flops | bytes accessed | tf_op | source)
XLA Modules:
  0.0 259.1 jit_solution(14416072044689434050)
XLA Ops:
  8.0 1.2 convolution_bitcast_fusion
  9.2 1.0 convolution_bitcast_fusion.1
  10.9 0.8 convert_bitcast_fusion
  12.3 0.7 multiply_add_fusion
  13.3 2.3 multiply_reduce_fusion.1
  15.6 1.7 fusion.2
  17.3 2.1 reshape_transpose_reshape.9
  19.4 10.8 %all-to-all-start = ((f32[64,18,128]{2,1,0:T(8,128)}), f32[64,18,128]{2,1,0:T(8,128)}, u32[]{:S(2)}, u32[]{:S(2)}) async-start(f32[64,18,128]{2,1,0:T(8,128)} %reshape_transpose_reshape.9), calls=%async_computation | async-start | bytes 1572864 | tf_op jit(solution)/shard_map/all_to_all | solution.py:95
  38.0 15.4 %all-to-all-done = f32[64,18,128]{2,1,0:T(8,128)} async-done(((f32[64,18,128]{2,1,0:T(8,128)}), f32[64,18,128]{2,1,0:T(8,128)}, u32[]{:S(2)}, u32[]{:S(2)}) %all-to-all-start) | async-done | bytes 589856 | tf_op jit(solution)/shard_map/all_to_all | solution.py:95
  53.4 1.2 copy.301
  54.7 1.2 fusion.63
  55.9 1.6 copy.270
  57.4 5.6 %collective-permute-start = (f32[1,18,64]{1,2,0:T(8,128)S(1)}, f32[1,18,64]{1,2,0:T(8,128)S(1)}, u32[]{:S(2)}, u32[]{:S(2)}) collective-permute-start(f32[1,18,64]{1,2,0:T(8,128)S(1)} %bitcast.225), channel_id=1, source_target_pairs={{0,64},{64,128},{128,192},{192,256},{256,320},{320,384},{384,448},... | collective-permute-start | bytes 13832 | tf_op jit(solution)/shard_map/ppermute | solution.py:20
  63.1 1.1 fusion.61
  64.2 1.2 fusion.62
  65.3 1.6 copy.273
  66.9 1.9 collective-permute-start.1
  68.8 0.7 gather_fusion
  69.5 0.8 multiply_bitcast_fusion.3
  70.3 1.4 copy.237
  71.8 2.2 collective-permute-done.1
  74.7 1.4 copy.241
  76.2 1.5 copy.246
  77.7 1.5 copy.248
  79.2 30.0 %all-gather.2.cloned.1.call-done = f32[72,8192]{1,0:T(8,128)} async-done(((f32[72,128]{1,0:T(8,128)}), f32[72,8192]{1,0:T(8,128)}) %all-gather.2.cloned.1.call-update) | async-done | bytes 2359312 | tf_op jit(solution)/shard_map/all_gather | solution.py:175
  109.2 3.4 %reshape.656 = f32[2,36,8192]{2,1,0:T(8,128)} reshape(f32[72,8192]{1,0:T(8,128)} %all-gather.2.cloned.1.call-done) | data formatting | bytes 4718592 | tf_op jit(solution)/shard_map/reshape | solution.py:179
  112.5 1.9 negate_maximum_fusion
  117.6 1.9 fusion.14
  119.6 0.9 slice_add_fusion.3
  120.5 3.3 %scatter-add.14 = f32[1,18,64,128]{3,2,1,0:T(8,128)S(1)} dynamic-update-slice(f32[1,18,64,128]{3,2,1,0:T(8,128)S(1)} %fusion.14, f32[1,18,64,1]{3,2,1,0:T(8,128)} %slice_add_fusion.3, s32[]{:T(128)} %constant.169.clone.1, s32[]{:T(128)} %constant.169.clone.1, s32[]{:T(128)} %constant.169.clone.1, s32[]{:T(128)} %constant.169.clone.1) | dynamic-update-slice | bytes 9220 | tf_op jit(solution)/shard_map/scatter-add | solution.py:84
  123.8 2.1 fusion.9
  125.9 4.6 %scatter-add.15 = f32[18,64,128]{2,1,0:T(8,128)S(1)} dynamic-update-slice(f32[18,64,128]{2,1,0:T(8,128)S(1)} %bitcast.205, f32[18,64,1]{2,1,0:T(8,128)} %fusion.9, s32[]{:T(128)} %constant.169.clone.1, s32[]{:T(128)} %constant.169.clone.1, s32[]{:T(128)} %constant.177.clone.1) | dynamic-update-slice | bytes 9220 | tf_op jit(solution)/shard_map/scatter-add | solution.py:84
  130.7 5.9 %fusion.27 = f32[18,64,128]{2,1,0:T(8,128)S(1)} fusion(f32[18,64,128]{2,1,0:T(8,128)S(1)} %scatter-add.15, f32[128,128]{1,0:T(8,128)S(1)} %fusion.30, f32[18]{0:T(128)} %get-tuple-element.118, f32[128,128]{1,0:T(8,128)S(1)} %get-tuple-element.114, f32[18]{0:T(128)} %get-tuple-element.79, f32[18]{0:T(128)} %get-tuple-element.119, ...), kind=kOutput, calls=%fused_computation.59 | convolution fusion | flops 228261888 | bytes 1409312 | tf_op jit(solution)/shard_map/abij,abyj->abyi/dot_general | solution.py:85
  136.7 2.2 convolution_multiply_fusion.3
  139.2 30.9 %all_to_all.45 = f32[18,64,128]{2,0,1:T(8,128)S(1)} all-to-all(f32[18,64,128]{2,0,1:T(8,128)S(1)} %copy.250), channel_id=1, replica_groups=mesh['grid'=16,'space'=32,'spec'=2] {'space','spec'}, dimensions={1} | all-to-all | bytes 1179648 | tf_op jit(solution)/shard_map/all_to_all | solution.py:194
  170.1 0.9 reshape_transpose_reshape.10
  171.2 2.1 fusion.6
  173.4 1.1 reshape_transpose_reshape.11
  174.5 6.7 %all-to-all-start.2 = ((f32[64,18,128]{2,1,0:T(8,128)}), f32[64,18,128]{2,1,0:T(8,128)}, u32[]{:S(2)}, u32[]{:S(2)}) async-start(f32[64,18,128]{2,1,0:T(8,128)} %reshape_transpose_reshape.11), calls=%async_computation.2 | async-start | bytes 1572864 | tf_op jit(solution)/shard_map/all_to_all | solution.py:95
  181.4 0.9 mul.521
  182.7 1.4 broadcast_multiply_fusion.1
  184.2 1.9 fusion.22
  186.1 17.6 %all-to-all-done.2 = f32[64,18,128]{2,1,0:T(8,128)} async-done(((f32[64,18,128]{2,1,0:T(8,128)}), f32[64,18,128]{2,1,0:T(8,128)}, u32[]{:S(2)}, u32[]{:S(2)}) %all-to-all-start.2) | async-done | bytes 589856 | tf_op jit(solution)/shard_map/all_to_all | solution.py:95
  203.8 1.2 copy.300
  205.0 1.2 fusion.60
  206.2 1.1 fusion.58
  207.3 1.6 copy.280
  208.9 4.8 %collective-permute-start.2 = (f32[1,18,64]{1,2,0:T(8,128)S(1)}, f32[1,18,64]{1,2,0:T(8,128)S(1)}, u32[]{:S(2)}, u32[]{:S(2)}) collective-permute-start(f32[1,18,64]{1,2,0:T(8,128)S(1)} %bitcast.227), channel_id=1, source_target_pairs={{0,64},{64,128},{128,192},{192,256},{256,320},{320,384},{384,448},... | collective-permute-start | bytes 13832 | tf_op jit(solution)/shard_map/ppermute | solution.py:20
  213.6 1.2 fusion.59
  214.8 1.6 copy.283
  216.4 1.9 collective-permute-start.3
  218.3 0.7 gather_fusion.2
  219.1 1.4 copy.255
  220.5 2.8 %collective-permute-done.3 = f32[1,18,64]{1,2,0:T(8,128)S(1)} collective-permute-done((f32[1,18,64]{1,2,0:T(8,128)S(1)}, f32[1,18,64]{1,2,0:T(8,128)S(1)}, u32[]{:S(2)}, u32[]{:S(2)}) %collective-permute-start.3) | collective-permute-done | bytes 4640 | tf_op jit(solution)/shard_map/ppermute | solution.py:20
  224.2 1.5 copy.259
  225.6 1.5 copy.264
  227.2 3.5 %fusion.20 = f32[1,18,64,128]{3,2,1,0:T(8,128)S(1)} fusion(f32[1,18,64,127]{3,2,1,0:T(8,128)} %get-tuple-element.90, f32[1,18,64,1]{3,2,1,0:T(8,128)} %copy.255, f32[1,18,64,1]{3,2,1,0:T(8,128)} %copy.259, f32[1,18,64,127]{3,2,1,0:T(8,128)} %get-tuple-element.89, f32[1,18,63,128]{3,2,1,0:T(8,128)} %get-tuple-element.88, ...), kind=kLoop, calls=%fused_computation.47 | loop fusion | flops 2064384 | bytes 5879808 | tf_op jit(solution)/shard_map/sub | solution.py:76
  230.7 0.9 slice_add_fusion.1
  231.6 3.3 %scatter-add.16 = f32[1,18,64,128]{3,2,1,0:T(8,128)S(1)} dynamic-update-slice(f32[1,18,64,128]{3,2,1,0:T(8,128)S(1)} %fusion.20, f32[1,18,64,1]{3,2,1,0:T(8,128)} %slice_add_fusion.1, s32[]{:T(128)} %constant.169.clone.1, s32[]{:T(128)} %constant.169.clone.1, s32[]{:T(128)} %constant.169.clone.1, s32[]{:T(128)} %constant.169.clone.1) | dynamic-update-slice | bytes 9220 | tf_op jit(solution)/shard_map/scatter-add | solution.py:84
  234.9 1.4 copy.266
  236.4 2.1 fusion.8
  238.5 4.6 %scatter-add.19 = f32[18,64,128]{2,1,0:T(8,128)S(1)} dynamic-update-slice(f32[18,64,128]{2,1,0:T(8,128)S(1)} %bitcast.204, f32[18,64,1]{2,1,0:T(8,128)} %fusion.8, s32[]{:T(128)} %constant.169.clone.1, s32[]{:T(128)} %constant.169.clone.1, s32[]{:T(128)} %constant.177.clone.1) | dynamic-update-slice | bytes 9220 | tf_op jit(solution)/shard_map/scatter-add | solution.py:84
  243.3 5.9 %fusion.26 = f32[18,64,128]{2,1,0:T(8,128)S(1)} fusion(f32[18,64,128]{2,1,0:T(8,128)S(1)} %scatter-add.19, f32[128,128]{1,0:T(8,128)S(1)} %fusion.30, f32[18]{0:T(128)} %get-tuple-element.118, f32[128,128]{1,0:T(8,128)S(1)} %copy-done.17, f32[18]{0:T(128)} %get-tuple-element.79, f32[18]{0:T(128)} %get-tuple-element.119, f32[128,128]{1,0:T(8,128)S(1)} %copy-done.19, ...), kind=kOutput, calls=%fused_computation.58 | convolution fusion | flops 228261888 | bytes 1409312 | tf_op jit(solution)/shard_map/abij,abyj->abyi/dot_general | solution.py:85
  249.3 3.0 %fusion.7 = f32[1,1,18,64,128]{4,3,2,1,0:T(8,128)} fusion(f32[18,64,128]{2,1,0:T(8,128)S(1)} %fusion.26, f32[64,128]{1,0:T(8,128)S(1)} %get-tuple-element.107, f32[64,64]{1,0:T(8,128)S(1)} %copy-done.21, f32[18]{0:T(128)S(1)} %copy-done.54, f32[64,64]{1,0:T(8,128)S(1)} %copy-done.23, f32[18]{0:T(128)S(1)} %copy-done.52, f32[18]{0:T(128)S(1)} %copy-done.50, ...), kind=kOutput, calls=%fused_computation.15 | convolution fusion | flops 113836032 | bytes 1270048 | tf_op jit(solution)/shard_map/abij,abjx->abix/dot_general | solution.py:86
  (169 shorter events, 16.0 us)
Async XLA Ops:
  7.2 8.4 %copy-start = (bf16[1152,1152]{1,0:T(8,128)(2,1)S(1)}, bf16[1152,1152]{1,0:T(8,128)(2,1)}, u32[]{:S(2)}) copy-start(bf16[1152,1152]{1,0:T(8,128)(2,1)} %param.25) | copy-start | bytes 7962628
  7.2 8.4 %copy-start.15 = (f32[1,32,36,1,128]{4,3,2,1,0:T(1,128)S(1)}, f32[1,32,36,1,128]{4,3,2,1,0:T(1,128)}, u32[]{:S(2)}) copy-start(f32[1,32,36,1,128]{4,3,2,1,0:T(1,128)} %param.19) | copy-start | bytes 1769476
  7.2 102.0 %all-gather.2.cloned.1.call-start = ((), (), s32[]{:S(2)}) async-start(), calls=%async_computation.3 | async-start | bytes 2396160 | tf_op jit(solution)/shard_map/all_gather | solution.py:175
  7.3 1.9 copy-start.42
  7.3 2.9 %copy-start.44 = (f32[64]{0:T(128)}, f32[64]{0:T(128)S(1)}, u32[]{:S(2)}) copy-start(f32[64]{0:T(128)S(1)} %add_negate_fusion) | copy-start | bytes 772
  13.0 4.3 %copy-start.57 = (f32[128]{0:T(128)}, f32[128]{0:T(128)S(1)}, u32[]{:S(2)}) copy-start(f32[128]{0:T(128)S(1)} %fusion.46) | copy-start | bytes 1540
  13.2 4.2 %copy-start.31 = (f32[1152]{0:T(1024)}, f32[1152]{0:T(1024)S(1)}, u32[]{:S(2)}) copy-start(f32[1152]{0:T(1024)S(1)} %add.228) | copy-start | bytes 13828
  13.3 4.0 %copy-start.32 = (f32[1152]{0:T(1024)}, f32[1152]{0:T(1024)S(1)}, u32[]{:S(2)}) copy-start(f32[1152]{0:T(1024)S(1)} %mul.473) | copy-start | bytes 13828
  17.3 14.2 %copy-start.55 = (s32[1,64]{1,0:T(1,128)S(1)}, s32[1,64]{1,0:T(1,128)}, u32[]{:S(2)}) copy-start(s32[1,64]{1,0:T(1,128)} %param.21) | copy-start | bytes 772
  17.3 14.8 %copy-start.56 = (s32[1,64]{1,0:T(1,128)S(1)}, s32[1,64]{1,0:T(1,128)}, u32[]{:S(2)}) copy-start(s32[1,64]{1,0:T(1,128)} %param.22) | copy-start | bytes 772
  19.4 34.0 %all-to-all-start = ((f32[64,18,128]{2,1,0:T(8,128)}), f32[64,18,128]{2,1,0:T(8,128)}, u32[]{:S(2)}, u32[]{:S(2)}) async-start(f32[64,18,128]{2,1,0:T(8,128)} %reshape_transpose_reshape.9), calls=%async_computation | async-start | bytes 1572864 | tf_op jit(solution)/shard_map/all_to_all | solution.py:95
  31.0 24.9 %copy-start.29 = (f32[18]{0:T(128)}, f32[18]{0:T(128)S(1)}, u32[]{:S(2)}) copy-start(f32[18]{0:T(128)S(1)} %get-tuple-element.78) | copy-start | bytes 220
  31.5 24.4 %copy-start.26 = (f32[18]{0:T(128)}, f32[18]{0:T(128)S(1)}, u32[]{:S(2)}) copy-start(f32[18]{0:T(128)S(1)} %get-tuple-element.80) | copy-start | bytes 220
  35.8 94.8 %copy-start.16 = (f32[128,128]{1,0:T(8,128)}, f32[128,128]{1,0:T(8,128)S(1)}, u32[]{:S(2)}) copy-start(f32[128,128]{1,0:T(8,128)S(1)} %get-tuple-element.114) | copy-start | bytes 196612
  35.8 94.8 %copy-start.18 = (f32[128,128]{1,0:T(8,128)}, f32[128,128]{1,0:T(8,128)S(1)}, u32[]{:S(2)}) copy-start(f32[128,128]{1,0:T(8,128)S(1)} %get-tuple-element.115) | copy-start | bytes 196612
  57.4 11.4 %collective-permute-start = (f32[1,18,64]{1,2,0:T(8,128)S(1)}, f32[1,18,64]{1,2,0:T(8,128)S(1)}, u32[]{:S(2)}, u32[]{:S(2)}) collective-permute-start(f32[1,18,64]{1,2,0:T(8,128)S(1)} %bitcast.225), channel_id=1, source_target_pairs={{0,64},{64,128},{128,192},{192,256},{256,320},{320,384},{384,448},... | collective-permute-start | bytes 13832 | tf_op jit(solution)/shard_map/ppermute | solution.py:20
  65.3 9.3 %copy-start.27 = (f32[18]{0:T(128)S(1)}, f32[18]{0:T(128)}, u32[]{:S(2)}) copy-start(f32[18]{0:T(128)} %copy-done.26) | copy-start | bytes 220
  65.3 9.3 %copy-start.37 = (pred[64]{0:T(512)(128)(4,1)S(1)}, pred[64]{0:T(512)(128)(4,1)}, u32[]{:S(2)}) copy-start(pred[64]{0:T(512)(128)(4,1)} %compare_and_fusion) | copy-start | bytes 196
  66.9 7.0 %collective-permute-start.1 = (f32[1,18,64]{1,2,0:T(8,128)S(1)}, f32[1,18,64]{1,2,0:T(8,128)S(1)}, u32[]{:S(2)}, u32[]{:S(2)}) collective-permute-start(f32[1,18,64]{1,2,0:T(8,128)S(1)} %bitcast.226), channel_id=1, source_target_pairs={{64,0},{128,64},{192,128},{256,192},{320,256},{384,320},{448,384},... | collective-permute-start | bytes 13832 | tf_op jit(solution)/shard_map/ppermute | solution.py:20
  114.5 0.9 copy-start.1
  114.5 1.5 copy-start.10
  114.7 1.0 copy-start.2
  114.7 2.0 copy-start.7
  114.7 2.4 copy-start.8
  114.7 2.5 copy-start.9
  114.9 4.7 %copy-start.3 = (f32[3,8,64,128]{3,2,1,0:T(8,128)}, f32[3,8,64,128]{3,2,1,0:T(8,128)S(1)}, u32[]{:S(2)}) copy-start(f32[3,8,64,128]{3,2,1,0:T(8,128)S(1)} %copy.292) | copy-start | bytes 2359300
  114.9 2.6 copy-start.5
  114.9 2.7 %copy-start.6 = (f32[1,18,64,1]{3,2,1,0:T(8,128)S(1)}, f32[1,18,64,1]{3,2,1,0:T(8,128)}, u32[]{:S(2)}) copy-start(f32[1,18,64,1]{3,2,1,0:T(8,128)} %copy.241) | copy-start | bytes 13828
  115.1 4.5 %copy-start.4 = (f32[3,8,64,128]{3,2,1,0:T(8,128)}, f32[3,8,64,128]{3,2,1,0:T(8,128)S(1)}, u32[]{:S(2)}) copy-start(f32[3,8,64,128]{3,2,1,0:T(8,128)S(1)} %copy.293) | copy-start | bytes 2359300
  117.6 1.9 copy-start.11
  130.6 6.0 %copy-start.20 = (f32[64,64]{1,0:T(8,128)S(1)}, f32[64,64]{1,0:T(8,128)}, u32[]{:S(2)}) copy-start(f32[64,64]{1,0:T(8,128)} %fusion.31) | copy-start | bytes 49156
  130.6 6.0 %copy-start.22 = (f32[64,64]{1,0:T(8,128)S(1)}, f32[64,64]{1,0:T(8,128)}, u32[]{:S(2)}) copy-start(f32[64,64]{1,0:T(8,128)} %get-tuple-element.120) | copy-start | bytes 49156
  130.6 6.0 %copy-start.24 = (f32[64,64]{1,0:T(8,128)S(1)}, f32[64,64]{1,0:T(8,128)}, u32[]{:S(2)}) copy-start(f32[64,64]{1,0:T(8,128)} %get-tuple-element.121) | copy-start | bytes 49156
  130.6 6.0 %copy-start.33 = (pred[64,64]{1,0:T(8,128)(4,1)S(1)}, pred[64,64]{1,0:T(8,128)(4,1)}, u32[]{:S(2)}) copy-start(pred[64,64]{1,0:T(8,128)(4,1)} %get-tuple-element.122) | copy-start | bytes 12292
  130.6 6.0 %copy-start.35 = (pred[64,64]{1,0:T(8,128)(4,1)S(1)}, pred[64,64]{1,0:T(8,128)(4,1)}, u32[]{:S(2)}) copy-start(pred[64,64]{1,0:T(8,128)(4,1)} %get-tuple-element.123) | copy-start | bytes 12292
  130.6 6.0 %copy-start.47 = (f32[18]{0:T(128)S(1)}, f32[18]{0:T(128)}, u32[]{:S(2)}) copy-start(f32[18]{0:T(128)} %get-tuple-element.75) | copy-start | bytes 220
  130.6 6.0 %copy-start.49 = (f32[18]{0:T(128)S(1)}, f32[18]{0:T(128)}, u32[]{:S(2)}) copy-start(f32[18]{0:T(128)} %get-tuple-element.109) | copy-start | bytes 220
  130.6 6.0 %copy-start.51 = (f32[18]{0:T(128)S(1)}, f32[18]{0:T(128)}, u32[]{:S(2)}) copy-start(f32[18]{0:T(128)} %get-tuple-element.110) | copy-start | bytes 220
  130.6 6.0 %copy-start.53 = (f32[18]{0:T(128)S(1)}, f32[18]{0:T(128)}, u32[]{:S(2)}) copy-start(f32[18]{0:T(128)} %get-tuple-element.111) | copy-start | bytes 220
  173.4 1.1 copy-start.13
  173.4 7.8 %copy-start.41 = (f32[36]{0:T(128)S(1)}, f32[36]{0:T(128)}, u32[]{:S(2)}) copy-start(f32[36]{0:T(128)} %copy-done.40) | copy-start | bytes 436
  173.4 7.8 %copy-start.43 = (f32[36]{0:T(128)S(1)}, f32[36]{0:T(128)}, u32[]{:S(2)}) copy-start(f32[36]{0:T(128)} %copy-done.42) | copy-start | bytes 436
  173.4 7.8 %copy-start.45 = (f32[64]{0:T(128)S(1)}, f32[64]{0:T(128)}, u32[]{:S(2)}) copy-start(f32[64]{0:T(128)} %copy-done.44) | copy-start | bytes 772
  173.4 7.8 %copy-start.46 = (f32[64]{0:T(128)S(1)}, f32[64]{0:T(128)}, u32[]{:S(2)}) copy-start(f32[64]{0:T(128)} %get-tuple-element.73) | copy-start | bytes 772
  174.5 29.3 %all-to-all-start.2 = ((f32[64,18,128]{2,1,0:T(8,128)}), f32[64,18,128]{2,1,0:T(8,128)}, u32[]{:S(2)}, u32[]{:S(2)}) async-start(f32[64,18,128]{2,1,0:T(8,128)} %reshape_transpose_reshape.11), calls=%async_computation.2 | async-start | bytes 1572864 | tf_op jit(solution)/shard_map/all_to_all | solution.py:95
  182.3 1.9 copy-start.14
  208.9 10.2 %copy-start.30 = (f32[18]{0:T(128)S(1)}, f32[18]{0:T(128)}, u32[]{:S(2)}) copy-start(f32[18]{0:T(128)} %copy-done.29) | copy-start | bytes 220
  208.9 10.2 %copy-start.39 = (pred[64]{0:T(512)(128)(4,1)S(1)}, pred[64]{0:T(512)(128)(4,1)}, u32[]{:S(2)}) copy-start(pred[64]{0:T(512)(128)(4,1)} %compare_and_fusion.1) | copy-start | bytes 196
  208.9 9.4 %collective-permute-start.2 = (f32[1,18,64]{1,2,0:T(8,128)S(1)}, f32[1,18,64]{1,2,0:T(8,128)S(1)}, u32[]{:S(2)}, u32[]{:S(2)}) collective-permute-start(f32[1,18,64]{1,2,0:T(8,128)S(1)} %bitcast.227), channel_id=1, source_target_pairs={{0,64},{64,128},{128,192},{192,256},{256,320},{320,384},{384,448},... | collective-permute-start | bytes 13832 | tf_op jit(solution)/shard_map/ppermute | solution.py:20
  214.8 9.3 %copy-start.28 = (f32[18]{0:T(128)S(1)}, f32[18]{0:T(128)}, u32[]{:S(2)}) copy-start(f32[18]{0:T(128)} %copy-done.26) | copy-start | bytes 220
  214.8 9.3 %copy-start.38 = (pred[64]{0:T(512)(128)(4,1)S(1)}, pred[64]{0:T(512)(128)(4,1)}, u32[]{:S(2)}) copy-start(pred[64]{0:T(512)(128)(4,1)} %compare_and_fusion) | copy-start | bytes 196
  216.4 7.0 %collective-permute-start.3 = (f32[1,18,64]{1,2,0:T(8,128)S(1)}, f32[1,18,64]{1,2,0:T(8,128)S(1)}, u32[]{:S(2)}, u32[]{:S(2)}) collective-permute-start(f32[1,18,64]{1,2,0:T(8,128)S(1)} %bitcast.224), channel_id=1, source_target_pairs={{64,0},{128,64},{192,128},{256,192},{320,256},{384,320},{448,384},... | collective-permute-start | bytes 13832 | tf_op jit(solution)/shard_map/ppermute | solution.py:20
  227.1 3.6 %copy-start.12 = (f32[1,18,64,1]{3,2,1,0:T(8,128)S(1)}, f32[1,18,64,1]{3,2,1,0:T(8,128)}, u32[]{:S(2)}) copy-start(f32[1,18,64,1]{3,2,1,0:T(8,128)} %copy.264) | copy-start | bytes 13828
  236.4 6.8 %copy-start.17 = (f32[128,128]{1,0:T(8,128)S(1)}, f32[128,128]{1,0:T(8,128)}, u32[]{:S(2)}) copy-start(f32[128,128]{1,0:T(8,128)} %copy-done.16) | copy-start | bytes 196612
  236.4 6.8 %copy-start.19 = (f32[128,128]{1,0:T(8,128)S(1)}, f32[128,128]{1,0:T(8,128)}, u32[]{:S(2)}) copy-start(f32[128,128]{1,0:T(8,128)} %copy-done.18) | copy-start | bytes 196612
  243.2 6.0 %copy-start.21 = (f32[64,64]{1,0:T(8,128)S(1)}, f32[64,64]{1,0:T(8,128)}, u32[]{:S(2)}) copy-start(f32[64,64]{1,0:T(8,128)} %fusion.31) | copy-start | bytes 49156
  243.2 6.0 %copy-start.23 = (f32[64,64]{1,0:T(8,128)S(1)}, f32[64,64]{1,0:T(8,128)}, u32[]{:S(2)}) copy-start(f32[64,64]{1,0:T(8,128)} %get-tuple-element.120) | copy-start | bytes 49156
  243.2 6.0 %copy-start.25 = (f32[64,64]{1,0:T(8,128)S(1)}, f32[64,64]{1,0:T(8,128)}, u32[]{:S(2)}) copy-start(f32[64,64]{1,0:T(8,128)} %get-tuple-element.121) | copy-start | bytes 49156
  243.2 6.0 %copy-start.34 = (pred[64,64]{1,0:T(8,128)(4,1)S(1)}, pred[64,64]{1,0:T(8,128)(4,1)}, u32[]{:S(2)}) copy-start(pred[64,64]{1,0:T(8,128)(4,1)} %get-tuple-element.122) | copy-start | bytes 12292
  243.2 6.0 %copy-start.36 = (pred[64,64]{1,0:T(8,128)(4,1)S(1)}, pred[64,64]{1,0:T(8,128)(4,1)}, u32[]{:S(2)}) copy-start(pred[64,64]{1,0:T(8,128)(4,1)} %get-tuple-element.123) | copy-start | bytes 12292
  243.2 6.0 %copy-start.48 = (f32[18]{0:T(128)S(1)}, f32[18]{0:T(128)}, u32[]{:S(2)}) copy-start(f32[18]{0:T(128)} %get-tuple-element.75) | copy-start | bytes 220
  243.2 6.0 %copy-start.50 = (f32[18]{0:T(128)S(1)}, f32[18]{0:T(128)}, u32[]{:S(2)}) copy-start(f32[18]{0:T(128)} %get-tuple-element.109) | copy-start | bytes 220
  243.2 6.0 %copy-start.52 = (f32[18]{0:T(128)S(1)}, f32[18]{0:T(128)}, u32[]{:S(2)}) copy-start(f32[18]{0:T(128)} %get-tuple-element.110) | copy-start | bytes 220
  243.3 6.0 %copy-start.54 = (f32[18]{0:T(128)S(1)}, f32[18]{0:T(128)}, u32[]{:S(2)}) copy-start(f32[18]{0:T(128)} %get-tuple-element.111) | copy-start | bytes 220
  (1 other events, 0.7 us)
Sparse Core Ops, SparseCore 0:
  12.9 96.2 all-gather.1
where the time goes:
time: 261 us; the launch traced here: 259 us
  waiting for transfers between devices  68 us (26%)
  local copies, waits for them, and re-layouts  59.3 us (23%)
  starting transfers between devices  31.8 us (12%)
  blocking collectives  30.9 us (12%)
  other arithmetic  28.9 us (11%)
  matrix products  25 us (10%)
  between operations  15.2 us (6%)
    all_to_all x2, waiting for transfers between devices, to_cells(): lax.all_to_all(payload, ('space', 'spec'), split_axis=0, concat_axis=2, t...  33.1 us
    all_to_all x1, blocking collectives, shards(): lax.all_to_all(shaped, ('space', 'spec'), split_axis=1, concat_axis=0, ti...  30.9 us
    all_gather x1, waiting for transfers between devices, shards(): lax.all_gather(flow_points.reshape(2 * freq_count, points), ('space', 'sp...  30 us
    all_to_all x2, starting transfers between devices, to_cells(): lax.all_to_all(payload, ('space', 'spec'), split_axis=0, concat_axis=2, t...  17.5 us
    scatter-add x4, local copies, waits for them, and re-layouts, propagate(): moved = moved.at[..., 0].add(inflow_west).at[..., -1].add(inflow_east)  15.9 us
    ppermute x4, starting transfers between devices, shifted(): return lax.ppermute(block, axis, route)  14.2 us
    dot_general x2, matrix products, propagate(): swept = jnp.einsum('abij,abyj->abyi', sweep_cols, moved, precision=highest)  11.8 us
    another operation x4, local copies, waits for them, and re-layouts  5.99 us
  transfers between devices with their start and end apart: 7, of which 5 were waited for; matrix products, arithmetic and copies ran while one was open for 16% of the time, Pallas kernels for 0%

commit v1 on v0

v1 whole, which is shorter than its diff:
```python
import jax
import jax.numpy as jnp
import numpy as np
from jax import lax
from jax.experimental import pallas as pl
from jax.experimental.pallas import tpu as pltpu
from jax.sharding import PartitionSpec as P

ND, NF, LEV, NCOL, NROW = 32, 36, 64, 128, 64
COMPS = ND * NF
TILES = COMPS // 128
PLANE = ("space", "spec")
EVERY = ("grid", "space", "spec")
f32 = np.float32
highest = lax.Precision.HIGHEST
MSG = 20
VM = pl.BlockSpec(memory_space=pltpu.VMEM)
SM = pl.BlockSpec(memory_space=pltpu.SMEM)
INTERPRET = False


def host_tables():
    steps = np.arange(NF).astype(f32)
    radian = f32(0.2199) * f32(1.1) ** steps
    wave = radian * radian / f32(9.81)
    speeds = f32(3.0) * f32(1.1) ** (-steps)
    angles = f32(2.0 * np.pi) * np.arange(ND).astype(f32) / f32(ND)
    depths = -(np.arange(LEV).astype(f32) + f32(0.5))
    decays = np.exp(2.0 * wave[:, None].astype(np.float64) * depths[None, :])
    current = decays / decays.sum(1, keepdims=True)
    drifts = (radian * wave)[:, None] * decays
    drifts = drifts / drifts.sum(0, keepdims=True)
    cosines, sines = np.cos(angles), np.sin(angles)
    return speeds, cosines, sines, current, drifts


SPEEDS, COS, SIN, CURRENT, DRIFTS = host_tables()
CX = (COS[:, None] * SPEEDS[None, :]).astype(f32).reshape(-1)
CY = (SIN[:, None] * SPEEDS[None, :]).astype(f32).reshape(-1)


def scan_table(courant, block, extra):
    rows = []
    for part in (np.maximum(courant, 0), np.maximum(-courant, 0)):
        part = part.astype(np.float64)
        ratio = part / (1.0 + part)
        rows.append(1.0 / (1.0 + part))
        rows.extend(ratio**n for n in range(1, block + 1))
        rows.extend(ratio ** (block * n) for n in extra)
    rows.append(np.maximum(courant, 0))
    rows.append(np.maximum(-courant, 0))
    return np.stack(rows).astype(f32)


KX = scan_table(CX, 16, (2, 4))
KY = scan_table(CY, 8, (2, 4))
KY[-2:] = KX[-2:]
INFLOW = (KX.shape[0] - 2, KY.shape[0] - 2)
HAS = {
    name: [[bool((s * c[128 * k : 128 * k + 128] > 0).any()) for s in (1, -1)] for k in range(TILES)]
    for name, c in (("x", CX), ("y", CY))
}
FLOW_W = np.zeros((128, 2 * COMPS), f32)
FLOW_W[:LEV, :COMPS] = np.tile(CURRENT.T, (1, ND))
FLOW_W[LEV:, COMPS:] = np.tile(CURRENT.T, (1, ND))
GAIN = 2.0 / np.sqrt(float(ND))
STOKES_T = np.concatenate(
    [(DRIFTS.T[:, None, :] * (trig * GAIN)[None, :, None]).reshape(LEV, COMPS) for trig in (COS, SIN)]
).T.astype(f32)


def sweep_scalars():
    c = np.abs(CX.astype(np.float64)).reshape(ND, NF)
    ratio = c / (1 + c)
    cols = [1 / (1 + c), ratio] + [ratio**n for n in (2, 16, 32, 64)]
    cols += [np.zeros_like(c)] * 2
    table = np.stack(cols, -1).reshape(ND * 2, NF // 2, 8)
    return table.reshape(ND * 2, -1).astype(f32)


SWEEP = sweep_scalars()
AHEAD = (COS >= 0).astype(np.int32)


def down(x, first=None):
    top = jnp.zeros_like(x[:1]) if first is None else first
    return jnp.concatenate([top, x[:-1]], axis=0)


def up(x, last=None):
    end = jnp.zeros_like(x[:1]) if last is None else last
    return jnp.concatenate([x[1:], end], axis=0)


def hop(x, n, forward):
    z = jnp.zeros_like(x[:n])
    return jnp.concatenate([z, x[:-n]] if forward else [x[n:], z], axis=0)


def block_scan(tiles, table, base, lanes, forward):
    block = len(tiles)
    row = lambda n: table[pl.ds(base + n, 1), lanes]
    scale, ratio = row(0), row(1)
    order = list(range(block)) if forward else list(range(block - 1, -1, -1))
    out = [None] * block
    state = None
    for t in order:
        state = scale * tiles[t] if state is None else scale * tiles[t] + ratio * state
        out[t] = state
    ends = state
    ends = ends + row(block) * hop(ends, 1, forward)
    ends = ends + row(block + 1) * hop(ends, 2, forward)
    ends = ends + row(block + 2) * hop(ends, 4, forward)
    carry = hop(ends, 1, forward)
    for n, t in enumerate(order):
        out[t] = out[t] + row(n + 1) * carry
    return out


def sweep(tiles, table, k, has):
    lanes = pl.ds(128 * k, 128)
    size = len(tiles) + 3
    if has[0]:
        tiles = block_scan(tiles, table, 0, lanes, True)
    if has[1]:
        tiles = block_scan(tiles, table, size, lanes, False)
    return tiles


def source_step(spec_ref, transfer, wind, damp, sea_row, out_ref):
    spectra = spec_ref[...]
    redist = jnp.dot(transfer[...], spectra.astype(jnp.bfloat16), preferred_element_type=jnp.float32)
    energy = jnp.sum(spectra * spectra, axis=0, keepdims=True) * (1.0 / COMPS)
    turns = lax.broadcasted_iota(jnp.int32, (2 * NF, NF), 0)
    turns = jnp.where(turns >= NF, turns - NF, turns)
    pick = turns == lax.broadcasted_iota(jnp.int32, (2 * NF, NF), 1)
    wind_col = jnp.sum(jnp.where(pick, wind, 0.0), axis=1, keepdims=True)
    damp_col = jnp.sum(jnp.where(pick, damp, 0.0), axis=1, keepdims=True)
    shrink = sea_row / (1.0 + 0.5 * damp_col * energy)
    first = lax.broadcasted_iota(jnp.int32, (2 * NF, 1), 0) < NF
    for pair in range(ND // 2):
        rows = slice(2 * NF * pair, 2 * NF * (pair + 1))
        near, far = (float(0.25 * (1.0 + COS[2 * pair + n])) for n in range(2))
        gain = 1.0 + jnp.where(first, near, far) * wind_col
        out_ref[rows, :] = (spectra[rows] * gain + 0.5 * redist[rows]) * shrink


def rows_source(place, spec, transfer, wind, damp, land_sea, out, east, west, work):
    sea_row = land_sea[pl.ds(place[0], 1), :].astype(jnp.float32)
    source_step(spec, transfer, wind[...], damp[...], sea_row, work)
    for k in range(TILES):
        turned = work[128 * k : 128 * k + 128, :].T
        out[pl.ds(k, 128, stride=TILES), :] = turned
        west[pl.ds(k, 1), :] = turned[:1]
        east[pl.ds(k, 1), :] = turned[127:]


def flows(uv, weights, east_flow, north_flow):
    for k in range(TILES):
        for n, ref in ((0, east_flow), (TILES, north_flow)):
            lanes = slice(128 * (k + n), 128 * (k + n) + 128)
            ref[k] = jnp.dot(uv, weights[:, lanes], precision=highest, preferred_element_type=jnp.float32)


def rows_flow(u, v, weights, uv, east_flow, north_flow):
    turned = jnp.concatenate([u[...], v[...]], axis=0).T
    uv[...] = turned
    flows(turned, weights, east_flow, north_flow)


def advect(mid, west, east, north, south, a, b):
    return (
        mid
        - jnp.maximum(a, 0.0) * (mid - west)
        - jnp.maximum(-a, 0.0) * (mid - east)
        - jnp.maximum(b, 0.0) * (mid - north)
        - jnp.maximum(-b, 0.0) * (mid - south)
    )


def rows_move(place, spec, north, south, ghosts, east_flow, north_flow, uv, table, out):
    west_at, east_at = place[1], place[2]
    edge = lax.broadcasted_iota(jnp.int32, (8, 128), 0)
    for k in range(TILES):
        tile = lambda ref, t: ref[pl.ds(t * TILES + k, 8, stride=16 * TILES), :]
        flow = lambda ref, t: ref.at[k][pl.ds(t, 8, stride=16), :]
        ghost_west = ghosts[pl.ds(west_at * (2 * TILES) + k, 1), :]
        ghost_east = ghosts[pl.ds(east_at * (2 * TILES) + TILES + k, 1), :]
        mids = [tile(spec, t) for t in range(16)]
        moved = []
        for t in range(16):
            west = mids[t - 1] if t else down(mids[15], ghost_west)
            east = mids[t + 1] if t < 15 else up(mids[0], ghost_east)
            moved.append(
                advect(mids[t], west, east, tile(north, t), tile(south, t), flow(east_flow, t), flow(north_flow, t))
            )
        lanes = pl.ds(128 * k, 128)
        into_west = table[pl.ds(INFLOW[0], 1), lanes] * ghost_west
        into_east = table[pl.ds(INFLOW[0] + 1, 1), lanes] * ghost_east
        moved[0] = moved[0] + jnp.where(edge == 0, into_west, 0.0)
        moved[15] = moved[15] + jnp.where(edge == 7, into_east, 0.0)
        for t, value in enumerate(sweep(moved, table, k, HAS["x"][k])):
            out[pl.ds(t * (TILES + 1) + k, 8, stride=16 * (TILES + 1)), :] = value
    out[pl.ds(TILES, 128, stride=TILES + 1), :] = uv[...]


def columns_source(place, arrived, transfer, wind, damp, land_sea, table, near, far, sea, turned, held, work):
    lane = lax.broadcasted_iota(jnp.int32, (NROW, NCOL), 1)
    land = land_sea[...].astype(jnp.float32)
    for side in range(2):
        column = jnp.sum(jnp.where(lane == 2 * place[0] + side, land, 0.0), axis=1, keepdims=True)
        sea[NROW * side : NROW * (side + 1), :] = jnp.broadcast_to(column, (NROW, 128))
    for k in range(TILES):
        for side in range(2):
            tiles = [
                arrived[pl.ds((2 * s + side) * (TILES + 1) + k, 8, stride=16 * (TILES + 1)), :] for s in range(8)
            ]
            for s, value in enumerate(sweep(tiles, table, k, HAS["y"][k])):
                at = pl.ds(NROW * side + s, 8, stride=8)
                turned.at[k][at, :] = value * sea[at, :]
        held[128 * k : 128 * k + 128, :] = turned[k].T
    source_step(held, transfer, wind[...], damp[...], sea[...].T[:1], work)
    for k in range(TILES):
        back = work[128 * k : 128 * k + 128, :].T
        near[k] = back[:NROW]
        far[k] = back[NROW:]


def columns_flow(arrived, near, far, weights, stokes_table, east_flow, north_flow, stokes):
    uv = jnp.concatenate(
        [arrived[pl.ds(TILES + side * (TILES + 1), NROW, stride=MSG), :] for side in range(2)], axis=0
    )
    flows(uv, weights, east_flow, north_flow)
    total = jnp.zeros((128, 128), jnp.float32)
    for k in range(TILES):
        spectra = jnp.concatenate([near[k], far[k]], axis=0)
        total = total + jnp.dot(
            spectra, stokes_table[128 * k : 128 * k + 128, :], precision=highest, preferred_element_type=jnp.float32
        )
    stokes[...] = total


def columns_move(
    flags, near, far, from_west, from_east, pick_west, pick_east, east_flow, north_flow, stokes, table, out,
    west_halo, east_halo, held, turned,
):
    for k in range(TILES):
        west_halo[...] = jnp.dot(pick_west[...], from_west[k], precision=highest, preferred_element_type=jnp.float32)
        east_halo[...] = jnp.dot(pick_east[...], from_east[k], precision=highest, preferred_element_type=jnp.float32)
        lanes = pl.ds(128 * k, 128)
        into = [table[pl.ds(INFLOW[1] + n, 1), lanes] * flags[n] for n in range(2)]
        cells = [[ref.at[k][pl.ds(s, 8, stride=8), :] for s in range(8)] for ref in (near, far)]
        for side in range(2):
            halo = west_halo if side == 0 else east_halo
            moved = []
            for s in range(8):
                at = pl.ds(NROW * side + s, 8, stride=8)
                beyond = halo[pl.ds(s, 8, stride=8), :]
                mids = cells[side]
                north = mids[s - 1] if s else down(mids[7])
                south = mids[s + 1] if s < 7 else up(mids[0])
                west = beyond if side == 0 else cells[0][s]
                east = cells[1][s] if side == 0 else beyond
                value = advect(mids[s], west, east, north, south, east_flow.at[k][at, :], north_flow.at[k][at, :])
                moved.append(value + into[side] * beyond)
            for s, value in enumerate(sweep(moved, table, k, HAS["y"][k])):
                held[pl.ds(NROW * side + s, 8, stride=8), :] = value
        turned[128 * k : 128 * k + 128, :] = held[...].T
    half = NF // 2
    for i in range(half):
        out[pl.ds(i, 64, stride=MSG), :] = turned[pl.ds(i, 64, stride=half), :]
    for side in range(2):
        out[pl.ds(half + side, 64, stride=MSG), :] = stokes[NROW * side : NROW * (side + 1), :]


def comps_sweep(ahead, scalars, arrived, land_sea, waves, stokes, work, rows):
    half = NF // 2
    low = lax.broadcasted_iota(jnp.int32, (8, 128), 1) < NROW

    def solve(forward):
        for i in range(half):
            scale, ratio, ratio2, hop1, hop2, hop4 = (scalars[0, 8 * i + n] for n in range(6))
            tiles = [arrived[pl.ds(t * MSG + i, 8, stride=8 * MSG), :] * scale for t in range(8)]
            order = list(range(8)) if forward else list(range(7, -1, -1))
            state, states = None, {}
            for t in order:
                swapped = pltpu.roll(tiles[t], NROW, 1)
                a = tiles[t] + ratio * swapped
                b = swapped + ratio * tiles[t]
                pair = jnp.where(low, b, a) if forward else jnp.where(low, a, b)
                state = pair if state is None else pair + ratio2 * state
                states[t] = state
            ends = state
            ends = ends + hop1 * hop(ends, 1, forward)
            ends = ends + hop2 * hop(ends, 2, forward)
            ends = ends + hop4 * hop(ends, 4, forward)
            before = hop(ends, 1, forward)
            carry = before
            for t in order:
                carry = ratio2 * carry
                now = states[t] + carry
                other = tiles[t] + ratio * before
                value = jnp.where(low, other, now) if forward else jnp.where(low, now, other)
                work[pl.ds(NROW * i + t, 8, stride=8), :] = value
                before = now

    @pl.when(ahead[0] == 1)
    def _():
        solve(True)

    @pl.when(ahead[0] == 0)
    def _():
        solve(False)

    land = land_sea[...].astype(jnp.float32)
    which = lax.broadcasted_iota(jnp.int32, (128, 256), 0)
    there = lax.broadcasted_iota(jnp.int32, (128, 256), 1)
    spread = [
        (2 * jnp.where(which >= NROW, which - NROW, which) + side + jnp.where(which >= NROW, 128, 0) == there)
        .astype(jnp.float32)
        .astype(jnp.bfloat16)
        for side in range(2)
    ]
    for pair in range(half // 2):
        both = work[128 * pair : 128 * pair + 128, :].T
        total = jnp.zeros((NROW, 256), jnp.float32)
        for side in range(2):
            left = both[NROW * side : NROW * (side + 1)]
            for n in range(3):
                part = left.astype(jnp.bfloat16)
                total = total + jnp.dot(part, spread[side], preferred_element_type=jnp.float32)
                if n < 2:
                    left = left - part.astype(jnp.float32)
        for n in range(2):
            i = 2 * pair + n
            waves[NROW * i : NROW * (i + 1), :] = total[:, 128 * n : 128 * n + 128] * land
    for side in range(2):
        rows[pl.ds(side, 64, stride=2), :] = arrived[pl.ds(half + side, 64, stride=MSG), :]
    stokes[...] = rows[...].T


def kernel(body, outs, scratch, specs, flops, nbytes, name):
    return pl.pallas_call(
        body,
        out_shape=[jax.ShapeDtypeStruct(s, jnp.float32) for s in outs],
        in_specs=specs,
        out_specs=[VM] * len(outs),
        scratch_shapes=[pltpu.VMEM(s, jnp.float32) for s in scratch],
        compiler_params=pltpu.CompilerParams(vmem_limit_bytes=32 << 20),
        cost_estimate=pl.CostEstimate(flops=flops, bytes_accessed=nbytes, transcendentals=0),
        interpret=INTERPRET,
        name=name,
    )


def step(axis, by):
    size = lax.axis_size(axis)
    return [(i, i + by) for i in range(size) if 0 <= i + by < size]


def exchange(block, per):
    sent = block.reshape(64, per, 1, 128)
    got = lax.all_to_all(sent, PLANE, split_axis=0, concat_axis=0, tiled=True)
    return got.reshape(64 * per, 128)


def shards(spectrum, land_sea, west_index, east_index, current_u, current_v, transfer, wind_rate, dissipation):
    space = lax.axis_index("space")
    place = (space * 2 + lax.axis_index("spec")).astype(jnp.int32)
    spec = spectrum.reshape(COMPS, NCOL)
    sea = land_sea[0]
    wind, damp = wind_rate.reshape(1, NF), dissipation.reshape(1, NF)
    u, v = current_u.reshape(LEV, NCOL), current_v.reshape(LEV, NCOL)
    where = jnp.stack([place, west_index[0, place], east_index[0, place]])
    full, flow = (COMPS, 128), (TILES, 128, 128)

    rows, east, west = kernel(
        rows_source, [full, (TILES, 128), (TILES, 128)], [full], [SM] + [VM] * 5, 340_000_000, 4_000_000, "rows_source"
    )(where, spec, transfer, wind, damp, sea)
    uv, a_rows, b_rows = kernel(
        rows_flow, [(128, 128), flow, flow], [], [VM] * 3, 75_000_000, 2_500_000, "rows_flow"
    )(u, v, FLOW_W)
    from_west = lax.ppermute(east, "grid", step("grid", 1))
    from_east = lax.ppermute(west, "grid", step("grid", -1))
    north = lax.ppermute(rows, PLANE, step(PLANE, 1))
    south = lax.ppermute(rows, PLANE, step(PLANE, -1))
    edges = jnp.concatenate([from_west, from_east], axis=0)
    ghosts = exchange(jnp.broadcast_to(edges[None], (64, 2 * TILES, 128)), 2 * TILES)
    (sent,) = kernel(rows_move, [(64 * MSG, 128)], [], [SM] + [VM] * 8, 10_000_000, 5_000_000, "rows_move")(
        where, rows, north, south, ghosts, a_rows, b_rows, uv, KX
    )
    arrived = exchange(sent, MSG)

    half = (TILES, NROW, 128)
    near, far = kernel(
        columns_source,
        [half, half],
        [(128, 128), flow, full, full],
        [SM] + [VM] * 6,
        340_000_000,
        4_000_000,
        "columns_source",
    )(where, arrived, transfer, wind, damp, sea, KY)
    a_cols, b_cols, drift = kernel(
        columns_flow, [flow, flow, (128, 128)], [], [VM] * 5, 100_000_000, 4_000_000, "columns_flow"
    )(arrived, near, far, FLOW_W, STOKES_T)
    from_west = lax.ppermute(far, EVERY, step(EVERY, 1))
    from_east = lax.ppermute(near, EVERY, step(EVERY, -1))
    at_ends = jnp.stack([place == 0, place == 63])
    steady = jnp.arange(NROW, dtype=jnp.int32)
    picks = [
        (jnp.where(at_ends[n], index[0], steady)[:, None] == steady[None, :]).astype(jnp.float32)
        for n, index in enumerate((west_index, east_index))
    ]
    (sent,) = kernel(
        columns_move,
        [(64 * MSG, 128)],
        [(NROW, 128), (NROW, 128), (128, 128), full],
        [SM] + [VM] * 10,
        10_000_000,
        5_000_000,
        "columns_move",
    )(at_ends.astype(jnp.float32), near, far, from_west, from_east, *picks, a_cols, b_cols, drift, KY)
    arrived = exchange(sent, MSG)

    scalars = lax.dynamic_slice_in_dim(jnp.asarray(SWEEP), place, 1, 0)
    ahead = lax.dynamic_slice_in_dim(jnp.asarray(AHEAD), space, 1, 0)
    waves, stokes = kernel(
        comps_sweep,
        [full, (128, 128)],
        [full, (128, 128)],
        [SM, SM, VM, VM],
        100_000_000,
        2_000_000,
        "comps_sweep",
    )(ahead, scalars, arrived, sea)
    return waves.reshape(1, 1, NF // 2, NROW, NCOL), stokes.reshape(1, 2 * LEV, 1, NCOL)


def solution(mesh):
    rows = P("grid", None, None, PLANE, None)
    depth = P("grid", None, PLANE, None)
    return jax.shard_map(
        shards,
        mesh=mesh,
        in_specs=(rows, P("grid", None, None), P("grid", None), P("grid", None), depth, depth, P(), P(), P()),
        out_specs=(P("grid", "space", "spec", None, None), depth),
        check_vma=False,
    )
```

time: 261 us -> 150 us (0.57)
  the two profiles are of different devices: /device:TPU:192 before, /device:TPU:199 now
where the time goes in v1:
time: 150 us; the launch traced here: 149 us
  waiting for transfers between devices  58.8 us (39%)
  starting transfers between devices  52.7 us (35%)
  local copies, waits for them, and re-layouts  21 us (14%)
  Pallas kernels  14.2 us (9%)
  other arithmetic  1.52 us (1%)
    all_to_all x3, waiting for transfers between devices, exchange(): got = lax.all_to_all(sent, PLANE, split_axis=0, concat_axis=0, tiled=True)  38.5 us
    all_to_all x3, starting transfers between devices, exchange(): got = lax.all_to_all(sent, PLANE, split_axis=0, concat_axis=0, tiled=True)  35.9 us
    unnamed x64, local copies, waits for them, and re-layouts  17.2 us
    ppermute x1, waiting for transfers between devices, shards(): north = lax.ppermute(rows, PLANE, step(PLANE, 1))  11.1 us
    ppermute x1, starting transfers between devices, shards(): from_west = lax.ppermute(east, 'grid', step('grid', 1))  5.21 us
    ppermute x1, waiting for transfers between devices, shards(): from_east = lax.ppermute(near, EVERY, step(EVERY, -1))  4.31 us
    ppermute x1, waiting for transfers between devices, shards(): from_east = lax.ppermute(west, 'grid', step('grid', -1))  3.67 us
    ppermute x1, starting transfers between devices, shards(): north = lax.ppermute(rows, PLANE, step(PLANE, 1))  3.38 us
  transfers between devices with their start and end apart: 9, of which 6 were waited for; matrix products, arithmetic and copies ran while one was open for 1% of the time, Pallas kernels for 2%

profile of v1, /device:TPU:199, one launch (start us, length us, event | category | flops | bytes accessed | tf_op | source)
XLA Modules:
  0.0 149.1 jit_solution(7028480245898308898)
XLA Ops:
  0.6 0.0 copy-start.23
  0.6 1.3 constant_dynamic-slice_fusion
  2.0 1.3 pad_add_fusion.place
  3.3 1.7 %copy-done = bf16[1152,1152]{1,0:T(8,128)(2,1)S(1)} copy-done((bf16[1152,1152]{1,0:T(8,128)(2,1)S(1)}, bf16[1152,1152]{1,0:T(8,128)(2,1)}, u32[]{:S(2)}) %copy-start) | copy-done | bytes 2654232
  5.1 1.1 copy-done.7
  6.1 0.8 copy-done.20
  6.9 0.7 copy-done.25
  7.5 0.7 copy-done.27
  8.2 1.5 rows_source.1
  9.7 0.0 copy-start.9
  9.7 5.2 %collective-permute-start.2 = (f32[9,128]{1,0:T(8,128)S(1)}, f32[9,128]{1,0:T(8,128)S(1)}, u32[]{:S(2)}, u32[]{:S(2)}) collective-permute-start(f32[9,128]{1,0:T(8,128)S(1)} %get-tuple-element.16), channel_id=1, source_target_pairs={{0,64},{64,128},{128,192},{192,256},{256,320},{320,384},{384,448},... | collective-permute-start | bytes 13832 | tf_op jit(solution)/shard_map/ppermute | solution.py:383
  14.9 1.9 %collective-permute-start.3 = (f32[9,128]{1,0:T(8,128)S(1)}, f32[9,128]{1,0:T(8,128)S(1)}, u32[]{:S(2)}, u32[]{:S(2)}) collective-permute-start(f32[9,128]{1,0:T(8,128)S(1)} %get-tuple-element.17), channel_id=1, source_target_pairs={{64,0},{128,64},{192,128},{256,192},{320,256},{384,320},{448,384},... | collective-permute-start | bytes 13832 | tf_op jit(solution)/shard_map/ppermute | solution.py:384
  16.9 0.0 collective-permute-done.2
  16.9 3.7 %collective-permute-done.3 = f32[9,128]{1,0:T(8,128)S(1)} collective-permute-done((f32[9,128]{1,0:T(8,128)S(1)}, f32[9,128]{1,0:T(8,128)S(1)}, u32[]{:S(2)}, u32[]{:S(2)}) %collective-permute-start.3) | collective-permute-done | bytes 4640 | tf_op jit(solution)/shard_map/ppermute | solution.py:384
  20.5 1.1 reshape.63
  21.7 12.5 %all-to-all-start = ((f32[64,18,1,128]{3,2,1,0:T(1,128)}), f32[64,18,1,128]{3,2,1,0:T(1,128)S(1)}, u32[]{:S(2)}, u32[]{:S(2)}) async-start(f32[64,18,1,128]{3,2,1,0:T(1,128)} %reshape.63), calls=%async_computation | async-start | bytes 1179648 | tf_op jit(solution)/shard_map/all_to_all | solution.py:363
  34.2 3.4 %collective-permute-start = (f32[1152,128]{1,0:T(8,128)S(1)}, f32[1152,128]{1,0:T(8,128)S(1)}, u32[]{:S(2)}, u32[]{:S(2)}) collective-permute-start(f32[1152,128]{1,0:T(8,128)S(1)} %get-tuple-element.15.spec), channel_id=1, source_target_pairs={{0,1},{1,2},{2,3},{3,4},{4,5},{5,6},{6,7},{7,8},{8,9},{9,10},{10,1... | collective-permute-start | bytes 1769480 | tf_op jit(solution)/shard_map/ppermute | solution.py:385
  37.6 1.9 %collective-permute-start.1 = (f32[1152,128]{1,0:T(8,128)S(1)}, f32[1152,128]{1,0:T(8,128)S(1)}, u32[]{:S(2)}, u32[]{:S(2)}) collective-permute-start(f32[1152,128]{1,0:T(8,128)S(1)} %get-tuple-element.15.spec), channel_id=1, source_target_pairs={{1,0},{2,1},{3,2},{4,3},{5,4},{6,5},{7,6},{8,7},{9,8},{10,9},{11,1... | collective-permute-start | bytes 1769480 | tf_op jit(solution)/shard_map/ppermute | solution.py:386
  39.5 0.0 copy-done.23
  39.5 0.0 copy-done.2
  39.5 1.1 rows_flow.1
  40.7 0.8 copy-done.15
  41.5 0.8 copy-done.17
  42.3 11.1 %collective-permute-done.north = f32[1152,128]{1,0:T(8,128)S(1)} collective-permute-done((f32[1152,128]{1,0:T(8,128)S(1)}, f32[1152,128]{1,0:T(8,128)S(1)}, u32[]{:S(2)}, u32[]{:S(2)}) %collective-permute-start) | collective-permute-done | bytes 589856 | tf_op jit(solution)/shard_map/ppermute | solution.py:385
  53.5 0.8 copy-done.11
  54.3 1.1 collective-permute-done.1.south
  55.4 0.8 copy-done.13
  56.2 0.0 all-to-all-done
  56.2 0.8 copy-done.5
  57.1 1.1 copy-done.6
  58.1 1.1 copy-done.10
  59.2 1.1 copy-done.12
  60.3 1.1 copy-done.14
  61.3 1.1 copy-done.16
  62.4 1.1 copy-done.18
  63.5 0.9 copy-done.22
  64.4 0.0 copy-start.21
  64.4 0.0 copy-start.26
  64.4 0.0 copy-start.28
  64.4 2.0 %rows_move.1 = f32[1280,128]{1,0:T(8,128)S(1)} custom-call(s32[3]{0:T(128)S(1)} %pad_add_fusion.place, f32[1152,128]{1,0:T(8,128)S(1)} %copy-done.10, f32[1152,128]{1,0:T(8,128)S(1)} %copy-done.12, f32[1152,128]{1,0:T(8,128)S(1)} %copy-done.14, f32[1152,128]{1,0:T(8,128)S(1)} %bitcast.28, f32[9,128,128]{2,1,0:T(8,128)S(1)} %copy-done.16, ...), custom_call_target="tpu_custom_call" | custom-call | flops 10000000 | bytes 5000000 | tf_op jit(solution)/shard_map/rows_move/pallas_call | solution.py:389
  66.4 0.0 copy-start.4
  66.4 0.9 copy-done.4
  67.3 10.2 %all-to-all-start.1 = ((f32[64,20,1,128]{3,2,1,0:T(1,128)}), f32[64,20,1,128]{3,2,1,0:T(1,128)S(1)}, u32[]{:S(2)}, u32[]{:S(2)}) async-start(f32[64,20,1,128]{3,2,1,0:T(1,128)} %bitcast.27), calls=%async_computation.1 | async-start | bytes 1310720 | tf_op jit(solution)/shard_map/all_to_all | solution.py:363
  77.6 0.0 copy-done.30
  77.6 19.9 %all-to-all-done.1 = f32[64,20,1,128]{3,2,1,0:T(1,128)S(1)} async-done(((f32[64,20,1,128]{3,2,1,0:T(1,128)}), f32[64,20,1,128]{3,2,1,0:T(1,128)S(1)}, u32[]{:S(2)}, u32[]{:S(2)}) %all-to-all-start.1) | async-done | bytes 655392 | tf_op jit(solution)/shard_map/all_to_all | solution.py:363
  97.5 0.0 copy-done.19
  97.6 2.0 %columns_source.1 = (f32[9,64,128]{2,1,0:T(8,128)S(1)}, f32[9,64,128]{2,1,0:T(8,128)S(1)}) custom-call(s32[3]{0:T(128)S(1)} %pad_add_fusion.place, f32[1280,128]{1,0:T(8,128)S(1)} %bitcast.24, bf16[1152,1152]{1,0:T(8,128)(2,1)S(1)} %copy-done.1, f32[1,36]{1,0:T(1,128)S(1)} %bitcast.36, f32[1,36]{1,0:T(1,128)S(1)} %bitcast.38, s32[64,128]{1,0:T(8,128)S(1)} %bitcast.31, ...), custom_call_target="tpu_custom_call" | custom-call | flops 340000000 | bytes 4000000 | tf_op jit(solution)/shard_map/columns_source/pallas_call | solution.py:395
  99.5 2.4 %collective-permute-start.4 = (f32[9,64,128]{2,1,0:T(8,128)S(1)}, f32[9,64,128]{2,1,0:T(8,128)S(1)}, u32[]{:S(2)}, u32[]{:S(2)}) collective-permute-start(f32[9,64,128]{2,1,0:T(8,128)S(1)} %get-tuple-element.22.far), channel_id=1, source_target_pairs={{0,1},{1,2},{2,3},{3,4},{4,5},{5,6},{6,7},{7,8},{8,9},{9,10},{10,1... | collective-permute-start | bytes 884744 | tf_op jit(solution)/shard_map/ppermute | solution.py:407
  102.0 1.9 %collective-permute-start.5 = (f32[9,64,128]{2,1,0:T(8,128)S(1)}, f32[9,64,128]{2,1,0:T(8,128)S(1)}, u32[]{:S(2)}, u32[]{:S(2)}) collective-permute-start(f32[9,64,128]{2,1,0:T(8,128)S(1)} %get-tuple-element.21.near), channel_id=1, source_target_pairs={{1,0},{2,1},{3,2},{4,3},{5,4},{6,5},{7,6},{8,7},{9,8},{10,9},{11,1... | collective-permute-start | bytes 884744 | tf_op jit(solution)/shard_map/ppermute | solution.py:408
  103.9 0.1 add_convert_fusion.flags
  104.0 0.1 fusion
  104.0 0.0 copy-done.3
  104.1 0.0 copy-done.8
  104.1 1.6 %columns_flow.1 = (f32[9,128,128]{2,1,0:T(8,128)S(1)}, f32[9,128,128]{2,1,0:T(8,128)S(1)}, f32[128,128]{1,0:T(8,128)S(1)}) custom-call(f32[1280,128]{1,0:T(8,128)S(1)} %bitcast.25, f32[9,64,128]{2,1,0:T(8,128)S(1)} %get-tuple-element.21.near, f32[9,64,128]{2,1,0:T(8,128)S(1)} %get-tuple-element.22.far, f32[128,2304]{1,0:T(8,128)S(1)} %copy-done.3, ...), custom_call_target="tpu_custom_call" | custom-call | flops 100000000 | bytes 4000000 | tf_op jit(solution)/shard_map/columns_flow/pallas_call | solution.py:404
  105.7 0.0 copy-start.31
  105.7 0.0 collective-permute-done.4.from_west
  105.7 4.3 %collective-permute-done.5.from_east = f32[9,64,128]{2,1,0:T(8,128)S(1)} collective-permute-done((f32[9,64,128]{2,1,0:T(8,128)S(1)}, f32[9,64,128]{2,1,0:T(8,128)S(1)}, u32[]{:S(2)}, u32[]{:S(2)}) %collective-permute-start.5) | collective-permute-done | bytes 294944 | tf_op jit(solution)/shard_map/ppermute | solution.py:408
  110.0 2.8 %columns_move.1 = f32[1280,128]{1,0:T(8,128)} custom-call(f32[2]{0:T(128)S(1)} %add_convert_fusion.flags, f32[9,64,128]{2,1,0:T(8,128)S(1)} %get-tuple-element.21.near, f32[9,64,128]{2,1,0:T(8,128)S(1)} %get-tuple-element.22.far, f32[9,64,128]{2,1,0:T(8,128)S(1)} %collective-permute-done.4.from_west, f32[9,64,128]{2,1,0:T(8,128)S(1)} %collective-permute-done.5.from_east, ...), custom_call_target="tpu_custom_call" | custom-call | flops 10000000 | bytes 5000000 | tf_op jit(solution)/shard_map/columns_move/pallas_call | solution.py:415
  112.7 13.1 %all-to-all-start.2 = ((f32[64,20,1,128]{3,2,1,0:T(1,128)}), f32[64,20,1,128]{3,2,1,0:T(1,128)S(1)}, u32[]{:S(2)}, u32[]{:S(2)}) async-start(f32[64,20,1,128]{3,2,1,0:T(1,128)} %bitcast.16), calls=%async_computation.2 | async-start | bytes 1310720 | tf_op jit(solution)/shard_map/all_to_all | solution.py:363
  125.9 0.0 copy-done.31
  125.9 0.7 dynamic_slice.12.ahead
  126.6 0.7 constant_dynamic-slice_fusion.2.scalars
  127.3 18.6 %all-to-all-done.2 = f32[64,20,1,128]{3,2,1,0:T(1,128)S(1)} async-done(((f32[64,20,1,128]{3,2,1,0:T(1,128)}), f32[64,20,1,128]{3,2,1,0:T(1,128)S(1)}, u32[]{:S(2)}, u32[]{:S(2)}) %all-to-all-start.2) | async-done | bytes 655392 | tf_op jit(solution)/shard_map/all_to_all | solution.py:363
  145.9 3.2 %comps_sweep.1 = (f32[1152,128]{1,0:T(8,128)}, f32[128,128]{1,0:T(8,128)}) custom-call(s32[1]{0:T(128)} %dynamic_slice.12.ahead, f32[1,144]{1,0:T(1,128)S(1)} %constant_dynamic-slice_fusion.2.scalars, f32[1280,128]{1,0:T(8,128)S(1)} %bitcast.26, s32[64,128]{1,0:T(8,128)S(1)} %bitcast.32), custom_call_target="tpu_custom_call" | custom-call | flops 100000000 | bytes 2000000 | tf_op jit(solution)/shard_map/comps_sweep/pallas_call | solution.py:428
  (35 shorter events, 0.1 us)
Async XLA Ops:
  0.6 38.9 %copy-start.23 = (f32[1,64,1,128]{3,2,1,0:T(1,128)S(1)}, f32[1,64,1,128]{3,2,1,0:T(1,128)}, u32[]{:S(2)}) copy-start(f32[1,64,1,128]{3,2,1,0:T(1,128)} %param.19) | copy-start | bytes 98308
  3.3 1.8 %copy-start = (bf16[1152,1152]{1,0:T(8,128)(2,1)S(1)}, bf16[1152,1152]{1,0:T(8,128)(2,1)}, u32[]{:S(2)}) copy-start(bf16[1152,1152]{1,0:T(8,128)(2,1)} %transfer.3) | copy-start | bytes 7962628
  5.1 1.1 copy-start.7
  6.1 0.8 copy-start.20
  6.9 0.7 copy-start.25
  7.5 0.7 copy-start.27
  8.2 31.3 %copy-start.2 = (f32[128,2304]{1,0:T(8,128)S(1)}, f32[128,2304]{1,0:T(8,128)}, u32[]{:S(2)}) copy-start(f32[128,2304]{1,0:T(8,128)} %constant.30.clone.weights) | copy-start | bytes 3538948
  8.2 31.3 %copy-start.24 = (f32[1,64,1,128]{3,2,1,0:T(1,128)S(1)}, f32[1,64,1,128]{3,2,1,0:T(1,128)}, u32[]{:S(2)}) copy-start(f32[1,64,1,128]{3,2,1,0:T(1,128)} %param.20) | copy-start | bytes 98308
  9.7 47.4 %copy-start.9 = (f32[1152,128]{1,0:T(8,128)}, f32[1152,128]{1,0:T(8,128)S(1)}, u32[]{:S(2)}) copy-start(f32[1152,128]{1,0:T(8,128)S(1)} %get-tuple-element.15.spec) | copy-start | bytes 1769476
  9.7 7.1 %collective-permute-start.2 = (f32[9,128]{1,0:T(8,128)S(1)}, f32[9,128]{1,0:T(8,128)S(1)}, u32[]{:S(2)}, u32[]{:S(2)}) collective-permute-start(f32[9,128]{1,0:T(8,128)S(1)} %get-tuple-element.16), channel_id=1, source_target_pairs={{0,64},{64,128},{128,192},{192,256},{256,320},{320,384},{384,448},... | collective-permute-start | bytes 13832 | tf_op jit(solution)/shard_map/ppermute | solution.py:383
  14.9 5.6 %collective-permute-start.3 = (f32[9,128]{1,0:T(8,128)S(1)}, f32[9,128]{1,0:T(8,128)S(1)}, u32[]{:S(2)}, u32[]{:S(2)}) collective-permute-start(f32[9,128]{1,0:T(8,128)S(1)} %get-tuple-element.17), channel_id=1, source_target_pairs={{64,0},{128,64},{192,128},{256,192},{320,256},{384,320},{448,384},... | collective-permute-start | bytes 13832 | tf_op jit(solution)/shard_map/ppermute | solution.py:384
  21.7 34.6 %all-to-all-start = ((f32[64,18,1,128]{3,2,1,0:T(1,128)}), f32[64,18,1,128]{3,2,1,0:T(1,128)S(1)}, u32[]{:S(2)}, u32[]{:S(2)}) async-start(f32[64,18,1,128]{3,2,1,0:T(1,128)} %reshape.63), calls=%async_computation | async-start | bytes 1179648 | tf_op jit(solution)/shard_map/all_to_all | solution.py:363
  34.2 19.3 %collective-permute-start = (f32[1152,128]{1,0:T(8,128)S(1)}, f32[1152,128]{1,0:T(8,128)S(1)}, u32[]{:S(2)}, u32[]{:S(2)}) collective-permute-start(f32[1152,128]{1,0:T(8,128)S(1)} %get-tuple-element.15.spec), channel_id=1, source_target_pairs={{0,1},{1,2},{2,3},{3,4},{4,5},{5,6},{6,7},{7,8},{8,9},{9,10},{10,1... | collective-permute-start | bytes 1769480 | tf_op jit(solution)/shard_map/ppermute | solution.py:385
  37.6 17.9 %collective-permute-start.1 = (f32[1152,128]{1,0:T(8,128)S(1)}, f32[1152,128]{1,0:T(8,128)S(1)}, u32[]{:S(2)}, u32[]{:S(2)}) collective-permute-start(f32[1152,128]{1,0:T(8,128)S(1)} %get-tuple-element.15.spec), channel_id=1, source_target_pairs={{1,0},{2,1},{3,2},{4,3},{5,4},{6,5},{7,6},{8,7},{9,8},{10,9},{11,1... | collective-permute-start | bytes 1769480 | tf_op jit(solution)/shard_map/ppermute | solution.py:386
  40.7 0.8 copy-start.15
  41.5 0.8 copy-start.17
  53.5 0.8 copy-start.11
  55.4 0.8 copy-start.13
  56.2 0.8 copy-start.5
  57.1 1.1 copy-start.6
  58.1 1.1 copy-start.10
  59.2 1.1 copy-start.12
  60.3 1.1 copy-start.14
  61.3 1.1 copy-start.16
  62.4 1.1 copy-start.18
  63.4 0.9 copy-start.22
  64.4 13.2 %copy-start.29 = (s32[1,64]{1,0:T(1,128)S(1)}, s32[1,64]{1,0:T(1,128)}, u32[]{:S(2)}) copy-start(s32[1,64]{1,0:T(1,128)} %param.18) | copy-start | bytes 772
  64.4 13.2 %copy-start.30 = (s32[1,64]{1,0:T(1,128)S(1)}, s32[1,64]{1,0:T(1,128)}, u32[]{:S(2)}) copy-start(s32[1,64]{1,0:T(1,128)} %param.17) | copy-start | bytes 772
  64.4 33.1 %copy-start.1 = (bf16[1152,1152]{1,0:T(8,128)(2,1)S(1)}, bf16[1152,1152]{1,0:T(8,128)(2,1)}, u32[]{:S(2)}) copy-start(bf16[1152,1152]{1,0:T(8,128)(2,1)} %transfer.3) | copy-start | bytes 7962628
  64.4 33.1 %copy-start.19 = (f32[24,1152]{1,0:T(8,128)S(1)}, f32[24,1152]{1,0:T(8,128)}, u32[]{:S(2)}) copy-start(f32[24,1152]{1,0:T(8,128)} %constant.32.clone.table) | copy-start | bytes 331780
  64.4 33.1 %copy-start.21 = (s32[1,64,128]{2,1,0:T(8,128)S(1)}, s32[1,64,128]{2,1,0:T(8,128)}, u32[]{:S(2)}) copy-start(s32[1,64,128]{2,1,0:T(8,128)} %param.16) | copy-start | bytes 98308
  64.4 33.1 %copy-start.26 = (f32[36]{0:T(128)S(1)}, f32[36]{0:T(128)}, u32[]{:S(2)}) copy-start(f32[36]{0:T(128)} %param.22) | copy-start | bytes 436
  64.4 33.1 %copy-start.28 = (f32[36]{0:T(128)S(1)}, f32[36]{0:T(128)}, u32[]{:S(2)}) copy-start(f32[36]{0:T(128)} %param.23) | copy-start | bytes 436
  66.4 0.9 copy-start.4
  67.3 30.2 %all-to-all-start.1 = ((f32[64,20,1,128]{3,2,1,0:T(1,128)}), f32[64,20,1,128]{3,2,1,0:T(1,128)S(1)}, u32[]{:S(2)}, u32[]{:S(2)}) async-start(f32[64,20,1,128]{3,2,1,0:T(1,128)} %bitcast.27), calls=%async_computation.1 | async-start | bytes 1310720 | tf_op jit(solution)/shard_map/all_to_all | solution.py:363
  97.5 6.5 %copy-start.3 = (f32[128,2304]{1,0:T(8,128)S(1)}, f32[128,2304]{1,0:T(8,128)}, u32[]{:S(2)}) copy-start(f32[128,2304]{1,0:T(8,128)} %constant.30.clone.weights) | copy-start | bytes 3538948
  97.5 6.5 %copy-start.8 = (f32[1152,128]{1,0:T(8,128)S(1)}, f32[1152,128]{1,0:T(8,128)}, u32[]{:S(2)}) copy-start(f32[1152,128]{1,0:T(8,128)} %constant.33.clone.stokes_table) | copy-start | bytes 1769476
  99.5 6.1 %collective-permute-start.4 = (f32[9,64,128]{2,1,0:T(8,128)S(1)}, f32[9,64,128]{2,1,0:T(8,128)S(1)}, u32[]{:S(2)}, u32[]{:S(2)}) collective-permute-start(f32[9,64,128]{2,1,0:T(8,128)S(1)} %get-tuple-element.22.far), channel_id=1, source_target_pairs={{0,1},{1,2},{2,3},{3,4},{4,5},{5,6},{6,7},{7,8},{8,9},{9,10},{10,1... | collective-permute-start | bytes 884744 | tf_op jit(solution)/shard_map/ppermute | solution.py:407
  102.0 8.0 %collective-permute-start.5 = (f32[9,64,128]{2,1,0:T(8,128)S(1)}, f32[9,64,128]{2,1,0:T(8,128)S(1)}, u32[]{:S(2)}, u32[]{:S(2)}) collective-permute-start(f32[9,64,128]{2,1,0:T(8,128)S(1)} %get-tuple-element.21.near), channel_id=1, source_target_pairs={{1,0},{2,1},{3,2},{4,3},{5,4},{6,5},{7,6},{8,7},{9,8},{10,9},{11,1... | collective-permute-start | bytes 884744 | tf_op jit(solution)/shard_map/ppermute | solution.py:408
  105.7 20.2 %copy-start.31 = (s32[32]{0:T(128)S(1)}, s32[32]{0:T(128)}, u32[]{:S(2)}) copy-start(s32[32]{0:T(128)} %constant.35.clone) | copy-start | bytes 388
  112.7 33.1 %all-to-all-start.2 = ((f32[64,20,1,128]{3,2,1,0:T(1,128)}), f32[64,20,1,128]{3,2,1,0:T(1,128)S(1)}, u32[]{:S(2)}, u32[]{:S(2)}) async-start(f32[64,20,1,128]{3,2,1,0:T(1,128)} %bitcast.16), calls=%async_computation.2 | async-start | bytes 1310720 | tf_op jit(solution)/shard_map/all_to_all | solution.py:363

commit v2 on v1

--- a/solution.py
+++ b/solution.py
@@ -5,6 +5,7 @@
 from jax.experimental import pallas as pl
 from jax.experimental.pallas import tpu as pltpu
 from jax.sharding import PartitionSpec as P
+
 
 ND, NF, LEV, NCOL, NROW = 32, 36, 64, 128, 64
 COMPS = ND * NF
@@ -16,6 +17,9 @@
 MSG = 20
 VM = pl.BlockSpec(memory_space=pltpu.VMEM)
 SM = pl.BlockSpec(memory_space=pltpu.SMEM)
+FETCH = pl.BlockSpec(memory_space=pl.ANY)
+TILED = object()
+EDGE = 19
 INTERPRET = False
 
 
@@ -60,9 +64,8 @@
     name: [[bool((s * c[128 * k : 128 * k + 128] > 0).any()) for s in (1, -1)] for k in range(TILES)]
     for name, c in (("x", CX), ("y", CY))
 }
-FLOW_W = np.zeros((128, 2 * COMPS), f32)
-FLOW_W[:LEV, :COMPS] = np.tile(CURRENT.T, (1, ND))
-FLOW_W[LEV:, COMPS:] = np.tile(CURRENT.T, (1, ND))
+FLOW_W = np.tile(CURRENT.T, (2, ND)).astype(f32)
+FLOW_W = np.ascontiguousarray(FLOW_W.reshape(128, TILES, 128).transpose(1, 0, 2))
 GAIN = 2.0 / np.sqrt(float(ND))
 STOKES_T = np.concatenate(
     [(DRIFTS.T[:, None, :] * (trig * GAIN)[None, :, None]).reshape(LEV, COMPS) for trig in (COS, SIN)]
@@ -78,6 +81,17 @@
     return table.reshape(ND * 2, -1).astype(f32)
 
 
+def fade_rows():
+    rows = []
+    for courant in (CX, -CX):
+        part = np.maximum(courant, 0).astype(np.float64)
+        rows.append(np.where(part > 0, np.log(np.maximum(part, 1e-30) / (1 + part)), -1e30))
+    rows.append(1 / (1 + np.abs(CX.astype(np.float64))))
+    return np.stack(rows).astype(f32)
+
+
+KY = np.concatenate([KY, fade_rows()])
+FADES = KY.shape[0] - 3
 SWEEP = sweep_scalars()
 AHEAD = (COS >= 0).astype(np.int32)
 
@@ -145,27 +159,28 @@
         out_ref[rows, :] = (spectra[rows] * gain + 0.5 * redist[rows]) * shrink
 
 
-def rows_source(place, spec, transfer, wind, damp, land_sea, out, east, west, work):
+def rows_source(place, spec, transfer, wind, damp, land_sea, u, out, spread, work, edges):
     sea_row = land_sea[pl.ds(place[0], 1), :].astype(jnp.float32)
+    turned = jnp.concatenate([u[...], u[...]], axis=0).T
+    low = lax.broadcasted_iota(jnp.int32, (1, 128), 1) < LEV
+    edges[pl.ds(2 * TILES, 1), :] = jnp.where(low, turned[:1], turned[127:])
     source_step(spec, transfer, wind[...], damp[...], sea_row, work)
     for k in range(TILES):
         turned = work[128 * k : 128 * k + 128, :].T
-        out[pl.ds(k, 128, stride=TILES), :] = turned
-        west[pl.ds(k, 1), :] = turned[:1]
-        east[pl.ds(k, 1), :] = turned[127:]
-
-
-def flows(uv, weights, east_flow, north_flow):
-    for k in range(TILES):
-        for n, ref in ((0, east_flow), (TILES, north_flow)):
-            lanes = slice(128 * (k + n), 128 * (k + n) + 128)
-            ref[k] = jnp.dot(uv, weights[:, lanes], precision=highest, preferred_element_type=jnp.float32)
-
-
-def rows_flow(u, v, weights, uv, east_flow, north_flow):
-    turned = jnp.concatenate([u[...], v[...]], axis=0).T
-    uv[...] = turned
-    flows(turned, weights, east_flow, north_flow)
+        out[k] = turned
+        edges[pl.ds(k, 1), :] = turned[127:]
+        edges[pl.ds(TILES + k, 1), :] = turned[:1]
+    for n in range(EDGE):
+        spread[pl.ds(n, NROW // 2, stride=EDGE), :] = jnp.broadcast_to(edges[pl.ds(n, 1), :], (NROW // 2, 128))
+
+
+def exact(a, b):
+    return jnp.dot(a, b, precision=highest, preferred_element_type=jnp.float32)
+
+
+def halves(pair):
+    low = lax.broadcasted_iota(jnp.int32, pair.shape, 1) < LEV
+    return jnp.where(low, pair, 0.0), jnp.where(low, 0.0, pair)
 
 
 def advect(mid, west, east, north, south, a, b):
@@ -178,48 +193,76 @@
     )
 
 
-def rows_move(place, spec, north, south, ghosts, east_flow, north_flow, uv, table, out):
-    west_at, east_at = place[1], place[2]
-    edge = lax.broadcasted_iota(jnp.int32, (8, 128), 0)
+def rows_move(u, v, table, weights, spec, north, south, out, east_flow, north_flow):
+    uv = jnp.concatenate([u.get()[...], v.get()[...]], axis=0).T
+    out[pl.ds(TILES, 128, stride=TILES + 1), :] = uv
+    both = jnp.concatenate(halves(uv), axis=0)
+    table = table.get()
     for k in range(TILES):
-        tile = lambda ref, t: ref[pl.ds(t * TILES + k, 8, stride=16 * TILES), :]
-        flow = lambda ref, t: ref.at[k][pl.ds(t, 8, stride=16), :]
-        ghost_west = ghosts[pl.ds(west_at * (2 * TILES) + k, 1), :]
-        ghost_east = ghosts[pl.ds(east_at * (2 * TILES) + TILES + k, 1), :]
-        mids = [tile(spec, t) for t in range(16)]
+        flow = exact(both, weights.get(k)[...])
+        east_flow[...] = flow[:128]
+        north_flow[...] = flow[128:]
+        tile = lambda ref, t: ref[pl.ds(t, 8, stride=16), :]
+        now, above, below = (ref.get(k) for ref in (spec, north, south))
+        mids = [tile(now, t) for t in range(16)]
         moved = []
         for t in range(16):
-            west = mids[t - 1] if t else down(mids[15], ghost_west)
-            east = mids[t + 1] if t < 15 else up(mids[0], ghost_east)
+            west = mids[t - 1] if t else down(mids[15])
+            east = mids[t + 1] if t < 15 else up(mids[0])
             moved.append(
-                advect(mids[t], west, east, tile(north, t), tile(south, t), flow(east_flow, t), flow(north_flow, t))
+                advect(mids[t], west, east, tile(above, t), tile(below, t), tile(east_flow, t), tile(north_flow, t))
             )
-        lanes = pl.ds(128 * k, 128)
-        into_west = table[pl.ds(INFLOW[0], 1), lanes] * ghost_west
-        into_east = table[pl.ds(INFLOW[0] + 1, 1), lanes] * ghost_east
-        moved[0] = moved[0] + jnp.where(edge == 0, into_west, 0.0)
-        moved[15] = moved[15] + jnp.where(edge == 7, into_east, 0.0)
         for t, value in enumerate(sweep(moved, table, k, HAS["x"][k])):
             out[pl.ds(t * (TILES + 1) + k, 8, stride=16 * (TILES + 1)), :] = value
-    out[pl.ds(TILES, 128, stride=TILES + 1), :] = uv[...]
-
-
-def columns_source(place, arrived, transfer, wind, damp, land_sea, table, near, far, sea, turned, held, work):
+
+
+def senders(core, axis):
+    n = lax.broadcasted_iota(jnp.int32, (NROW, NROW), axis)
+    half = NROW // 2
+    return jnp.where(n < half, 2 * n + core, 2 * (n - half) + 1 - core)
+
+
+def columns_source(
+    place, land_sea, wind, damp, table, index_west, index_east, west_own, west_other, east_own, east_other, ends_own,
+    ends_other, weights, arrived, transfer, near, far, sea, turned, held, work, inflow,
+):
     lane = lax.broadcasted_iota(jnp.int32, (NROW, NCOL), 1)
+    core = place[0] % 2
+    pick_row = (senders(core, 1) == lax.broadcasted_iota(jnp.int32, (NROW, NROW), 0)).astype(jnp.float32)
+    land_sea, table, index_west, index_east = (x.get() for x in (land_sea, table, index_west, index_east))
+    picks = [(index[...] == senders(core, 0)).astype(jnp.float32).T for index in (index_west, index_east)]
+    edges = [[x.get() for x in pair] for pair in ((west_own, west_other), (east_own, east_other))]
+    ends = jnp.concatenate([ends_own.get()[...], ends_other.get()[...]], axis=0)
+    arrived = arrived.get() if isinstance(arrived, Fetched) else arrived
     land = land_sea[...].astype(jnp.float32)
     for side in range(2):
         column = jnp.sum(jnp.where(lane == 2 * place[0] + side, land, 0.0), axis=1, keepdims=True)
         sea[NROW * side : NROW * (side + 1), :] = jnp.broadcast_to(column, (NROW, 128))
+    behind = (place[0] * 2).astype(jnp.float32)
+    ends = jnp.concatenate(halves(exact(pick_row, ends)), axis=0)
     for k in range(TILES):
+        lanes = pl.ds(128 * k, 128)
+        row = lambda n: table[pl.ds(n, 1), lanes]
+        flow = exact(ends, weights.get(k)[...])
+        fades = []
+        for n, (pick, pair, sign) in enumerate(zip(picks, edges, (1.0, -1.0))):
+            speed = jnp.maximum(sign * flow[NROW * n : NROW * (n + 1)], 0.0) + row(INFLOW[1] + n)
+            column = jnp.concatenate([ref[pl.ds(k, NROW // 2, stride=TILES), :] for ref in pair], axis=0)
+            inflow[NROW * n : NROW * (n + 1), :] = speed * exact(pick, column)
+            steps = [behind, behind + 1.0] if n == 0 else [NCOL - 1.0 - behind, NCOL - 2.0 - behind]
+            fades.append([row(FADES + 2) * jnp.exp(row(FADES + n) * count) for count in steps])
         for side in range(2):
             tiles = [
-                arrived[pl.ds((2 * s + side) * (TILES + 1) + k, 8, stride=16 * (TILES + 1)), :] for s in range(8)
+                arrived[pl.ds((2 * s + side) * (TILES + 1) + k, 8, stride=16 * (TILES + 1)), :]
+                + fades[0][side] * inflow[pl.ds(s, 8, stride=8), :]
+                + fades[1][side] * inflow[pl.ds(NROW + s, 8, stride=8), :]
+                for s in range(8)
             ]
             for s, value in enumerate(sweep(tiles, table, k, HAS["y"][k])):
                 at = pl.ds(NROW * side + s, 8, stride=8)
                 turned.at[k][at, :] = value * sea[at, :]
         held[128 * k : 128 * k + 128, :] = turned[k].T
-    source_step(held, transfer, wind[...], damp[...], sea[...].T[:1], work)
+    source_step(held, transfer.get(), wind.get()[...], damp.get()[...], sea[...].T[:1], work)
     for k in range(TILES):
         back = work[128 * k : 128 * k + 128, :].T
         near[k] = back[:NROW]
@@ -230,23 +273,31 @@
     uv = jnp.concatenate(
         [arrived[pl.ds(TILES + side * (TILES + 1), NROW, stride=MSG), :] for side in range(2)], axis=0
     )
-    flows(uv, weights, east_flow, north_flow)
+    both = jnp.concatenate(halves(uv), axis=0)
     total = jnp.zeros((128, 128), jnp.float32)
     for k in range(TILES):
+        flow = exact(both, weights[k])
+        east_flow[k] = flow[:128]
+        north_flow[k] = flow[128:]
         spectra = jnp.concatenate([near[k], far[k]], axis=0)
-        total = total + jnp.dot(
-            spectra, stokes_table[128 * k : 128 * k + 128, :], precision=highest, preferred_element_type=jnp.float32
-        )
+        total = total + exact(spectra, stokes_table[128 * k : 128 * k + 128, :])
     stokes[...] = total
 
 
 def columns_move(
-    flags, near, far, from_west, from_east, pick_west, pick_east, east_flow, north_flow, stokes, table, out,
+    place, near, far, from_west, from_east, index_west, index_east, east_flow, north_flow, stokes, table, out,
     west_halo, east_halo, held, turned,
 ):
+    at_end = [place[0] == 0, place[0] == NROW - 1]
+    flags = [jnp.where(end, 1.0, 0.0) for end in at_end]
+    across, along = (lax.broadcasted_iota(jnp.int32, (NROW, NROW), n) for n in (0, 1))
+    picks = [
+        (jnp.where(end, jnp.broadcast_to(index[...], (NROW, NROW)), along) == across).astype(jnp.float32).T
+        for end, index in zip(at_end, (index_west, index_east))
+    ]
     for k in range(TILES):
-        west_halo[...] = jnp.dot(pick_west[...], from_west[k], precision=highest, preferred_element_type=jnp.float32)
-        east_halo[...] = jnp.dot(pick_east[...], from_east[k], precision=highest, preferred_element_type=jnp.float32)
+        west_halo[...] = exact(picks[0], from_west[k])
+        east_halo[...] = exact(picks[1], from_east[k])
         lanes = pl.ds(128 * k, 128)
         into = [table[pl.ds(INFLOW[1] + n, 1), lanes] * flags[n] for n in range(2)]
         cells = [[ref.at[k][pl.ds(s, 8, stride=8), :] for s in range(8)] for ref in (near, far)]
@@ -339,18 +390,46 @@
     stokes[...] = rows[...].T
 
 
-def kernel(body, outs, scratch, specs, flops, nbytes, name):
+class Fetched:
+    def __init__(self, source, buffer, sem, tiled):
+        self.ref, self.tiled = buffer, tiled
+        if tiled:
+            parts = range(source.shape[0])
+            self.copies = [pltpu.make_async_copy(source.at[k], buffer.at[k], sem.at[k]) for k in parts]
+        else:
+            self.copies = [pltpu.make_async_copy(source, buffer, sem.at[0])]
+
+    def get(self, k=0):
+        self.copies[k].wait()
+        return self.ref.at[k] if self.tiled else self.ref
+
+
+def kernel(body, outs, scratch, specs, args, flops, nbytes, limit=60):
+    late = [n for n, spec in enumerate(specs) if spec is FETCH or spec is TILED]
+
+    def whole(*refs):
+        size = len(refs) - 2 * len(late)
+        refs, buffers, sems = list(refs[:size]), refs[size : size + len(late)], refs[size + len(late) :]
+        for at, buffer, sem in zip(late, buffers, sems):
+            refs[at] = Fetched(refs[at], buffer, sem, specs[at] is TILED)
+        for k in range(TILES):
+            for at in late:
+                if k < len(refs[at].copies):
+                    refs[at].copies[k].start()
+        body(*refs)
+
+    buffers = [pltpu.VMEM(args[at].shape, args[at].dtype) for at in late]
+    sems = [pltpu.SemaphoreType.DMA((TILES if specs[at] is TILED else 1,)) for at in late]
     return pl.pallas_call(
-        body,
+        whole if late else body,
         out_shape=[jax.ShapeDtypeStruct(s, jnp.float32) for s in outs],
-        in_specs=specs,
+        in_specs=[pl.BlockSpec(memory_space=pl.ANY) if spec is TILED else spec for spec in specs],
         out_specs=[VM] * len(outs),
-        scratch_shapes=[pltpu.VMEM(s, jnp.float32) for s in scratch],
-        compiler_params=pltpu.CompilerParams(vmem_limit_bytes=32 << 20),
+        scratch_shapes=[pltpu.VMEM(s, jnp.float32) for s in scratch] + buffers + sems,
+        compiler_params=pltpu.CompilerParams(vmem_limit_bytes=limit << 20),
         cost_estimate=pl.CostEstimate(flops=flops, bytes_accessed=nbytes, transcendentals=0),
         interpret=INTERPRET,
-        name=name,
-    )
+    )(*args)
 
 
 def step(axis, by):
@@ -358,82 +437,102 @@
     return [(i, i + by) for i in range(size) if 0 <= i + by < size]
 
 
-def exchange(block, per):
-    sent = block.reshape(64, per, 1, 128)
-    got = lax.all_to_all(sent, PLANE, split_axis=0, concat_axis=0, tiled=True)
-    return got.reshape(64 * per, 128)
-
-
-def shards(spectrum, land_sea, west_index, east_index, current_u, current_v, transfer, wind_rate, dissipation):
-    space = lax.axis_index("space")
-    place = (space * 2 + lax.axis_index("spec")).astype(jnp.int32)
+def exchange(block, per, axes=PLANE):
+    sent = block.reshape(lax.axis_size(axes), per, 1, 128)
+    got = lax.all_to_all(sent, axes, split_axis=0, concat_axis=0, tiled=True)
+    return got.reshape(-1, 128)
+
+
+def model(spectrum, land_sea, west_index, east_index, current_u, current_v, transfer, wind_rate, dissipation):
+    space = lax.axis_index("space").astype(jnp.int32)
+    place = space * 2 + lax.axis_index("spec").astype(jnp.int32)
+    at = place.reshape(1)
     spec = spectrum.reshape(COMPS, NCOL)
     sea = land_sea[0]
     wind, damp = wind_rate.reshape(1, NF), dissipation.reshape(1, NF)
     u, v = current_u.reshape(LEV, NCOL), current_v.reshape(LEV, NCOL)
-    where = jnp.stack([place, west_index[0, place], east_index[0, place]])
-    full, flow = (COMPS, 128), (TILES, 128, 128)
-
-    rows, east, west = kernel(
-        rows_source, [full, (TILES, 128), (TILES, 128)], [full], [SM] + [VM] * 5, 340_000_000, 4_000_000, "rows_source"
-    )(where, spec, transfer, wind, damp, sea)
-    uv, a_rows, b_rows = kernel(
-        rows_flow, [(128, 128), flow, flow], [], [VM] * 3, 75_000_000, 2_500_000, "rows_flow"
-    )(u, v, FLOW_W)
-    from_west = lax.ppermute(east, "grid", step("grid", 1))
-    from_east = lax.ppermute(west, "grid", step("grid", -1))
+    full, flow, half, square = (COMPS, 128), (TILES, 128, 128), (TILES, NROW, 128), (128, 128)
+    weights = jnp.asarray(FLOW_W)
+
+    rows, spread = kernel(
+        rows_source,
+        [flow, (NROW // 2 * EDGE, 128)],
+        [full, (24, 128)],
+        [SM, VM, VM, VM, VM, VM, VM],
+        [at, spec, transfer, wind, damp, sea, u],
+        340_000_000,
+        4_000_000,
+    )
     north = lax.ppermute(rows, PLANE, step(PLANE, 1))
     south = lax.ppermute(rows, PLANE, step(PLANE, -1))
-    edges = jnp.concatenate([from_west, from_east], axis=0)
-    ghosts = exchange(jnp.broadcast_to(edges[None], (64, 2 * TILES, 128)), 2 * TILES)
-    (sent,) = kernel(rows_move, [(64 * MSG, 128)], [], [SM] + [VM] * 8, 10_000_000, 5_000_000, "rows_move")(
-        where, rows, north, south, ghosts, a_rows, b_rows, uv, KX
+    own = exchange(spread, EDGE, "space").reshape(NROW // 2, EDGE, 1, 128)
+    (sent,) = kernel(
+        rows_move,
+        [(64 * MSG, 128)],
+        [square, square],
+        [FETCH, FETCH, FETCH, TILED, TILED, TILED, TILED],
+        [u, v, jnp.asarray(KX), weights, rows, north, south],
+        90_000_000,
+        5_000_000,
     )
     arrived = exchange(sent, MSG)
 
-    half = (TILES, NROW, 128)
+    def shifted(part, by):
+        size = lax.axis_size("grid")
+        chips = step("grid", by) if by else [(i, i) for i in range(size)]
+        cross = [(2 * i + 1 - core, 2 * j + core) for i, j in chips for core in range(2)]
+        same = lax.ppermute(part, "grid", chips) if by else part
+        other = lax.ppermute(part, ("grid", "spec"), cross)
+        return [x.reshape(-1, 128) for x in (same, other)]
+
+    edges = shifted(own[:, :TILES], 1) + shifted(own[:, TILES : 2 * TILES], -1) + shifted(own[:, 2 * TILES :], 0)
+
     near, far = kernel(
         columns_source,
         [half, half],
-        [(128, 128), flow, full, full],
-        [SM] + [VM] * 6,
-        340_000_000,
+        [square, flow, full, full, square],
+        [SM] + [FETCH] * 12 + [TILED, FETCH, FETCH],
+        [at, sea, wind, damp, jnp.asarray(KY), west_index, east_index, *edges, weights, arrived, transfer],
+        400_000_000,
+        7_000_000,
+        60,
+    )
+    a_cols, b_cols, drift = kernel(
+        columns_flow,
+        [flow, flow, square],
+        [],
+        [VM] * 5,
+        [arrived, near, far, weights, jnp.asarray(STOKES_T)],
+        100_000_000,
         4_000_000,
-        "columns_source",
-    )(where, arrived, transfer, wind, damp, sea, KY)
-    a_cols, b_cols, drift = kernel(
-        columns_flow, [flow, flow, (128, 128)], [], [VM] * 5, 100_000_000, 4_000_000, "columns_flow"
-    )(arrived, near, far, FLOW_W, STOKES_T)
+        32,
+    )
     from_west = lax.ppermute(far, EVERY, step(EVERY, 1))
     from_east = lax.ppermute(near, EVERY, step(EVERY, -1))
-    at_ends = jnp.stack([place == 0, place == 63])
-    steady = jnp.arange(NROW, dtype=jnp.int32)
-    picks = [
-        (jnp.where(at_ends[n], index[0], steady)[:, None] == steady[None, :]).astype(jnp.float32)
-        for n, index in enumerate((west_index, east_index))
-    ]
     (sent,) = kernel(
         columns_move,
         [(64 * MSG, 128)],
-        [(NROW, 128), (NROW, 128), (128, 128), full],
+        [(NROW, 128), (NROW, 128), square, full],
         [SM] + [VM] * 10,
+        [at, near, far, from_west, from_east, west_index, east_index, a_cols, b_cols, drift, jnp.asarray(KY)],
         10_000_000,
         5_000_000,
-        "columns_move",
-    )(at_ends.astype(jnp.float32), near, far, from_west, from_east, *picks, a_cols, b_cols, drift, KY)
+        32,
+    )
     arrived = exchange(sent, MSG)
 
     scalars = lax.dynamic_slice_in_dim(jnp.asarray(SWEEP), place, 1, 0)
     ahead = lax.dynamic_slice_in_dim(jnp.asarray(AHEAD), space, 1, 0)
     waves, stokes = kernel(
         comps_sweep,
-        [full, (128, 128)],
-        [full, (128, 128)],
+        [full, square],
+        [full, square],
         [SM, SM, VM, VM],
+        [ahead, scalars, arrived, sea],
         100_000_000,
         2_000_000,
-        "comps_sweep",
-    )(ahead, scalars, arrived, sea)
+        32,
+    )
     return waves.reshape(1, 1, NF // 2, NROW, NCOL), stokes.reshape(1, 2 * LEV, 1, NCOL)
 
 
@@ -441,7 +540,7 @@
     rows = P("grid", None, None, PLANE, None)
     depth = P("grid", None, PLANE, None)
     return jax.shard_map(
-        shards,
+        model,
         mesh=mesh,
         in_specs=(rows, P("grid", None, None), P("grid", None), P("grid", None), depth, depth, P(), P(), P()),
         out_specs=(P("grid", "space", "spec", None, None), depth),

time: 150 us -> 132 us (0.88)
  the two profiles are of different devices: /device:TPU:199 before, /device:TPU:1 now
where the time goes in v2:
time: 132 us
  starting transfers between devices  58.4 us (44%)
  waiting for transfers between devices  38.4 us (29%)
  Pallas kernels  25.9 us (20%)
  local copies, waits for them, and re-layouts  7.98 us (6%)
    all_to_all x3, starting transfers between devices, exchange(): got = lax.all_to_all(sent, axes, split_axis=0, concat_axis=0, tiled=True)  29.1 us
    pallas_call x6, Pallas kernels, kernel(): pl.pallas_call(whole if late else body, out_shape=[jax.ShapeDtypeStruct(s...  25.9 us
    all_to_all x3, waiting for transfers between devices, exchange(): got = lax.all_to_all(sent, axes, split_axis=0, concat_axis=0, tiled=True)  24.3 us
    ppermute x1, starting transfers between devices, model(): north = lax.ppermute(rows, PLANE, step(PLANE, 1))  10.7 us
    unnamed x42, local copies, waits for them, and re-layouts  6.62 us
    ppermute x1, waiting for transfers between devices, model(): north = lax.ppermute(rows, PLANE, step(PLANE, 1))  6.53 us
    ppermute x3, starting transfers between devices, shifted(): other = lax.ppermute(part, ('grid', 'spec'), cross)  5.65 us
    ppermute x2, starting transfers between devices, shifted(): same = lax.ppermute(part, 'grid', chips) if by else part  5.63 us
  transfers between devices with their start and end apart: 12, of which 7 were waited for; matrix products, arithmetic and copies ran while one was open for 1% of the time, Pallas kernels for 7%

profile of v2, /device:TPU:1, one launch (start us, length us, event | category | flops | bytes accessed | tf_op | source)
XLA Modules:
  0.0 131.7 jit_solution(14142690306917553565)
XLA Ops:
  0.6 3.8 %shard_map.158 = (f32[9,128,128]{2,1,0:T(8,128)}, f32[608,128]{1,0:T(8,128)}) custom-call(s32[1]{0:T(128)} %bitcast.place.refs_0_, f32[1152,128]{1,0:T(8,128)} %bitcast.31, bf16[1152,1152]{1,0:T(8,128)(2,1)} %refs_15_.1, f32[1,36]{1,0:T(1,128)} %bitcast.43, f32[1,36]{1,0:T(1,128)} %bitcast.45, s32[64,128]{1,0:T(8,128)} %bitcast.27, f32[64,128]{1,0:T(8,128)} %bitcast.37), custom_call_target="tpu_custom_call" | custom-call | flops 340000000 | bytes 4000000 | tf_op jit(solution)/shard_map/pallas_call | solution.py:423
  4.4 10.5 %all-to-all-start = ((f32[32,19,1,128]{3,2,1,0:T(1,128)}), f32[32,19,1,128]{3,2,1,0:T(1,128)S(1)}, u32[]{:S(2)}, u32[]{:S(2)}) async-start(f32[32,19,1,128]{3,2,1,0:T(1,128)} %bitcast.32), calls=%async_computation | async-start | bytes 622592 | tf_op jit(solution)/shard_map/all_to_all | solution.py:442
  14.9 10.7 %collective-permute-start.5 = (f32[9,128,128]{2,1,0:T(8,128)}, f32[9,128,128]{2,1,0:T(8,128)S(1)}, u32[]{:S(2)}, u32[]{:S(2)}) collective-permute-start(f32[9,128,128]{2,1,0:T(8,128)} %get-tuple-element.12.refs_4_), channel_id=1, source_target_pairs={{0,1},{1,2},{2,3},{3,4},{4,5},{5,6},{6,7},{7,8},{8,9},{9,10},{10,1... | collective-permute-start | bytes 1769480 | tf_op jit(solution)/shard_map/ppermute | solution.py:466
  25.6 1.9 %collective-permute-start.6 = (f32[9,128,128]{2,1,0:T(8,128)}, f32[9,128,128]{2,1,0:T(8,128)S(1)}, u32[]{:S(2)}, u32[]{:S(2)}) collective-permute-start(f32[9,128,128]{2,1,0:T(8,128)} %get-tuple-element.12.refs_4_), channel_id=1, source_target_pairs={{1,0},{2,1},{3,2},{4,3},{5,4},{6,5},{7,6},{8,7},{9,8},{10,9},{11,1... | collective-permute-start | bytes 1769480 | tf_op jit(solution)/shard_map/ppermute | solution.py:467
  27.5 6.5 %collective-permute-done.5.refs_5_ = f32[9,128,128]{2,1,0:T(8,128)S(1)} collective-permute-done((f32[9,128,128]{2,1,0:T(8,128)}, f32[9,128,128]{2,1,0:T(8,128)S(1)}, u32[]{:S(2)}, u32[]{:S(2)}) %collective-permute-start.5) | collective-permute-done | bytes 589856 | tf_op jit(solution)/shard_map/ppermute | solution.py:466
  34.1 2.9 %collective-permute-done.6.refs_6_ = f32[9,128,128]{2,1,0:T(8,128)S(1)} collective-permute-done((f32[9,128,128]{2,1,0:T(8,128)}, f32[9,128,128]{2,1,0:T(8,128)S(1)}, u32[]{:S(2)}, u32[]{:S(2)}) %collective-permute-start.6) | collective-permute-done | bytes 589856 | tf_op jit(solution)/shard_map/ppermute | solution.py:467
  37.0 0.0 copy-start.13
  37.0 0.0 copy-done.12
  37.0 0.8 copy-done.13
  37.8 7.5 %shard_map.159 = f32[1280,128]{1,0:T(8,128)} custom-call(f32[64,128]{1,0:T(8,128)} %bitcast.38, f32[64,128]{1,0:T(8,128)} %bitcast.41, f32[40,1152]{1,0:T(8,128)} %constant.29.clone.refs_2_, f32[9,128,128]{2,1,0:T(8,128)} %constant.28.clone.refs_3_.refs_13_.weights, f32[9,128,128]{2,1,0:T(8,128)} %get-tuple-element.12.refs_4_, f32[9,128,128]{2,1,0:T(8,128)} %copy-done.12, ...), custom_call_target="tpu_custom_call" | custom-call | flops 90000000 | bytes 5000000 | tf_op jit(solution)/shard_map/pallas_call | solution.py:423
  45.3 0.0 all-to-all-done
  45.3 10.2 %all-to-all-start.1 = ((f32[64,20,1,128]{3,2,1,0:T(1,128)}), f32[64,20,1,128]{3,2,1,0:T(1,128)S(1)}, u32[]{:S(2)}, u32[]{:S(2)}) async-start(f32[64,20,1,128]{3,2,1,0:T(1,128)} %bitcast.30), calls=%async_computation.1 | async-start | bytes 1310720 | tf_op jit(solution)/shard_map/all_to_all | solution.py:442
  55.5 0.0 copy-start.2
  55.5 0.0 copy-start.8
  55.6 1.4 %collective-permute-start.3 = (f32[32,9,1,128]{3,2,1,0:T(1,128)S(1)}, f32[32,9,1,128]{3,2,1,0:T(1,128)S(1)}, u32[]{:S(2)}, u32[]{:S(2)}) collective-permute-start(f32[32,9,1,128]{3,2,1,0:T(1,128)S(1)} %get-tuple-element.26), channel_id=1, source_target_pairs={{65,0},{64,1},{129,64},{128,65},{193,128},{192,129},{257,192},{256... | collective-permute-start | bytes 442376 | tf_op jit(solution)/shard_map/ppermute | solution.py:485
  57.0 4.3 %collective-permute-start = (f32[32,9,1,128]{3,2,1,0:T(1,128)S(1)}, f32[32,9,1,128]{3,2,1,0:T(1,128)S(1)}, u32[]{:S(2)}, u32[]{:S(2)}) collective-permute-start(f32[32,9,1,128]{3,2,1,0:T(1,128)S(1)} %get-tuple-element.27), channel_id=1, source_target_pairs={{0,64},{64,128},{128,192},{192,256},{256,320},{320,384},{384,448},... | collective-permute-start | bytes 442376 | tf_op jit(solution)/shard_map/ppermute | solution.py:484
  61.3 1.9 %collective-permute-start.1 = (f32[32,9,1,128]{3,2,1,0:T(1,128)S(1)}, f32[32,9,1,128]{3,2,1,0:T(1,128)S(1)}, u32[]{:S(2)}, u32[]{:S(2)}) collective-permute-start(f32[32,9,1,128]{3,2,1,0:T(1,128)S(1)} %get-tuple-element.27), channel_id=1, source_target_pairs={{1,64},{0,65},{65,128},{64,129},{129,192},{128,193},{193,256},{192... | collective-permute-start | bytes 442376 | tf_op jit(solution)/shard_map/ppermute | solution.py:485
  63.2 1.3 collective-permute-start.2
  64.5 0.0 copy-start.18
  64.5 2.4 %collective-permute-start.4 = (f32[32,1,1,128]{3,0,2,1:T(8,128)S(1)}, f32[32,1,1,128]{3,0,2,1:T(8,128)S(1)}, u32[]{:S(2)}, u32[]{:S(2)}) collective-permute-start(f32[32,1,1,128]{3,0,2,1:T(8,128)S(1)} %bitcast.39), channel_id=1, source_target_pairs={{1,0},{0,1},{65,64},{64,65},{129,128},{128,129},{193,192},{192,193... | collective-permute-start | bytes 49160 | tf_op jit(solution)/shard_map/ppermute | solution.py:485
  66.9 0.8 collective-permute-done.4
  67.7 0.0 copy-start.19
  67.7 0.0 collective-permute-done.3
  67.7 0.0 copy-start.14
  67.7 0.0 collective-permute-done
  67.7 0.0 copy-start.15
  67.8 0.0 collective-permute-done.1
  67.8 0.0 copy-start.16
  67.8 2.3 %collective-permute-done.2 = f32[32,9,1,128]{3,2,1,0:T(1,128)S(1)} collective-permute-done((f32[32,9,1,128]{3,2,1,0:T(1,128)S(1)}, f32[32,9,1,128]{3,2,1,0:T(1,128)S(1)}, u32[]{:S(2)}, u32[]{:S(2)}) %collective-permute-start.2) | collective-permute-done | bytes 147488 | tf_op jit(solution)/shard_map/ppermute | solution.py:484
  70.1 5.5 %all-to-all-done.1 = f32[64,20,1,128]{3,2,1,0:T(1,128)S(1)} async-done(((f32[64,20,1,128]{3,2,1,0:T(1,128)}), f32[64,20,1,128]{3,2,1,0:T(1,128)S(1)}, u32[]{:S(2)}, u32[]{:S(2)}) %all-to-all-start.1) | async-done | bytes 655392 | tf_op jit(solution)/shard_map/all_to_all | solution.py:442
  75.6 0.0 copy-done.18
  75.6 0.0 copy-done.19
  75.6 0.0 copy-done.14
  75.6 0.0 copy-done.15
  75.6 0.0 copy-done.16
  75.6 0.0 copy-done.17
  75.6 0.8 copy-done
  76.4 7.7 %shard_map.160 = (f32[9,64,128]{2,1,0:T(8,128)}, f32[9,64,128]{2,1,0:T(8,128)}) custom-call(s32[1]{0:T(128)} %bitcast.place.refs_0_, s32[64,128]{1,0:T(8,128)} %bitcast.28, f32[1,36]{1,0:T(1,128)} %bitcast.44, f32[1,36]{1,0:T(1,128)} %bitcast.46, f32[27,1152]{1,0:T(8,128)} %constant.30.clone.refs_4_.table, s32[1,64]{1,0:T(1,128)} %index_west.1, ...), custom_call_target="tpu_custom_call" | custom-call | flops 400000000 | bytes 7000000 | tf_op jit(solution)/shard_map/pallas_call | solution.py:423
  84.2 3.4 %collective-permute-start.7 = (f32[9,64,128]{2,1,0:T(8,128)}, f32[9,64,128]{2,1,0:T(8,128)S(1)}, u32[]{:S(2)}, u32[]{:S(2)}) collective-permute-start(f32[9,64,128]{2,1,0:T(8,128)} %get-tuple-element.14.far), channel_id=1, source_target_pairs={{0,1},{1,2},{2,3},{3,4},{4,5},{5,6},{6,7},{7,8},{8,9},{9,10},{10,1... | collective-permute-start | bytes 884744 | tf_op jit(solution)/shard_map/ppermute | solution.py:510
  87.5 2.1 %collective-permute-start.8 = (f32[9,64,128]{2,1,0:T(8,128)}, f32[9,64,128]{2,1,0:T(8,128)S(1)}, u32[]{:S(2)}, u32[]{:S(2)}) collective-permute-start(f32[9,64,128]{2,1,0:T(8,128)} %get-tuple-element.13.near), channel_id=1, source_target_pairs={{1,0},{2,1},{3,2},{4,3},{5,4},{6,5},{7,6},{8,7},{9,8},{10,9},{11,1... | collective-permute-start | bytes 884744 | tf_op jit(solution)/shard_map/ppermute | solution.py:511
  89.6 0.0 copy-done.2
  89.6 0.0 copy-done.8
  89.6 0.0 copy-start.1
  89.7 1.1 copy-done.1
  90.7 1.0 copy-done.3
  91.7 1.0 copy-done.5
  92.7 1.5 %shard_map.161 = (f32[9,128,128]{2,1,0:T(8,128)S(1)}, f32[9,128,128]{2,1,0:T(8,128)S(1)}, f32[128,128]{1,0:T(8,128)S(1)}) custom-call(f32[1280,128]{1,0:T(8,128)S(1)} %bitcast.25, f32[9,64,128]{2,1,0:T(8,128)S(1)} %copy-done.3, f32[9,64,128]{2,1,0:T(8,128)S(1)} %copy-done.5, f32[9,128,128]{2,1,0:T(8,128)S(1)} %copy-done.2, f32[1152,128]{1,0:T(8,128)S(1)} %copy-done.8), custom_call_target="tpu_custom_call" | custom-call | flops 100000000 | bytes 4000000 | tf_op jit(solution)/shard_map/pallas_call | solution.py:423
  94.2 0.0 copy-start.20
  94.2 0.0 collective-permute-done.7.from_west
  94.2 1.5 %collective-permute-done.8.from_east = f32[9,64,128]{2,1,0:T(8,128)S(1)} collective-permute-done((f32[9,64,128]{2,1,0:T(8,128)}, f32[9,64,128]{2,1,0:T(8,128)S(1)}, u32[]{:S(2)}, u32[]{:S(2)}) %collective-permute-start.8) | collective-permute-done | bytes 294944 | tf_op jit(solution)/shard_map/ppermute | solution.py:511
  95.8 0.0 copy-done.7
  95.8 0.0 copy-done.10
  95.8 0.0 copy-done.11
  95.8 0.0 copy-start.4
  95.8 1.0 copy-done.4
  96.7 1.0 copy-done.6
  97.7 2.2 %shard_map.162 = f32[1280,128]{1,0:T(8,128)} custom-call(s32[1]{0:T(128)} %bitcast.place.refs_0_, f32[9,64,128]{2,1,0:T(8,128)S(1)} %copy-done.4, f32[9,64,128]{2,1,0:T(8,128)S(1)} %copy-done.6, f32[9,64,128]{2,1,0:T(8,128)S(1)} %collective-permute-done.7.from_west, f32[9,64,128]{2,1,0:T(8,128)S(1)} %collective-permute-done.8.from_east, ...), custom_call_target="tpu_custom_call" | custom-call | flops 10000000 | bytes 5000000 | tf_op jit(solution)/shard_map/pallas_call | solution.py:423
  99.9 8.4 %all-to-all-start.2 = ((f32[64,20,1,128]{3,2,1,0:T(1,128)}), f32[64,20,1,128]{3,2,1,0:T(1,128)S(1)}, u32[]{:S(2)}, u32[]{:S(2)}) async-start(f32[64,20,1,128]{3,2,1,0:T(1,128)} %bitcast.16), calls=%async_computation.2 | async-start | bytes 1310720 | tf_op jit(solution)/shard_map/all_to_all | solution.py:442
  108.3 0.0 copy-done.20
  108.3 0.6 dynamic_slice.6.ahead
  108.9 0.7 constant_dynamic-slice_fusion.scalars
  109.6 18.8 %all-to-all-done.2 = f32[64,20,1,128]{3,2,1,0:T(1,128)S(1)} async-done(((f32[64,20,1,128]{3,2,1,0:T(1,128)}), f32[64,20,1,128]{3,2,1,0:T(1,128)S(1)}, u32[]{:S(2)}, u32[]{:S(2)}) %all-to-all-start.2) | async-done | bytes 655392 | tf_op jit(solution)/shard_map/all_to_all | solution.py:442
  128.4 0.0 copy-done.9
  128.4 3.2 %shard_map.163 = (f32[1152,128]{1,0:T(8,128)}, f32[128,128]{1,0:T(8,128)}) custom-call(s32[1]{0:T(128)} %dynamic_slice.6.ahead, f32[1,144]{1,0:T(1,128)S(1)} %constant_dynamic-slice_fusion.scalars, f32[1280,128]{1,0:T(8,128)S(1)} %bitcast.26, s32[64,128]{1,0:T(8,128)S(1)} %bitcast.29), custom_call_target="tpu_custom_call" | custom-call | flops 100000000 | bytes 2000000 | tf_op jit(solution)/shard_map/pallas_call | solution.py:423
  (12 shorter events, 0.1 us)
Async XLA Ops:
  4.4 40.9 %all-to-all-start = ((f32[32,19,1,128]{3,2,1,0:T(1,128)}), f32[32,19,1,128]{3,2,1,0:T(1,128)S(1)}, u32[]{:S(2)}, u32[]{:S(2)}) async-start(f32[32,19,1,128]{3,2,1,0:T(1,128)} %bitcast.32), calls=%async_computation | async-start | bytes 622592 | tf_op jit(solution)/shard_map/all_to_all | solution.py:442
  14.9 19.2 %collective-permute-start.5 = (f32[9,128,128]{2,1,0:T(8,128)}, f32[9,128,128]{2,1,0:T(8,128)S(1)}, u32[]{:S(2)}, u32[]{:S(2)}) collective-permute-start(f32[9,128,128]{2,1,0:T(8,128)} %get-tuple-element.12.refs_4_), channel_id=1, source_target_pairs={{0,1},{1,2},{2,3},{3,4},{4,5},{5,6},{6,7},{7,8},{8,9},{9,10},{10,1... | collective-permute-start | bytes 1769480 | tf_op jit(solution)/shard_map/ppermute | solution.py:466
  25.6 11.4 %collective-permute-start.6 = (f32[9,128,128]{2,1,0:T(8,128)}, f32[9,128,128]{2,1,0:T(8,128)S(1)}, u32[]{:S(2)}, u32[]{:S(2)}) collective-permute-start(f32[9,128,128]{2,1,0:T(8,128)} %get-tuple-element.12.refs_4_), channel_id=1, source_target_pairs={{1,0},{2,1},{3,2},{4,3},{5,4},{6,5},{7,6},{8,7},{9,8},{10,9},{11,1... | collective-permute-start | bytes 1769480 | tf_op jit(solution)/shard_map/ppermute | solution.py:467
  34.1 3.0 %copy-start.12 = (f32[9,128,128]{2,1,0:T(8,128)}, f32[9,128,128]{2,1,0:T(8,128)S(1)}, u32[]{:S(2)}) copy-start(f32[9,128,128]{2,1,0:T(8,128)S(1)} %collective-permute-done.5.refs_5_) | copy-start | bytes 1769476
  37.0 0.8 copy-start.13
  45.3 30.3 %all-to-all-start.1 = ((f32[64,20,1,128]{3,2,1,0:T(1,128)}), f32[64,20,1,128]{3,2,1,0:T(1,128)S(1)}, u32[]{:S(2)}, u32[]{:S(2)}) async-start(f32[64,20,1,128]{3,2,1,0:T(1,128)} %bitcast.30), calls=%async_computation.1 | async-start | bytes 1310720 | tf_op jit(solution)/shard_map/all_to_all | solution.py:442
  55.5 34.1 %copy-start.2 = (f32[9,128,128]{2,1,0:T(8,128)S(1)}, f32[9,128,128]{2,1,0:T(8,128)}, u32[]{:S(2)}) copy-start(f32[9,128,128]{2,1,0:T(8,128)} %constant.28.clone.refs_3_.refs_13_.weights) | copy-start | bytes 1769476
  55.5 34.1 %copy-start.8 = (f32[1152,128]{1,0:T(8,128)S(1)}, f32[1152,128]{1,0:T(8,128)}, u32[]{:S(2)}) copy-start(f32[1152,128]{1,0:T(8,128)} %constant.31.clone.stokes_table) | copy-start | bytes 1769476
  55.6 12.2 %collective-permute-start.3 = (f32[32,9,1,128]{3,2,1,0:T(1,128)S(1)}, f32[32,9,1,128]{3,2,1,0:T(1,128)S(1)}, u32[]{:S(2)}, u32[]{:S(2)}) collective-permute-start(f32[32,9,1,128]{3,2,1,0:T(1,128)S(1)} %get-tuple-element.26), channel_id=1, source_target_pairs={{65,0},{64,1},{129,64},{128,65},{193,128},{192,129},{257,192},{256... | collective-permute-start | bytes 442376 | tf_op jit(solution)/shard_map/ppermute | solution.py:485
  57.0 10.7 %collective-permute-start = (f32[32,9,1,128]{3,2,1,0:T(1,128)S(1)}, f32[32,9,1,128]{3,2,1,0:T(1,128)S(1)}, u32[]{:S(2)}, u32[]{:S(2)}) collective-permute-start(f32[32,9,1,128]{3,2,1,0:T(1,128)S(1)} %get-tuple-element.27), channel_id=1, source_target_pairs={{0,64},{64,128},{128,192},{192,256},{256,320},{320,384},{384,448},... | collective-permute-start | bytes 442376 | tf_op jit(solution)/shard_map/ppermute | solution.py:484
  61.3 6.4 %collective-permute-start.1 = (f32[32,9,1,128]{3,2,1,0:T(1,128)S(1)}, f32[32,9,1,128]{3,2,1,0:T(1,128)S(1)}, u32[]{:S(2)}, u32[]{:S(2)}) collective-permute-start(f32[32,9,1,128]{3,2,1,0:T(1,128)S(1)} %get-tuple-element.27), channel_id=1, source_target_pairs={{1,64},{0,65},{65,128},{64,129},{129,192},{128,193},{193,256},{192... | collective-permute-start | bytes 442376 | tf_op jit(solution)/shard_map/ppermute | solution.py:485
  63.2 6.8 %collective-permute-start.2 = (f32[32,9,1,128]{3,2,1,0:T(1,128)S(1)}, f32[32,9,1,128]{3,2,1,0:T(1,128)S(1)}, u32[]{:S(2)}, u32[]{:S(2)}) collective-permute-start(f32[32,9,1,128]{3,2,1,0:T(1,128)S(1)} %get-tuple-element.26), channel_id=1, source_target_pairs={{64,0},{128,64},{192,128},{256,192},{320,256},{384,320},{448,384},... | collective-permute-start | bytes 442376 | tf_op jit(solution)/shard_map/ppermute | solution.py:484
  64.5 11.1 %copy-start.18 = (f32[32,1,1,128]{3,2,1,0:T(1,128)}, f32[32,1,1,128]{3,2,1,0:T(1,128)S(1)}, u32[]{:S(2)}) copy-start(f32[32,1,1,128]{3,2,1,0:T(1,128)S(1)} %slice.14) | copy-start | bytes 49156
  64.5 3.2 %collective-permute-start.4 = (f32[32,1,1,128]{3,0,2,1:T(8,128)S(1)}, f32[32,1,1,128]{3,0,2,1:T(8,128)S(1)}, u32[]{:S(2)}, u32[]{:S(2)}) collective-permute-start(f32[32,1,1,128]{3,0,2,1:T(8,128)S(1)} %bitcast.39), channel_id=1, source_target_pairs={{1,0},{0,1},{65,64},{64,65},{129,128},{128,129},{193,192},{192,193... | collective-permute-start | bytes 49160 | tf_op jit(solution)/shard_map/ppermute | solution.py:485
  67.7 7.9 %copy-start.19 = (f32[32,1,1,128]{3,0,2,1:T(8,128)}, f32[32,1,1,128]{3,0,2,1:T(8,128)S(1)}, u32[]{:S(2)}) copy-start(f32[32,1,1,128]{3,0,2,1:T(8,128)S(1)} %collective-permute-done.4) | copy-start | bytes 49156
  67.7 7.9 %copy-start.14 = (f32[32,9,1,128]{3,2,1,0:T(1,128)}, f32[32,9,1,128]{3,2,1,0:T(1,128)S(1)}, u32[]{:S(2)}) copy-start(f32[32,9,1,128]{3,2,1,0:T(1,128)S(1)} %collective-permute-done.3) | copy-start | bytes 442372
  67.7 7.9 %copy-start.15 = (f32[32,9,1,128]{3,2,1,0:T(1,128)}, f32[32,9,1,128]{3,2,1,0:T(1,128)S(1)}, u32[]{:S(2)}) copy-start(f32[32,9,1,128]{3,2,1,0:T(1,128)S(1)} %collective-permute-done) | copy-start | bytes 442372
  67.8 7.8 %copy-start.16 = (f32[32,9,1,128]{3,2,1,0:T(1,128)}, f32[32,9,1,128]{3,2,1,0:T(1,128)S(1)}, u32[]{:S(2)}) copy-start(f32[32,9,1,128]{3,2,1,0:T(1,128)S(1)} %collective-permute-done.1) | copy-start | bytes 442372
  70.1 5.6 %copy-start.17 = (f32[32,9,1,128]{3,2,1,0:T(1,128)}, f32[32,9,1,128]{3,2,1,0:T(1,128)S(1)}, u32[]{:S(2)}) copy-start(f32[32,9,1,128]{3,2,1,0:T(1,128)S(1)} %collective-permute-done.2) | copy-start | bytes 442372
  75.6 0.9 copy-start
  76.4 19.3 %copy-start.7 = (f32[27,1152]{1,0:T(8,128)S(1)}, f32[27,1152]{1,0:T(8,128)}, u32[]{:S(2)}) copy-start(f32[27,1152]{1,0:T(8,128)} %constant.30.clone.refs_4_.table) | copy-start | bytes 373252
  76.4 19.3 %copy-start.10 = (s32[1,64]{1,0:T(1,128)S(1)}, s32[1,64]{1,0:T(1,128)}, u32[]{:S(2)}) copy-start(s32[1,64]{1,0:T(1,128)} %index_west.1) | copy-start | bytes 772
  76.4 19.3 %copy-start.11 = (s32[1,64]{1,0:T(1,128)S(1)}, s32[1,64]{1,0:T(1,128)}, u32[]{:S(2)}) copy-start(s32[1,64]{1,0:T(1,128)} %index_east.1) | copy-start | bytes 772
  84.2 10.1 %collective-permute-start.7 = (f32[9,64,128]{2,1,0:T(8,128)}, f32[9,64,128]{2,1,0:T(8,128)S(1)}, u32[]{:S(2)}, u32[]{:S(2)}) collective-permute-start(f32[9,64,128]{2,1,0:T(8,128)} %get-tuple-element.14.far), channel_id=1, source_target_pairs={{0,1},{1,2},{2,3},{3,4},{4,5},{5,6},{6,7},{7,8},{8,9},{9,10},{10,1... | collective-permute-start | bytes 884744 | tf_op jit(solution)/shard_map/ppermute | solution.py:510
  87.5 8.3 %collective-permute-start.8 = (f32[9,64,128]{2,1,0:T(8,128)}, f32[9,64,128]{2,1,0:T(8,128)S(1)}, u32[]{:S(2)}, u32[]{:S(2)}) collective-permute-start(f32[9,64,128]{2,1,0:T(8,128)} %get-tuple-element.13.near), channel_id=1, source_target_pairs={{1,0},{2,1},{3,2},{4,3},{5,4},{6,5},{7,6},{8,7},{9,8},{10,9},{11,1... | collective-permute-start | bytes 884744 | tf_op jit(solution)/shard_map/ppermute | solution.py:511
  89.6 1.1 copy-start.1
  90.7 1.0 copy-start.3
  91.7 1.0 copy-start.5
  92.7 35.8 %copy-start.9 = (s32[1,64,128]{2,1,0:T(8,128)S(1)}, s32[1,64,128]{2,1,0:T(8,128)}, u32[]{:S(2)}) copy-start(s32[1,64,128]{2,1,0:T(8,128)} %param.16) | copy-start | bytes 98308
  94.2 14.1 %copy-start.20 = (s32[32]{0:T(128)S(1)}, s32[32]{0:T(128)}, u32[]{:S(2)}) copy-start(s32[32]{0:T(128)} %constant.33.clone) | copy-start | bytes 388
  95.8 1.0 copy-start.4
  96.7 1.0 copy-start.6
  99.9 28.5 %all-to-all-start.2 = ((f32[64,20,1,128]{3,2,1,0:T(1,128)}), f32[64,20,1,128]{3,2,1,0:T(1,128)S(1)}, u32[]{:S(2)}, u32[]{:S(2)}) async-start(f32[64,20,1,128]{3,2,1,0:T(1,128)} %bitcast.16), calls=%async_computation.2 | async-start | bytes 1310720 | tf_op jit(solution)/shard_map/all_to_all | solution.py:442

commit v3 on v2

--- a/solution.py
+++ b/solution.py
@@ -14,6 +14,7 @@
 EVERY = ("grid", "space", "spec")
 f32 = np.float32
 highest = lax.Precision.HIGHEST
+INFLOW_LIMIT = 60
 MSG = 20
 VM = pl.BlockSpec(memory_space=pltpu.VMEM)
 SM = pl.BlockSpec(memory_space=pltpu.SMEM)
@@ -65,7 +66,6 @@
     for name, c in (("x", CX), ("y", CY))
 }
 FLOW_W = np.tile(CURRENT.T, (2, ND)).astype(f32)
-FLOW_W = np.ascontiguousarray(FLOW_W.reshape(128, TILES, 128).transpose(1, 0, 2))
 GAIN = 2.0 / np.sqrt(float(ND))
 STOKES_T = np.concatenate(
     [(DRIFTS.T[:, None, :] * (trig * GAIN)[None, :, None]).reshape(LEV, COMPS) for trig in (COS, SIN)]
@@ -193,15 +193,14 @@
     )
 
 
-def rows_move(u, v, table, weights, spec, north, south, out, east_flow, north_flow):
+def rows_move(u, v, weights, table, spec, north, south, out, flow):
     uv = jnp.concatenate([u.get()[...], v.get()[...]], axis=0).T
     out[pl.ds(TILES, 128, stride=TILES + 1), :] = uv
-    both = jnp.concatenate(halves(uv), axis=0)
+    both = exact(jnp.concatenate(halves(uv), axis=0), weights.get()[...])
+    for k in range(TILES):
+        flow[k] = both[:, 128 * k : 128 * k + 128]
     table = table.get()
     for k in range(TILES):
-        flow = exact(both, weights.get(k)[...])
-        east_flow[...] = flow[:128]
-        north_flow[...] = flow[128:]
         tile = lambda ref, t: ref[pl.ds(t, 8, stride=16), :]
         now, above, below = (ref.get(k) for ref in (spec, north, south))
         mids = [tile(now, t) for t in range(16)]
@@ -209,9 +208,8 @@
         for t in range(16):
             west = mids[t - 1] if t else down(mids[15])
             east = mids[t + 1] if t < 15 else up(mids[0])
-            moved.append(
-                advect(mids[t], west, east, tile(above, t), tile(below, t), tile(east_flow, t), tile(north_flow, t))
-            )
+            along, across = tile(flow.at[k], t), tile(flow.at[k], 128 + t)
+            moved.append(advect(mids[t], west, east, tile(above, t), tile(below, t), along, across))
         for t, value in enumerate(sweep(moved, table, k, HAS["x"][k])):
             out[pl.ds(t * (TILES + 1) + k, 8, stride=16 * (TILES + 1)), :] = value
 
@@ -222,47 +220,59 @@
     return jnp.where(n < half, 2 * n + core, 2 * (n - half) + 1 - core)
 
 
+def columns_inflow(
+    place, wide, table, index_west, index_east, west_own, west_other, east_own, east_other, ends_own, ends_other, out,
+    flow,
+):
+    core = place[0] % 2
+    pick_row = (senders(core, 1) == lax.broadcasted_iota(jnp.int32, (NROW, NROW), 0)).astype(jnp.float32)
+    ends = exact(pick_row, jnp.concatenate([ends_own[...], ends_other[...]], axis=0))
+    flow[...] = exact(jnp.concatenate(halves(ends), axis=0), wide[...])
+    behind = (place[0] * 2).astype(jnp.float32)
+    added = [[], []]
+    for n, (index, own, other, sign) in enumerate(
+        ((index_west, west_own, west_other, 1.0), (index_east, east_own, east_other, -1.0))
+    ):
+        pick = (index[...] == senders(core, 0)).astype(jnp.float32).T
+        columns = jnp.concatenate(
+            [
+                jnp.concatenate([ref[pl.ds(k, NROW // 2, stride=TILES), :] for ref in (own, other)], axis=0)
+                for k in range(TILES)
+            ],
+            axis=1,
+        )
+        speed = jnp.maximum(sign * flow[NROW * n : NROW * (n + 1), :], 0.0) + table[pl.ds(INFLOW[1] + n, 1), :]
+        inflow = speed * exact(pick, columns)
+        steps = [behind, behind + 1.0] if n == 0 else [NCOL - 1.0 - behind, NCOL - 2.0 - behind]
+        for side in range(2):
+            fade = table[pl.ds(FADES + 2, 1), :] * jnp.exp(table[pl.ds(FADES + n, 1), :] * steps[side])
+            added[side].append(fade * inflow)
+    for side in range(2):
+        total = added[side][0] + added[side][1]
+        for k in range(TILES):
+            out[k, NROW * side : NROW * (side + 1), :] = total[:, 128 * k : 128 * k + 128]
+
+
 def columns_source(
-    place, land_sea, wind, damp, table, index_west, index_east, west_own, west_other, east_own, east_other, ends_own,
-    ends_other, weights, arrived, transfer, near, far, sea, turned, held, work, inflow,
+    place, land_sea, wind, damp, table, inflow, arrived, transfer, near, far, sea, turned, held, work
 ):
     lane = lax.broadcasted_iota(jnp.int32, (NROW, NCOL), 1)
-    core = place[0] % 2
-    pick_row = (senders(core, 1) == lax.broadcasted_iota(jnp.int32, (NROW, NROW), 0)).astype(jnp.float32)
-    land_sea, table, index_west, index_east = (x.get() for x in (land_sea, table, index_west, index_east))
-    picks = [(index[...] == senders(core, 0)).astype(jnp.float32).T for index in (index_west, index_east)]
-    edges = [[x.get() for x in pair] for pair in ((west_own, west_other), (east_own, east_other))]
-    ends = jnp.concatenate([ends_own.get()[...], ends_other.get()[...]], axis=0)
-    arrived = arrived.get() if isinstance(arrived, Fetched) else arrived
     land = land_sea[...].astype(jnp.float32)
     for side in range(2):
         column = jnp.sum(jnp.where(lane == 2 * place[0] + side, land, 0.0), axis=1, keepdims=True)
         sea[NROW * side : NROW * (side + 1), :] = jnp.broadcast_to(column, (NROW, 128))
-    behind = (place[0] * 2).astype(jnp.float32)
-    ends = jnp.concatenate(halves(exact(pick_row, ends)), axis=0)
-    for k in range(TILES):
-        lanes = pl.ds(128 * k, 128)
-        row = lambda n: table[pl.ds(n, 1), lanes]
-        flow = exact(ends, weights.get(k)[...])
-        fades = []
-        for n, (pick, pair, sign) in enumerate(zip(picks, edges, (1.0, -1.0))):
-            speed = jnp.maximum(sign * flow[NROW * n : NROW * (n + 1)], 0.0) + row(INFLOW[1] + n)
-            column = jnp.concatenate([ref[pl.ds(k, NROW // 2, stride=TILES), :] for ref in pair], axis=0)
-            inflow[NROW * n : NROW * (n + 1), :] = speed * exact(pick, column)
-            steps = [behind, behind + 1.0] if n == 0 else [NCOL - 1.0 - behind, NCOL - 2.0 - behind]
-            fades.append([row(FADES + 2) * jnp.exp(row(FADES + n) * count) for count in steps])
+    for k in range(TILES):
         for side in range(2):
+            places = [pl.ds(NROW * side + s, 8, stride=8) for s in range(8)]
             tiles = [
                 arrived[pl.ds((2 * s + side) * (TILES + 1) + k, 8, stride=16 * (TILES + 1)), :]
-                + fades[0][side] * inflow[pl.ds(s, 8, stride=8), :]
-                + fades[1][side] * inflow[pl.ds(NROW + s, 8, stride=8), :]
+                + inflow.at[k][places[s], :]
                 for s in range(8)
             ]
             for s, value in enumerate(sweep(tiles, table, k, HAS["y"][k])):
-                at = pl.ds(NROW * side + s, 8, stride=8)
-                turned.at[k][at, :] = value * sea[at, :]
+                turned.at[k][places[s], :] = value * sea[places[s], :]
         held[128 * k : 128 * k + 128, :] = turned[k].T
-    source_step(held, transfer.get(), wind.get()[...], damp.get()[...], sea[...].T[:1], work)
+    source_step(held, transfer, wind[...], damp[...], sea[...].T[:1], work)
     for k in range(TILES):
         back = work[128 * k : 128 * k + 128, :].T
         near[k] = back[:NROW]
@@ -273,12 +283,11 @@
     uv = jnp.concatenate(
         [arrived[pl.ds(TILES + side * (TILES + 1), NROW, stride=MSG), :] for side in range(2)], axis=0
     )
-    both = jnp.concatenate(halves(uv), axis=0)
+    both = exact(jnp.concatenate(halves(uv), axis=0), weights[...])
     total = jnp.zeros((128, 128), jnp.float32)
     for k in range(TILES):
-        flow = exact(both, weights[k])
-        east_flow[k] = flow[:128]
-        north_flow[k] = flow[128:]
+        east_flow[k] = both[:128, 128 * k : 128 * k + 128]
+        north_flow[k] = both[128:, 128 * k : 128 * k + 128]
         spectra = jnp.concatenate([near[k], far[k]], axis=0)
         total = total + exact(spectra, stokes_table[128 * k : 128 * k + 128, :])
     stokes[...] = total
@@ -469,9 +478,9 @@
     (sent,) = kernel(
         rows_move,
         [(64 * MSG, 128)],
-        [square, square],
-        [FETCH, FETCH, FETCH, TILED, TILED, TILED, TILED],
-        [u, v, jnp.asarray(KX), weights, rows, north, south],
+        [(TILES, 256, 128)],
+        [FETCH, FETCH, FETCH, FETCH, TILED, TILED, TILED],
+        [u, v, weights, jnp.asarray(KX), rows, north, south],
         90_000_000,
         5_000_000,
     )
@@ -487,15 +496,26 @@
 
     edges = shifted(own[:, :TILES], 1) + shifted(own[:, TILES : 2 * TILES], -1) + shifted(own[:, 2 * TILES :], 0)
 
+    table = jnp.asarray(KY)
+    (inflow,) = kernel(
+        columns_inflow,
+        [flow],
+        [(128, COMPS)],
+        [SM] + [VM] * 10,
+        [at, weights, table, west_index, east_index, *edges],
+        60_000_000,
+        3_000_000,
+        INFLOW_LIMIT,
+    )
     near, far = kernel(
         columns_source,
         [half, half],
-        [square, flow, full, full, square],
-        [SM] + [FETCH] * 12 + [TILED, FETCH, FETCH],
-        [at, sea, wind, damp, jnp.asarray(KY), west_index, east_index, *edges, weights, arrived, transfer],
+        [square, flow, full, full],
+        [SM] + [VM] * 7,
+        [at, sea, wind, damp, table, inflow, arrived, transfer],
         400_000_000,
         7_000_000,
-        60,
+        32,
     )
     a_cols, b_cols, drift = kernel(
         columns_flow,
@@ -514,7 +534,7 @@
         [(64 * MSG, 128)],
         [(NROW, 128), (NROW, 128), square, full],
         [SM] + [VM] * 10,
-        [at, near, far, from_west, from_east, west_index, east_index, a_cols, b_cols, drift, jnp.asarray(KY)],
+        [at, near, far, from_west, from_east, west_index, east_index, a_cols, b_cols, drift, table],
         10_000_000,
         5_000_000,
         32,

time: 132 us -> 126 us (0.955)
  the two profiles are of different devices: /device:TPU:1 before, /device:TPU:199 now
where the time goes in v3:
time: 126 us; the launch traced here: 125 us
  starting transfers between devices  59.6 us (47%)
  waiting for transfers between devices  37.1 us (29%)
  Pallas kernels  21.3 us (17%)
  local copies, waits for them, and re-layouts  5.86 us (5%)
    all_to_all x3, starting transfers between devices, exchange(): got = lax.all_to_all(sent, axes, split_axis=0, concat_axis=0, tiled=True)  32.4 us
    pallas_call x7, Pallas kernels, kernel(): pl.pallas_call(whole if late else body, out_shape=[jax.ShapeDtypeStruct(s...  21.3 us
    all_to_all x3, waiting for transfers between devices, exchange(): got = lax.all_to_all(sent, axes, split_axis=0, concat_axis=0, tiled=True)  18.6 us
    ppermute x3, starting transfers between devices, shifted(): other = lax.ppermute(part, ('grid', 'spec'), cross)  8.38 us
    ppermute x1, waiting for transfers between devices, model(): north = lax.ppermute(rows, PLANE, step(PLANE, 1))  7.55 us
    ppermute x2, starting transfers between devices, shifted(): same = lax.ppermute(part, 'grid', chips) if by else part  7.13 us
    ppermute x1, waiting for transfers between devices, model(): from_east = lax.ppermute(near, EVERY, step(EVERY, -1))  4.4 us
    ppermute x1, starting transfers between devices, model(): north = lax.ppermute(rows, PLANE, step(PLANE, 1))  4.22 us
  transfers between devices with their start and end apart: 12, of which 7 were waited for; matrix products, arithmetic and copies ran while one was open for 3% of the time, Pallas kernels for 8%

profile of v3, /device:TPU:199, one launch (start us, length us, event | category | flops | bytes accessed | tf_op | source)
XLA Modules:
  0.0 124.8 jit_solution(10041010246121650623)
XLA Ops:
  0.6 3.8 %shard_map.158 = (f32[9,128,128]{2,1,0:T(8,128)}, f32[608,128]{1,0:T(8,128)}) custom-call(s32[1]{0:T(128)} %bitcast.place, f32[1152,128]{1,0:T(8,128)} %bitcast.35, bf16[1152,1152]{1,0:T(8,128)(2,1)} %transfer.3, f32[1,36]{1,0:T(1,128)} %bitcast.30, f32[1,36]{1,0:T(1,128)} %bitcast.32, s32[64,128]{1,0:T(8,128)} %bitcast.27, f32[64,128]{1,0:T(8,128)} %bitcast.40), custom_call_target="tpu_custom_call" | custom-call | flops 340000000 | bytes 4000000 | tf_op jit(solution)/shard_map/pallas_call | solution.py:432
  4.4 9.7 %all-to-all-start = ((f32[32,19,1,128]{3,2,1,0:T(1,128)}), f32[32,19,1,128]{3,2,1,0:T(1,128)S(1)}, u32[]{:S(2)}, u32[]{:S(2)}) async-start(f32[32,19,1,128]{3,2,1,0:T(1,128)} %bitcast.36), calls=%async_computation | async-start | bytes 622592 | tf_op jit(solution)/shard_map/all_to_all | solution.py:451
  14.1 4.2 %collective-permute-start.5 = (f32[9,128,128]{2,1,0:T(8,128)}, f32[9,128,128]{2,1,0:T(8,128)S(1)}, u32[]{:S(2)}, u32[]{:S(2)}) collective-permute-start(f32[9,128,128]{2,1,0:T(8,128)} %get-tuple-element.12.refs_4_), channel_id=1, source_target_pairs={{0,1},{1,2},{2,3},{3,4},{4,5},{5,6},{6,7},{7,8},{8,9},{9,10},{10,1... | collective-permute-start | bytes 1769480 | tf_op jit(solution)/shard_map/ppermute | solution.py:475
  18.3 1.9 %collective-permute-start.6 = (f32[9,128,128]{2,1,0:T(8,128)}, f32[9,128,128]{2,1,0:T(8,128)S(1)}, u32[]{:S(2)}, u32[]{:S(2)}) collective-permute-start(f32[9,128,128]{2,1,0:T(8,128)} %get-tuple-element.12.refs_4_), channel_id=1, source_target_pairs={{1,0},{2,1},{3,2},{4,3},{5,4},{6,5},{7,6},{8,7},{9,8},{10,9},{11,1... | collective-permute-start | bytes 1769480 | tf_op jit(solution)/shard_map/ppermute | solution.py:476
  20.2 7.5 %collective-permute-done.5.refs_5_ = f32[9,128,128]{2,1,0:T(8,128)S(1)} collective-permute-done((f32[9,128,128]{2,1,0:T(8,128)}, f32[9,128,128]{2,1,0:T(8,128)S(1)}, u32[]{:S(2)}, u32[]{:S(2)}) %collective-permute-start.5) | collective-permute-done | bytes 589856 | tf_op jit(solution)/shard_map/ppermute | solution.py:475
  27.8 2.2 %collective-permute-done.6.refs_6_ = f32[9,128,128]{2,1,0:T(8,128)S(1)} collective-permute-done((f32[9,128,128]{2,1,0:T(8,128)}, f32[9,128,128]{2,1,0:T(8,128)S(1)}, u32[]{:S(2)}, u32[]{:S(2)}) %collective-permute-start.6) | collective-permute-done | bytes 589856 | tf_op jit(solution)/shard_map/ppermute | solution.py:476
  30.0 0.0 copy-done.11
  30.0 0.8 copy-done.12
  30.8 5.5 %shard_map.160 = f32[1280,128]{1,0:T(8,128)} custom-call(f32[64,128]{1,0:T(8,128)} %bitcast.41, f32[64,128]{1,0:T(8,128)} %bitcast.44, f32[128,1152]{1,0:T(8,128)} %constant.28.clone.wide.refs_2_.weights, f32[40,1152]{1,0:T(8,128)} %constant.29.clone.refs_3_, f32[9,128,128]{2,1,0:T(8,128)} %get-tuple-element.12.refs_4_, f32[9,128,128]{2,1,0:T(8,128)} %copy-done.11, ...), custom_call_target="tpu_custom_call" | custom-call | flops 90000000 | bytes 5000000 | tf_op jit(solution)/shard_map/pallas_call | solution.py:432
  36.4 0.0 copy-start
  36.4 0.0 copy-start.3
  36.4 0.0 copy-start.5
  36.4 0.0 copy-start.6
  36.4 0.0 copy-start.7
  36.4 0.0 all-to-all-done
  36.4 0.0 copy-start.10
  36.4 0.7 copy-done.10
  37.1 10.2 %all-to-all-start.1 = ((f32[64,20,1,128]{3,2,1,0:T(1,128)}), f32[64,20,1,128]{3,2,1,0:T(1,128)S(1)}, u32[]{:S(2)}, u32[]{:S(2)}) async-start(f32[64,20,1,128]{3,2,1,0:T(1,128)} %bitcast.34), calls=%async_computation.1 | async-start | bytes 1310720 | tf_op jit(solution)/shard_map/all_to_all | solution.py:451
  47.4 1.0 fusion
  48.4 1.9 %collective-permute-start.3 = (f32[32,9,1,128]{3,2,1,0:T(1,128)S(1)}, f32[32,9,1,128]{3,2,1,0:T(1,128)S(1)}, u32[]{:S(2)}, u32[]{:S(2)}) collective-permute-start(f32[32,9,1,128]{3,2,1,0:T(1,128)S(1)} %get-tuple-element.26), channel_id=1, source_target_pairs={{65,0},{64,1},{129,64},{128,65},{193,128},{192,129},{257,192},{256... | collective-permute-start | bytes 442376 | tf_op jit(solution)/shard_map/ppermute | solution.py:494
  50.3 5.2 %collective-permute-start = (f32[32,9,1,128]{3,2,1,0:T(1,128)S(1)}, f32[32,9,1,128]{3,2,1,0:T(1,128)S(1)}, u32[]{:S(2)}, u32[]{:S(2)}) collective-permute-start(f32[32,9,1,128]{3,2,1,0:T(1,128)S(1)} %get-tuple-element.27), channel_id=1, source_target_pairs={{0,64},{64,128},{128,192},{192,256},{256,320},{320,384},{384,448},... | collective-permute-start | bytes 442376 | tf_op jit(solution)/shard_map/ppermute | solution.py:493
  55.6 4.6 %collective-permute-start.1 = (f32[32,9,1,128]{3,2,1,0:T(1,128)S(1)}, f32[32,9,1,128]{3,2,1,0:T(1,128)S(1)}, u32[]{:S(2)}, u32[]{:S(2)}) collective-permute-start(f32[32,9,1,128]{3,2,1,0:T(1,128)S(1)} %get-tuple-element.27), channel_id=1, source_target_pairs={{1,64},{0,65},{65,128},{64,129},{129,192},{128,193},{193,256},{192... | collective-permute-start | bytes 442376 | tf_op jit(solution)/shard_map/ppermute | solution.py:494
  60.1 1.9 %collective-permute-start.2 = (f32[32,9,1,128]{3,2,1,0:T(1,128)S(1)}, f32[32,9,1,128]{3,2,1,0:T(1,128)}, u32[]{:S(2)}, u32[]{:S(2)}) collective-permute-start(f32[32,9,1,128]{3,2,1,0:T(1,128)S(1)} %get-tuple-element.26), channel_id=1, source_target_pairs={{64,0},{128,64},{192,128},{256,192},{320,256},{384,320},{448,384},... | collective-permute-start | bytes 442376 | tf_op jit(solution)/shard_map/ppermute | solution.py:493
  62.0 0.7 slice.14
  62.8 1.9 %collective-permute-start.4 = (f32[32,1,1,128]{3,0,2,1:T(8,128)S(1)}, f32[32,1,1,128]{3,0,2,1:T(8,128)S(1)}, u32[]{:S(2)}, u32[]{:S(2)}) collective-permute-start(f32[32,1,1,128]{3,0,2,1:T(8,128)S(1)} %bitcast.42), channel_id=1, source_target_pairs={{1,0},{0,1},{65,64},{64,65},{129,128},{128,129},{193,192},{192,193... | collective-permute-start | bytes 49160 | tf_op jit(solution)/shard_map/ppermute | solution.py:494
  64.7 1.1 collective-permute-done.4
  65.8 0.0 collective-permute-done.3
  65.8 0.0 collective-permute-done
  65.8 0.0 copy-start.14
  65.9 0.0 collective-permute-done.1
  65.9 0.0 copy-start.15
  65.9 3.0 %collective-permute-done.2 = f32[32,9,1,128]{3,2,1,0:T(1,128)} collective-permute-done((f32[32,9,1,128]{3,2,1,0:T(1,128)S(1)}, f32[32,9,1,128]{3,2,1,0:T(1,128)}, u32[]{:S(2)}, u32[]{:S(2)}) %collective-permute-start.2) | collective-permute-done | bytes 147488 | tf_op jit(solution)/shard_map/ppermute | solution.py:493
  68.9 0.0 copy-done.16
  68.9 0.0 copy-done.17
  68.9 0.0 copy-done.13
  68.9 0.0 copy-done.14
  68.9 0.0 copy-done.15
  68.9 3.5 %shard_map.159.inflow = f32[9,128,128]{2,1,0:T(8,128)} custom-call(s32[1]{0:T(128)} %bitcast.place, f32[128,1152]{1,0:T(8,128)} %constant.28.clone.wide.refs_2_.weights, f32[27,1152]{1,0:T(8,128)} %constant.30.clone.table, s32[1,64]{1,0:T(1,128)} %index_west.3, s32[1,64]{1,0:T(1,128)} %index_east.3, f32[288,128]{1,0:T(8,128)} %bitcast.38, ...), custom_call_target="tpu_custom_call" | custom-call | flops 60000000 | bytes 3000000 | tf_op jit(solution)/shard_map/pallas_call | solution.py:432
  72.4 0.0 all-to-all-done.1
  72.4 0.0 copy-done
  72.4 0.0 copy-done.3
  72.4 0.0 copy-done.5
  72.4 0.0 copy-done.6
  72.4 0.0 copy-done.7
  72.5 0.0 copy-start.2
  72.5 1.1 copy-done.2
  73.6 1.5 %shard_map.161 = (f32[9,64,128]{2,1,0:T(8,128)S(1)}, f32[9,64,128]{2,1,0:T(8,128)S(1)}) custom-call(s32[1]{0:T(128)} %bitcast.place, s32[64,128]{1,0:T(8,128)S(1)} %bitcast.28, f32[1,36]{1,0:T(1,128)S(1)} %bitcast.31, f32[1,36]{1,0:T(1,128)S(1)} %bitcast.33, f32[27,1152]{1,0:T(8,128)S(1)} %copy-done.3, f32[9,128,128]{2,1,0:T(8,128)S(1)} %copy-done.2, ...), custom_call_target="tpu_custom_call" | custom-call | flops 400000000 | bytes 7000000 | tf_op jit(solution)/shard_map/pallas_call | solution.py:432
  75.1 3.7 %collective-permute-start.7 = (f32[9,64,128]{2,1,0:T(8,128)S(1)}, f32[9,64,128]{2,1,0:T(8,128)S(1)}, u32[]{:S(2)}, u32[]{:S(2)}) collective-permute-start(f32[9,64,128]{2,1,0:T(8,128)S(1)} %get-tuple-element.14.far), channel_id=1, source_target_pairs={{0,1},{1,2},{2,3},{3,4},{4,5},{5,6},{6,7},{7,8},{8,9},{9,10},{10,1... | collective-permute-start | bytes 884744 | tf_op jit(solution)/shard_map/ppermute | solution.py:530
  78.8 1.9 %collective-permute-start.8 = (f32[9,64,128]{2,1,0:T(8,128)S(1)}, f32[9,64,128]{2,1,0:T(8,128)S(1)}, u32[]{:S(2)}, u32[]{:S(2)}) collective-permute-start(f32[9,64,128]{2,1,0:T(8,128)S(1)} %get-tuple-element.13.near), channel_id=1, source_target_pairs={{1,0},{2,1},{3,2},{4,3},{5,4},{6,5},{7,6},{8,7},{9,8},{10,9},{11,1... | collective-permute-start | bytes 884744 | tf_op jit(solution)/shard_map/ppermute | solution.py:531
  80.7 0.0 copy-done.1
  80.7 0.0 copy-done.4
  80.8 1.6 %shard_map.162 = (f32[9,128,128]{2,1,0:T(8,128)S(1)}, f32[9,128,128]{2,1,0:T(8,128)S(1)}, f32[128,128]{1,0:T(8,128)S(1)}) custom-call(f32[1280,128]{1,0:T(8,128)S(1)} %bitcast.25, f32[9,64,128]{2,1,0:T(8,128)S(1)} %get-tuple-element.13.near, f32[9,64,128]{2,1,0:T(8,128)S(1)} %get-tuple-element.14.far, f32[128,1152]{1,0:T(8,128)S(1)} %copy-done.1, ...), custom_call_target="tpu_custom_call" | custom-call | flops 100000000 | bytes 4000000 | tf_op jit(solution)/shard_map/pallas_call | solution.py:432
  82.3 0.0 copy-start.18
  82.3 0.1 collective-permute-done.7.from_west
  82.4 4.4 %collective-permute-done.8.from_east = f32[9,64,128]{2,1,0:T(8,128)S(1)} collective-permute-done((f32[9,64,128]{2,1,0:T(8,128)S(1)}, f32[9,64,128]{2,1,0:T(8,128)S(1)}, u32[]{:S(2)}, u32[]{:S(2)}) %collective-permute-start.8) | collective-permute-done | bytes 294944 | tf_op jit(solution)/shard_map/ppermute | solution.py:531
  86.8 0.0 copy-done.8
  86.8 0.0 copy-done.9
  86.9 2.2 %shard_map.163 = f32[1280,128]{1,0:T(8,128)} custom-call(s32[1]{0:T(128)} %bitcast.place, f32[9,64,128]{2,1,0:T(8,128)S(1)} %get-tuple-element.13.near, f32[9,64,128]{2,1,0:T(8,128)S(1)} %get-tuple-element.14.far, f32[9,64,128]{2,1,0:T(8,128)S(1)} %collective-permute-done.7.from_west, f32[9,64,128]{2,1,0:T(8,128)S(1)} %collective-permute-done.8.from_east, ...), custom_call_target="tpu_custom_call" | custom-call | flops 10000000 | bytes 5000000 | tf_op jit(solution)/shard_map/pallas_call | solution.py:432
  89.1 12.5 %all-to-all-start.2 = ((f32[64,20,1,128]{3,2,1,0:T(1,128)}), f32[64,20,1,128]{3,2,1,0:T(1,128)S(1)}, u32[]{:S(2)}, u32[]{:S(2)}) async-start(f32[64,20,1,128]{3,2,1,0:T(1,128)} %bitcast.16), calls=%async_computation.2 | async-start | bytes 1310720 | tf_op jit(solution)/shard_map/all_to_all | solution.py:451
  101.5 0.0 copy-done.18
  101.5 0.7 dynamic_slice.6.ahead
  102.2 0.7 constant_dynamic-slice_fusion.scalars
  102.9 18.6 %all-to-all-done.2 = f32[64,20,1,128]{3,2,1,0:T(1,128)S(1)} async-done(((f32[64,20,1,128]{3,2,1,0:T(1,128)}), f32[64,20,1,128]{3,2,1,0:T(1,128)S(1)}, u32[]{:S(2)}, u32[]{:S(2)}) %all-to-all-start.2) | async-done | bytes 655392 | tf_op jit(solution)/shard_map/all_to_all | solution.py:451
  121.5 3.3 %shard_map.164 = (f32[1152,128]{1,0:T(8,128)}, f32[128,128]{1,0:T(8,128)}) custom-call(s32[1]{0:T(128)} %dynamic_slice.6.ahead, f32[1,144]{1,0:T(1,128)S(1)} %constant_dynamic-slice_fusion.scalars, f32[1280,128]{1,0:T(8,128)S(1)} %bitcast.26, s32[64,128]{1,0:T(8,128)S(1)} %bitcast.29), custom_call_target="tpu_custom_call" | custom-call | flops 100000000 | bytes 2000000 | tf_op jit(solution)/shard_map/pallas_call | solution.py:432
  (9 shorter events, 0.0 us)
Async XLA Ops:
  4.4 32.0 %all-to-all-start = ((f32[32,19,1,128]{3,2,1,0:T(1,128)}), f32[32,19,1,128]{3,2,1,0:T(1,128)S(1)}, u32[]{:S(2)}, u32[]{:S(2)}) async-start(f32[32,19,1,128]{3,2,1,0:T(1,128)} %bitcast.36), calls=%async_computation | async-start | bytes 622592 | tf_op jit(solution)/shard_map/all_to_all | solution.py:451
  14.1 13.7 %collective-permute-start.5 = (f32[9,128,128]{2,1,0:T(8,128)}, f32[9,128,128]{2,1,0:T(8,128)S(1)}, u32[]{:S(2)}, u32[]{:S(2)}) collective-permute-start(f32[9,128,128]{2,1,0:T(8,128)} %get-tuple-element.12.refs_4_), channel_id=1, source_target_pairs={{0,1},{1,2},{2,3},{3,4},{4,5},{5,6},{6,7},{7,8},{8,9},{9,10},{10,1... | collective-permute-start | bytes 1769480 | tf_op jit(solution)/shard_map/ppermute | solution.py:475
  18.3 11.7 %collective-permute-start.6 = (f32[9,128,128]{2,1,0:T(8,128)}, f32[9,128,128]{2,1,0:T(8,128)S(1)}, u32[]{:S(2)}, u32[]{:S(2)}) collective-permute-start(f32[9,128,128]{2,1,0:T(8,128)} %get-tuple-element.12.refs_4_), channel_id=1, source_target_pairs={{1,0},{2,1},{3,2},{4,3},{5,4},{6,5},{7,6},{8,7},{9,8},{10,9},{11,1... | collective-permute-start | bytes 1769480 | tf_op jit(solution)/shard_map/ppermute | solution.py:476
  27.8 2.2 %copy-start.11 = (f32[9,128,128]{2,1,0:T(8,128)}, f32[9,128,128]{2,1,0:T(8,128)S(1)}, u32[]{:S(2)}) copy-start(f32[9,128,128]{2,1,0:T(8,128)S(1)} %collective-permute-done.5.refs_5_) | copy-start | bytes 1769476
  30.0 0.8 copy-start.12
  36.4 36.1 %copy-start = (bf16[1152,1152]{1,0:T(8,128)(2,1)S(1)}, bf16[1152,1152]{1,0:T(8,128)(2,1)}, u32[]{:S(2)}) copy-start(bf16[1152,1152]{1,0:T(8,128)(2,1)} %transfer.3) | copy-start | bytes 7962628
  36.4 36.1 %copy-start.3 = (f32[27,1152]{1,0:T(8,128)S(1)}, f32[27,1152]{1,0:T(8,128)}, u32[]{:S(2)}) copy-start(f32[27,1152]{1,0:T(8,128)} %constant.30.clone.table) | copy-start | bytes 373252
  36.4 36.1 %copy-start.5 = (s32[1,64,128]{2,1,0:T(8,128)S(1)}, s32[1,64,128]{2,1,0:T(8,128)}, u32[]{:S(2)}) copy-start(s32[1,64,128]{2,1,0:T(8,128)} %param.16) | copy-start | bytes 98308
  36.4 36.1 %copy-start.6 = (f32[36]{0:T(128)S(1)}, f32[36]{0:T(128)}, u32[]{:S(2)}) copy-start(f32[36]{0:T(128)} %param.22) | copy-start | bytes 436
  36.4 36.0 %copy-start.7 = (f32[36]{0:T(128)S(1)}, f32[36]{0:T(128)}, u32[]{:S(2)}) copy-start(f32[36]{0:T(128)} %param.23) | copy-start | bytes 436
  36.4 0.7 copy-start.10
  37.1 35.3 %all-to-all-start.1 = ((f32[64,20,1,128]{3,2,1,0:T(1,128)}), f32[64,20,1,128]{3,2,1,0:T(1,128)S(1)}, u32[]{:S(2)}, u32[]{:S(2)}) async-start(f32[64,20,1,128]{3,2,1,0:T(1,128)} %bitcast.34), calls=%async_computation.1 | async-start | bytes 1310720 | tf_op jit(solution)/shard_map/all_to_all | solution.py:451
  48.4 17.4 %collective-permute-start.3 = (f32[32,9,1,128]{3,2,1,0:T(1,128)S(1)}, f32[32,9,1,128]{3,2,1,0:T(1,128)S(1)}, u32[]{:S(2)}, u32[]{:S(2)}) collective-permute-start(f32[32,9,1,128]{3,2,1,0:T(1,128)S(1)} %get-tuple-element.26), channel_id=1, source_target_pairs={{65,0},{64,1},{129,64},{128,65},{193,128},{192,129},{257,192},{256... | collective-permute-start | bytes 442376 | tf_op jit(solution)/shard_map/ppermute | solution.py:494
  50.3 15.5 %collective-permute-start = (f32[32,9,1,128]{3,2,1,0:T(1,128)S(1)}, f32[32,9,1,128]{3,2,1,0:T(1,128)S(1)}, u32[]{:S(2)}, u32[]{:S(2)}) collective-permute-start(f32[32,9,1,128]{3,2,1,0:T(1,128)S(1)} %get-tuple-element.27), channel_id=1, source_target_pairs={{0,64},{64,128},{128,192},{192,256},{256,320},{320,384},{384,448},... | collective-permute-start | bytes 442376 | tf_op jit(solution)/shard_map/ppermute | solution.py:493
  55.6 10.3 %collective-permute-start.1 = (f32[32,9,1,128]{3,2,1,0:T(1,128)S(1)}, f32[32,9,1,128]{3,2,1,0:T(1,128)S(1)}, u32[]{:S(2)}, u32[]{:S(2)}) collective-permute-start(f32[32,9,1,128]{3,2,1,0:T(1,128)S(1)} %get-tuple-element.27), channel_id=1, source_target_pairs={{1,64},{0,65},{65,128},{64,129},{129,192},{128,193},{193,256},{192... | collective-permute-start | bytes 442376 | tf_op jit(solution)/shard_map/ppermute | solution.py:494
  60.1 8.8 %collective-permute-start.2 = (f32[32,9,1,128]{3,2,1,0:T(1,128)S(1)}, f32[32,9,1,128]{3,2,1,0:T(1,128)}, u32[]{:S(2)}, u32[]{:S(2)}) collective-permute-start(f32[32,9,1,128]{3,2,1,0:T(1,128)S(1)} %get-tuple-element.26), channel_id=1, source_target_pairs={{64,0},{128,64},{192,128},{256,192},{320,256},{384,320},{448,384},... | collective-permute-start | bytes 442376 | tf_op jit(solution)/shard_map/ppermute | solution.py:493
  62.8 6.1 %copy-start.16 = (f32[32,1,1,128]{3,2,1,0:T(1,128)}, f32[32,1,1,128]{3,2,1,0:T(1,128)S(1)}, u32[]{:S(2)}) copy-start(f32[32,1,1,128]{3,2,1,0:T(1,128)S(1)} %slice.14) | copy-start | bytes 49156
  62.8 3.1 %collective-permute-start.4 = (f32[32,1,1,128]{3,0,2,1:T(8,128)S(1)}, f32[32,1,1,128]{3,0,2,1:T(8,128)S(1)}, u32[]{:S(2)}, u32[]{:S(2)}) collective-permute-start(f32[32,1,1,128]{3,0,2,1:T(8,128)S(1)} %bitcast.42), channel_id=1, source_target_pairs={{1,0},{0,1},{65,64},{64,65},{129,128},{128,129},{193,192},{192,193... | collective-permute-start | bytes 49160 | tf_op jit(solution)/shard_map/ppermute | solution.py:494
  65.8 3.1 %copy-start.17 = (f32[32,1,1,128]{3,0,2,1:T(8,128)}, f32[32,1,1,128]{3,0,2,1:T(8,128)S(1)}, u32[]{:S(2)}) copy-start(f32[32,1,1,128]{3,0,2,1:T(8,128)S(1)} %collective-permute-done.4) | copy-start | bytes 49156
  65.8 3.1 %copy-start.13 = (f32[32,9,1,128]{3,2,1,0:T(1,128)}, f32[32,9,1,128]{3,2,1,0:T(1,128)S(1)}, u32[]{:S(2)}) copy-start(f32[32,9,1,128]{3,2,1,0:T(1,128)S(1)} %collective-permute-done.3) | copy-start | bytes 442372
  65.8 3.1 %copy-start.14 = (f32[32,9,1,128]{3,2,1,0:T(1,128)}, f32[32,9,1,128]{3,2,1,0:T(1,128)S(1)}, u32[]{:S(2)}) copy-start(f32[32,9,1,128]{3,2,1,0:T(1,128)S(1)} %collective-permute-done) | copy-start | bytes 442372
  65.9 3.0 %copy-start.15 = (f32[32,9,1,128]{3,2,1,0:T(1,128)}, f32[32,9,1,128]{3,2,1,0:T(1,128)S(1)}, u32[]{:S(2)}) copy-start(f32[32,9,1,128]{3,2,1,0:T(1,128)S(1)} %collective-permute-done.1) | copy-start | bytes 442372
  72.4 8.3 %copy-start.1 = (f32[128,1152]{1,0:T(8,128)S(1)}, f32[128,1152]{1,0:T(8,128)}, u32[]{:S(2)}) copy-start(f32[128,1152]{1,0:T(8,128)} %constant.28.clone.wide.refs_2_.weights) | copy-start | bytes 1769476
  72.5 1.1 copy-start.2
  73.6 7.2 %copy-start.4 = (f32[1152,128]{1,0:T(8,128)S(1)}, f32[1152,128]{1,0:T(8,128)}, u32[]{:S(2)}) copy-start(f32[1152,128]{1,0:T(8,128)} %constant.31.clone.stokes_table) | copy-start | bytes 1769476
  73.6 13.3 %copy-start.8 = (s32[1,64]{1,0:T(1,128)S(1)}, s32[1,64]{1,0:T(1,128)}, u32[]{:S(2)}) copy-start(s32[1,64]{1,0:T(1,128)} %index_west.3) | copy-start | bytes 772
  73.6 13.3 %copy-start.9 = (s32[1,64]{1,0:T(1,128)S(1)}, s32[1,64]{1,0:T(1,128)}, u32[]{:S(2)}) copy-start(s32[1,64]{1,0:T(1,128)} %index_east.3) | copy-start | bytes 772
  75.1 7.3 %collective-permute-start.7 = (f32[9,64,128]{2,1,0:T(8,128)S(1)}, f32[9,64,128]{2,1,0:T(8,128)S(1)}, u32[]{:S(2)}, u32[]{:S(2)}) collective-permute-start(f32[9,64,128]{2,1,0:T(8,128)S(1)} %get-tuple-element.14.far), channel_id=1, source_target_pairs={{0,1},{1,2},{2,3},{3,4},{4,5},{5,6},{6,7},{7,8},{8,9},{9,10},{10,1... | collective-permute-start | bytes 884744 | tf_op jit(solution)/shard_map/ppermute | solution.py:530
  78.8 8.0 %collective-permute-start.8 = (f32[9,64,128]{2,1,0:T(8,128)S(1)}, f32[9,64,128]{2,1,0:T(8,128)S(1)}, u32[]{:S(2)}, u32[]{:S(2)}) collective-permute-start(f32[9,64,128]{2,1,0:T(8,128)S(1)} %get-tuple-element.13.near), channel_id=1, source_target_pairs={{1,0},{2,1},{3,2},{4,3},{5,4},{6,5},{7,6},{8,7},{9,8},{10,9},{11,1... | collective-permute-start | bytes 884744 | tf_op jit(solution)/shard_map/ppermute | solution.py:531
  82.3 19.2 %copy-start.18 = (s32[32]{0:T(128)S(1)}, s32[32]{0:T(128)}, u32[]{:S(2)}) copy-start(s32[32]{0:T(128)} %constant.33.clone) | copy-start | bytes 388
  89.1 32.4 %all-to-all-start.2 = ((f32[64,20,1,128]{3,2,1,0:T(1,128)}), f32[64,20,1,128]{3,2,1,0:T(1,128)S(1)}, u32[]{:S(2)}, u32[]{:S(2)}) async-start(f32[64,20,1,128]{3,2,1,0:T(1,128)} %bitcast.16), calls=%async_computation.2 | async-start | bytes 1310720 | tf_op jit(solution)/shard_map/all_to_all | solution.py:451

commit v4 on v3

--- a/solution.py
+++ b/solution.py
@@ -143,8 +143,9 @@
 
 def source_step(spec_ref, transfer, wind, damp, sea_row, out_ref):
     spectra = spec_ref[...]
+    energy = jnp.sum(spectra * spectra, axis=0, keepdims=True) * (1.0 / COMPS)
+    transfer = transfer.get() if isinstance(transfer, Fetched) else transfer
     redist = jnp.dot(transfer[...], spectra.astype(jnp.bfloat16), preferred_element_type=jnp.float32)
-    energy = jnp.sum(spectra * spectra, axis=0, keepdims=True) * (1.0 / COMPS)
     turns = lax.broadcasted_iota(jnp.int32, (2 * NF, NF), 0)
     turns = jnp.where(turns >= NF, turns - NF, turns)
     pick = turns == lax.broadcasted_iota(jnp.int32, (2 * NF, NF), 1)
@@ -159,7 +160,8 @@
         out_ref[rows, :] = (spectra[rows] * gain + 0.5 * redist[rows]) * shrink
 
 
-def rows_source(place, spec, transfer, wind, damp, land_sea, u, out, spread, work, edges):
+def rows_source(place, spec, transfer, u, land_sea, wind, damp, out, spread, work, edges):
+    u, land_sea, wind, damp, spec = (x.get() for x in (u, land_sea, wind, damp, spec))
     sea_row = land_sea[pl.ds(place[0], 1), :].astype(jnp.float32)
     turned = jnp.concatenate([u[...], u[...]], axis=0).T
     low = lax.broadcasted_iota(jnp.int32, (1, 128), 1) < LEV
@@ -220,27 +222,17 @@
     return jnp.where(n < half, 2 * n + core, 2 * (n - half) + 1 - core)
 
 
-def columns_inflow(
-    place, wide, table, index_west, index_east, west_own, west_other, east_own, east_other, ends_own, ends_other, out,
-    flow,
-):
+def columns_inflow(place, wide, table, index_west, index_east, own, other, out, flow):
     core = place[0] % 2
     pick_row = (senders(core, 1) == lax.broadcasted_iota(jnp.int32, (NROW, NROW), 0)).astype(jnp.float32)
-    ends = exact(pick_row, jnp.concatenate([ends_own[...], ends_other[...]], axis=0))
+    edge = lambda n: jnp.concatenate([ref[pl.ds(n, NROW // 2, stride=EDGE), :] for ref in (own, other)], axis=0)
+    ends = exact(pick_row, edge(2 * TILES))
     flow[...] = exact(jnp.concatenate(halves(ends), axis=0), wide[...])
     behind = (place[0] * 2).astype(jnp.float32)
     added = [[], []]
-    for n, (index, own, other, sign) in enumerate(
-        ((index_west, west_own, west_other, 1.0), (index_east, east_own, east_other, -1.0))
-    ):
+    for n, (index, sign) in enumerate(((index_west, 1.0), (index_east, -1.0))):
         pick = (index[...] == senders(core, 0)).astype(jnp.float32).T
-        columns = jnp.concatenate(
-            [
-                jnp.concatenate([ref[pl.ds(k, NROW // 2, stride=TILES), :] for ref in (own, other)], axis=0)
-                for k in range(TILES)
-            ],
-            axis=1,
-        )
+        columns = jnp.concatenate([edge(TILES * n + k) for k in range(TILES)], axis=1)
         speed = jnp.maximum(sign * flow[NROW * n : NROW * (n + 1), :], 0.0) + table[pl.ds(INFLOW[1] + n, 1), :]
         inflow = speed * exact(pick, columns)
         steps = [behind, behind + 1.0] if n == 0 else [NCOL - 1.0 - behind, NCOL - 2.0 - behind]
@@ -262,11 +254,12 @@
         column = jnp.sum(jnp.where(lane == 2 * place[0] + side, land, 0.0), axis=1, keepdims=True)
         sea[NROW * side : NROW * (side + 1), :] = jnp.broadcast_to(column, (NROW, 128))
     for k in range(TILES):
+        added = inflow.at[k]
         for side in range(2):
             places = [pl.ds(NROW * side + s, 8, stride=8) for s in range(8)]
             tiles = [
                 arrived[pl.ds((2 * s + side) * (TILES + 1) + k, 8, stride=16 * (TILES + 1)), :]
-                + inflow.at[k][places[s], :]
+                + added[places[s], :]
                 for s in range(8)
             ]
             for s, value in enumerate(sweep(tiles, table, k, HAS["y"][k])):
@@ -414,7 +407,7 @@
 
 
 def kernel(body, outs, scratch, specs, args, flops, nbytes, limit=60):
-    late = [n for n, spec in enumerate(specs) if spec is FETCH or spec is TILED]
+    late = [n for n, spec in enumerate(specs) if spec in (FETCH, TILED)]
 
     def whole(*refs):
         size = len(refs) - 2 * len(late)
@@ -467,8 +460,8 @@
         rows_source,
         [flow, (NROW // 2 * EDGE, 128)],
         [full, (24, 128)],
-        [SM, VM, VM, VM, VM, VM, VM],
-        [at, spec, transfer, wind, damp, sea, u],
+        [SM] + [FETCH] * 6,
+        [at, spec, transfer, u, sea, wind, damp],
         340_000_000,
         4_000_000,
     )
@@ -486,22 +479,18 @@
     )
     arrived = exchange(sent, MSG)
 
-    def shifted(part, by):
-        size = lax.axis_size("grid")
-        chips = step("grid", by) if by else [(i, i) for i in range(size)]
-        cross = [(2 * i + 1 - core, 2 * j + core) for i, j in chips for core in range(2)]
-        same = lax.ppermute(part, "grid", chips) if by else part
-        other = lax.ppermute(part, ("grid", "spec"), cross)
-        return [x.reshape(-1, 128) for x in (same, other)]
-
-    edges = shifted(own[:, :TILES], 1) + shifted(own[:, TILES : 2 * TILES], -1) + shifted(own[:, 2 * TILES :], 0)
+    west = lax.ppermute(own[:, :TILES], "grid", step("grid", 1))
+    east = lax.ppermute(own[:, TILES : 2 * TILES], "grid", step("grid", -1))
+    mine = jnp.concatenate([west, east, own[:, 2 * TILES :]], axis=1)
+    other = lax.ppermute(mine, "spec", [(0, 1), (1, 0)])
+    edges = [x.reshape(-1, 128) for x in (mine, other)]
 
     table = jnp.asarray(KY)
     (inflow,) = kernel(
         columns_inflow,
         [flow],
         [(128, COMPS)],
-        [SM] + [VM] * 10,
+        [SM] + [VM] * 6,
         [at, weights, table, west_index, east_index, *edges],
         60_000_000,
         3_000_000,

time: 126 us -> 124 us (0.984)
  the two profiles are of different devices: /device:TPU:199 before, /device:TPU:1 now
where the time goes in v4:
time: 124 us; the launch traced here: 123 us
  starting transfers between devices  53.1 us (43%)
  waiting for transfers between devices  40.8 us (33%)
  Pallas kernels  21.3 us (17%)
  local copies, waits for them, and re-layouts  6.51 us (5%)
    all_to_all x3, starting transfers between devices, exchange(): got = lax.all_to_all(sent, axes, split_axis=0, concat_axis=0, tiled=True)  29.4 us
    pallas_call x7, Pallas kernels, kernel(): pl.pallas_call(whole if late else body, out_shape=[jax.ShapeDtypeStruct(s...  21.3 us
    all_to_all x3, waiting for transfers between devices, exchange(): got = lax.all_to_all(sent, axes, split_axis=0, concat_axis=0, tiled=True)  20.8 us
    ppermute x1, starting transfers between devices, model(): north = lax.ppermute(rows, PLANE, step(PLANE, 1))  10.7 us
    ppermute x1, waiting for transfers between devices, model(): north = lax.ppermute(rows, PLANE, step(PLANE, 1))  6.53 us
    ppermute x1, waiting for transfers between devices, model(): from_east = lax.ppermute(near, EVERY, step(EVERY, -1))  4.4 us
    ppermute x1, waiting for transfers between devices, model(): east = lax.ppermute(own[:, TILES:2 * TILES], 'grid', step('grid', -1))  3.84 us
    unnamed x32, local copies, waits for them, and re-layouts  3.44 us
  transfers between devices with their start and end apart: 10, of which 9 were waited for; matrix products, arithmetic and copies ran while one was open for 3% of the time, Pallas kernels for 9%

profile of v4, /device:TPU:1, one launch (start us, length us, event | category | flops | bytes accessed | tf_op | source)
XLA Modules:
  0.0 122.9 jit_solution(12433530094794299150)
XLA Ops:
  0.6 3.9 %shard_map.158 = (f32[9,128,128]{2,1,0:T(8,128)}, f32[608,128]{1,0:T(8,128)}) custom-call(s32[1]{0:T(128)} %bitcast.refs_0_.place, f32[1152,128]{1,0:T(8,128)} %bitcast.30, bf16[1152,1152]{1,0:T(8,128)(2,1)} %transfer.1, f32[64,128]{1,0:T(8,128)} %bitcast.33, s32[64,128]{1,0:T(8,128)} %bitcast.21, f32[1,36]{1,0:T(1,128)} %bitcast.24, f32[1,36]{1,0:T(1,128)} %bitcast.26), custom_call_target="tpu_custom_call" | custom-call | flops 340000000 | bytes 4000000 | tf_op jit(solution)/shard_map/pallas_call | solution.py:425
  4.5 10.5 %all-to-all-start = ((f32[32,19,1,128]{3,2,1,0:T(1,128)}), f32[32,19,1,128]{3,2,1,0:T(1,128)S(1)}, u32[]{:S(2)}, u32[]{:S(2)}) async-start(f32[32,19,1,128]{3,2,1,0:T(1,128)} %bitcast.31), calls=%async_computation | async-start | bytes 622592 | tf_op jit(solution)/shard_map/all_to_all | solution.py:444
  15.0 10.7 %collective-permute-start.3 = (f32[9,128,128]{2,1,0:T(8,128)}, f32[9,128,128]{2,1,0:T(8,128)S(1)}, u32[]{:S(2)}, u32[]{:S(2)}) collective-permute-start(f32[9,128,128]{2,1,0:T(8,128)} %get-tuple-element.12.refs_4_), channel_id=1, source_target_pairs={{0,1},{1,2},{2,3},{3,4},{4,5},{5,6},{6,7},{7,8},{8,9},{9,10},{10,1... | collective-permute-start | bytes 1769480 | tf_op jit(solution)/shard_map/ppermute | solution.py:468
  25.7 1.9 %collective-permute-start.4 = (f32[9,128,128]{2,1,0:T(8,128)}, f32[9,128,128]{2,1,0:T(8,128)S(1)}, u32[]{:S(2)}, u32[]{:S(2)}) collective-permute-start(f32[9,128,128]{2,1,0:T(8,128)} %get-tuple-element.12.refs_4_), channel_id=1, source_target_pairs={{1,0},{2,1},{3,2},{4,3},{5,4},{6,5},{7,6},{8,7},{9,8},{10,9},{11,1... | collective-permute-start | bytes 1769480 | tf_op jit(solution)/shard_map/ppermute | solution.py:469
  27.6 6.5 %collective-permute-done.3.refs_5_ = f32[9,128,128]{2,1,0:T(8,128)S(1)} collective-permute-done((f32[9,128,128]{2,1,0:T(8,128)}, f32[9,128,128]{2,1,0:T(8,128)S(1)}, u32[]{:S(2)}, u32[]{:S(2)}) %collective-permute-start.3) | collective-permute-done | bytes 589856 | tf_op jit(solution)/shard_map/ppermute | solution.py:468
  34.2 0.0 copy-start.12
  34.2 2.9 %collective-permute-done.4.refs_6_ = f32[9,128,128]{2,1,0:T(8,128)S(1)} collective-permute-done((f32[9,128,128]{2,1,0:T(8,128)}, f32[9,128,128]{2,1,0:T(8,128)S(1)}, u32[]{:S(2)}, u32[]{:S(2)}) %collective-permute-start.4) | collective-permute-done | bytes 589856 | tf_op jit(solution)/shard_map/ppermute | solution.py:469
  37.1 0.0 copy-start.13
  37.1 0.0 copy-done.12
  37.1 0.8 copy-done.13
  38.0 5.5 %shard_map.160 = f32[1280,128]{1,0:T(8,128)} custom-call(f32[64,128]{1,0:T(8,128)} %bitcast.34, f32[64,128]{1,0:T(8,128)} %bitcast.35, f32[128,1152]{1,0:T(8,128)} %constant.28.clone.wide.refs_2_.weights, f32[40,1152]{1,0:T(8,128)} %constant.29.clone.refs_3_, f32[9,128,128]{2,1,0:T(8,128)} %get-tuple-element.12.refs_4_, f32[9,128,128]{2,1,0:T(8,128)} %copy-done.12, ...), custom_call_target="tpu_custom_call" | custom-call | flops 90000000 | bytes 5000000 | tf_op jit(solution)/shard_map/pallas_call | solution.py:425
  43.5 0.0 copy-start
  43.5 0.0 copy-start.3
  43.5 0.0 copy-start.5
  43.5 0.0 copy-start.6
  43.5 0.0 copy-start.7
  43.5 0.0 all-to-all-done
  43.5 0.0 copy-start.10
  43.5 0.7 copy-done.10
  44.2 10.3 %all-to-all-start.1 = ((f32[64,20,1,128]{3,2,1,0:T(1,128)}), f32[64,20,1,128]{3,2,1,0:T(1,128)S(1)}, u32[]{:S(2)}, u32[]{:S(2)}) async-start(f32[64,20,1,128]{3,2,1,0:T(1,128)} %bitcast.28), calls=%async_computation.1 | async-start | bytes 1310720 | tf_op jit(solution)/shard_map/all_to_all | solution.py:444
  54.5 1.0 fusion
  55.6 1.3 %collective-permute-start = (f32[32,9,1,128]{3,2,1,0:T(1,128)S(1)}, f32[32,9,1,128]{3,2,1,0:T(1,128)S(1)}, u32[]{:S(2)}, u32[]{:S(2)}) collective-permute-start(f32[32,9,1,128]{3,2,1,0:T(1,128)S(1)} %get-tuple-element.26), channel_id=1, source_target_pairs={{0,64},{64,128},{128,192},{192,256},{256,320},{320,384},{384,448},... | collective-permute-start | bytes 442376 | tf_op jit(solution)/shard_map/ppermute | solution.py:482
  56.9 1.3 %collective-permute-start.1 = (f32[32,9,1,128]{3,2,1,0:T(1,128)S(1)}, f32[32,9,1,128]{3,2,1,0:T(1,128)S(1)}, u32[]{:S(2)}, u32[]{:S(2)}) collective-permute-start(f32[32,9,1,128]{3,2,1,0:T(1,128)S(1)} %get-tuple-element.27), channel_id=1, source_target_pairs={{64,0},{128,64},{192,128},{256,192},{320,256},{384,320},{448,384},... | collective-permute-start | bytes 442376 | tf_op jit(solution)/shard_map/ppermute | solution.py:483
  58.2 0.7 slice.14
  58.9 1.0 collective-permute-done
  59.9 3.8 %collective-permute-done.1 = f32[32,9,1,128]{3,2,1,0:T(1,128)S(1)} collective-permute-done((f32[32,9,1,128]{3,2,1,0:T(1,128)S(1)}, f32[32,9,1,128]{3,2,1,0:T(1,128)S(1)}, u32[]{:S(2)}, u32[]{:S(2)}) %collective-permute-start.1) | collective-permute-done | bytes 147488 | tf_op jit(solution)/shard_map/ppermute | solution.py:483
  63.7 0.3 pad_maximum_fusion
  64.0 0.0 copy-start.11
  64.0 3.2 %collective-permute-start.2 = (f32[32,19,1,128]{3,2,1,0:T(1,128)S(1)}, f32[32,19,1,128]{3,2,1,0:T(1,128)S(1)}, u32[]{:S(2)}, u32[]{:S(2)}) collective-permute-start(f32[32,19,1,128]{3,2,1,0:T(1,128)S(1)} %pad_maximum_fusion), channel_id=1, source_target_pairs={{0,1},{1,0},{2,3},{3,2},{4,5},{5,4},{6,7},{7,6},{8,9},{9,8},{10,11... | collective-permute-start | bytes 933896 | tf_op jit(solution)/shard_map/ppermute | solution.py:485
  67.2 1.2 collective-permute-done.2
  68.4 0.0 copy-start.14
  68.4 0.7 copy-done.14
  69.2 0.0 copy-done.11
  69.2 3.4 %shard_map.159.inflow = f32[9,128,128]{2,1,0:T(8,128)} custom-call(s32[1]{0:T(128)} %bitcast.refs_0_.place, f32[128,1152]{1,0:T(8,128)} %constant.28.clone.wide.refs_2_.weights, f32[27,1152]{1,0:T(8,128)} %constant.30.clone.table, s32[1,64]{1,0:T(1,128)} %index_west.3, s32[1,64]{1,0:T(1,128)} %index_east.3, f32[608,128]{1,0:T(8,128)} %bitcast.29, ...), custom_call_target="tpu_custom_call" | custom-call | flops 60000000 | bytes 3000000 | tf_op jit(solution)/shard_map/pallas_call | solution.py:425
  72.6 2.0 %all-to-all-done.1 = f32[64,20,1,128]{3,2,1,0:T(1,128)S(1)} async-done(((f32[64,20,1,128]{3,2,1,0:T(1,128)}), f32[64,20,1,128]{3,2,1,0:T(1,128)S(1)}, u32[]{:S(2)}, u32[]{:S(2)}) %all-to-all-start.1) | async-done | bytes 655392 | tf_op jit(solution)/shard_map/all_to_all | solution.py:444
  74.6 0.0 copy-start.1
  74.6 0.0 copy-done
  74.6 0.0 copy-done.3
  74.6 0.0 copy-done.5
  74.6 0.0 copy-done.6
  74.7 0.0 copy-done.7
  74.7 0.0 copy-start.2
  74.7 1.1 copy-done.2
  75.8 0.0 copy-start.4
  75.8 0.0 copy-start.8
  75.8 0.0 copy-start.9
  75.8 1.5 %shard_map.161 = (f32[9,64,128]{2,1,0:T(8,128)S(1)}, f32[9,64,128]{2,1,0:T(8,128)S(1)}) custom-call(s32[1]{0:T(128)} %bitcast.refs_0_.place, s32[64,128]{1,0:T(8,128)S(1)} %bitcast.22, f32[1,36]{1,0:T(1,128)S(1)} %bitcast.25, f32[1,36]{1,0:T(1,128)S(1)} %bitcast.27, f32[27,1152]{1,0:T(8,128)S(1)} %copy-done.3, f32[9,128,128]{2,1,0:T(8,128)S(1)} %copy-done.2, ...), custom_call_target="tpu_custom_call" | custom-call | flops 400000000 | bytes 7000000 | tf_op jit(solution)/shard_map/pallas_call | solution.py:425
  77.3 3.3 %collective-permute-start.5 = (f32[9,64,128]{2,1,0:T(8,128)S(1)}, f32[9,64,128]{2,1,0:T(8,128)S(1)}, u32[]{:S(2)}, u32[]{:S(2)}) collective-permute-start(f32[9,64,128]{2,1,0:T(8,128)S(1)} %get-tuple-element.14.far), channel_id=1, source_target_pairs={{0,1},{1,2},{2,3},{3,4},{4,5},{5,6},{6,7},{7,8},{8,9},{9,10},{10,1... | collective-permute-start | bytes 884744 | tf_op jit(solution)/shard_map/ppermute | solution.py:519
  80.7 1.9 %collective-permute-start.6 = (f32[9,64,128]{2,1,0:T(8,128)S(1)}, f32[9,64,128]{2,1,0:T(8,128)S(1)}, u32[]{:S(2)}, u32[]{:S(2)}) collective-permute-start(f32[9,64,128]{2,1,0:T(8,128)S(1)} %get-tuple-element.13.near), channel_id=1, source_target_pairs={{1,0},{2,1},{3,2},{4,3},{5,4},{6,5},{7,6},{8,7},{9,8},{10,9},{11,1... | collective-permute-start | bytes 884744 | tf_op jit(solution)/shard_map/ppermute | solution.py:520
  82.6 0.0 copy-done.1
  82.6 0.0 copy-done.4
  82.6 1.6 %shard_map.162 = (f32[9,128,128]{2,1,0:T(8,128)S(1)}, f32[9,128,128]{2,1,0:T(8,128)S(1)}, f32[128,128]{1,0:T(8,128)S(1)}) custom-call(f32[1280,128]{1,0:T(8,128)S(1)} %bitcast.19, f32[9,64,128]{2,1,0:T(8,128)S(1)} %get-tuple-element.13.near, f32[9,64,128]{2,1,0:T(8,128)S(1)} %get-tuple-element.14.far, f32[128,1152]{1,0:T(8,128)S(1)} %copy-done.1, ...), custom_call_target="tpu_custom_call" | custom-call | flops 100000000 | bytes 4000000 | tf_op jit(solution)/shard_map/pallas_call | solution.py:425
  84.2 0.0 copy-start.15
  84.2 0.1 collective-permute-done.5.from_west
  84.3 4.4 %collective-permute-done.6.from_east = f32[9,64,128]{2,1,0:T(8,128)S(1)} collective-permute-done((f32[9,64,128]{2,1,0:T(8,128)S(1)}, f32[9,64,128]{2,1,0:T(8,128)S(1)}, u32[]{:S(2)}, u32[]{:S(2)}) %collective-permute-start.6) | collective-permute-done | bytes 294944 | tf_op jit(solution)/shard_map/ppermute | solution.py:520
  88.7 0.0 copy-done.8
  88.7 0.0 copy-done.9
  88.7 2.2 %shard_map.163 = f32[1280,128]{1,0:T(8,128)} custom-call(s32[1]{0:T(128)} %bitcast.refs_0_.place, f32[9,64,128]{2,1,0:T(8,128)S(1)} %get-tuple-element.13.near, f32[9,64,128]{2,1,0:T(8,128)S(1)} %get-tuple-element.14.far, f32[9,64,128]{2,1,0:T(8,128)S(1)} %collective-permute-done.5.from_west, f32[9,64,128]{2,1,0:T(8,128)S(1)} %collective-permute-done.6.from_east, ...), custom_call_target="tpu_custom_call" | custom-call | flops 10000000 | bytes 5000000 | tf_op jit(solution)/shard_map/pallas_call | solution.py:425
  90.9 8.6 %all-to-all-start.2 = ((f32[64,20,1,128]{3,2,1,0:T(1,128)}), f32[64,20,1,128]{3,2,1,0:T(1,128)S(1)}, u32[]{:S(2)}, u32[]{:S(2)}) async-start(f32[64,20,1,128]{3,2,1,0:T(1,128)} %bitcast.12), calls=%async_computation.2 | async-start | bytes 1310720 | tf_op jit(solution)/shard_map/all_to_all | solution.py:444
  99.6 0.0 copy-done.15
  99.6 0.6 dynamic_slice.6.ahead
  100.2 0.7 constant_dynamic-slice_fusion.scalars
  100.9 18.8 %all-to-all-done.2 = f32[64,20,1,128]{3,2,1,0:T(1,128)S(1)} async-done(((f32[64,20,1,128]{3,2,1,0:T(1,128)}), f32[64,20,1,128]{3,2,1,0:T(1,128)S(1)}, u32[]{:S(2)}, u32[]{:S(2)}) %all-to-all-start.2) | async-done | bytes 655392 | tf_op jit(solution)/shard_map/all_to_all | solution.py:444
  119.7 3.2 %shard_map.164 = (f32[1152,128]{1,0:T(8,128)}, f32[128,128]{1,0:T(8,128)}) custom-call(s32[1]{0:T(128)} %dynamic_slice.6.ahead, f32[1,144]{1,0:T(1,128)S(1)} %constant_dynamic-slice_fusion.scalars, f32[1280,128]{1,0:T(8,128)S(1)} %bitcast.20, s32[64,128]{1,0:T(8,128)S(1)} %bitcast.23), custom_call_target="tpu_custom_call" | custom-call | flops 100000000 | bytes 2000000 | tf_op jit(solution)/shard_map/pallas_call | solution.py:425
Async XLA Ops:
  4.5 39.0 %all-to-all-start = ((f32[32,19,1,128]{3,2,1,0:T(1,128)}), f32[32,19,1,128]{3,2,1,0:T(1,128)S(1)}, u32[]{:S(2)}, u32[]{:S(2)}) async-start(f32[32,19,1,128]{3,2,1,0:T(1,128)} %bitcast.31), calls=%async_computation | async-start | bytes 622592 | tf_op jit(solution)/shard_map/all_to_all | solution.py:444
  15.0 19.2 %collective-permute-start.3 = (f32[9,128,128]{2,1,0:T(8,128)}, f32[9,128,128]{2,1,0:T(8,128)S(1)}, u32[]{:S(2)}, u32[]{:S(2)}) collective-permute-start(f32[9,128,128]{2,1,0:T(8,128)} %get-tuple-element.12.refs_4_), channel_id=1, source_target_pairs={{0,1},{1,2},{2,3},{3,4},{4,5},{5,6},{6,7},{7,8},{8,9},{9,10},{10,1... | collective-permute-start | bytes 1769480 | tf_op jit(solution)/shard_map/ppermute | solution.py:468
  25.7 11.4 %collective-permute-start.4 = (f32[9,128,128]{2,1,0:T(8,128)}, f32[9,128,128]{2,1,0:T(8,128)S(1)}, u32[]{:S(2)}, u32[]{:S(2)}) collective-permute-start(f32[9,128,128]{2,1,0:T(8,128)} %get-tuple-element.12.refs_4_), channel_id=1, source_target_pairs={{1,0},{2,1},{3,2},{4,3},{5,4},{6,5},{7,6},{8,7},{9,8},{10,9},{11,1... | collective-permute-start | bytes 1769480 | tf_op jit(solution)/shard_map/ppermute | solution.py:469
  34.2 3.0 %copy-start.12 = (f32[9,128,128]{2,1,0:T(8,128)}, f32[9,128,128]{2,1,0:T(8,128)S(1)}, u32[]{:S(2)}) copy-start(f32[9,128,128]{2,1,0:T(8,128)S(1)} %collective-permute-done.3.refs_5_) | copy-start | bytes 1769476
  37.1 0.8 copy-start.13
  43.5 31.2 %copy-start = (bf16[1152,1152]{1,0:T(8,128)(2,1)S(1)}, bf16[1152,1152]{1,0:T(8,128)(2,1)}, u32[]{:S(2)}) copy-start(bf16[1152,1152]{1,0:T(8,128)(2,1)} %transfer.1) | copy-start | bytes 7962628
  43.5 31.2 %copy-start.3 = (f32[27,1152]{1,0:T(8,128)S(1)}, f32[27,1152]{1,0:T(8,128)}, u32[]{:S(2)}) copy-start(f32[27,1152]{1,0:T(8,128)} %constant.30.clone.table) | copy-start | bytes 373252
  43.5 31.2 %copy-start.5 = (s32[1,64,128]{2,1,0:T(8,128)S(1)}, s32[1,64,128]{2,1,0:T(8,128)}, u32[]{:S(2)}) copy-start(s32[1,64,128]{2,1,0:T(8,128)} %param.16) | copy-start | bytes 98308
  43.5 31.2 %copy-start.6 = (f32[36]{0:T(128)S(1)}, f32[36]{0:T(128)}, u32[]{:S(2)}) copy-start(f32[36]{0:T(128)} %param.22) | copy-start | bytes 436
  43.5 31.2 %copy-start.7 = (f32[36]{0:T(128)S(1)}, f32[36]{0:T(128)}, u32[]{:S(2)}) copy-start(f32[36]{0:T(128)} %param.23) | copy-start | bytes 436
  43.5 0.7 copy-start.10
  44.2 30.4 %all-to-all-start.1 = ((f32[64,20,1,128]{3,2,1,0:T(1,128)}), f32[64,20,1,128]{3,2,1,0:T(1,128)S(1)}, u32[]{:S(2)}, u32[]{:S(2)}) async-start(f32[64,20,1,128]{3,2,1,0:T(1,128)} %bitcast.28), calls=%async_computation.1 | async-start | bytes 1310720 | tf_op jit(solution)/shard_map/all_to_all | solution.py:444
  55.6 4.3 %collective-permute-start = (f32[32,9,1,128]{3,2,1,0:T(1,128)S(1)}, f32[32,9,1,128]{3,2,1,0:T(1,128)S(1)}, u32[]{:S(2)}, u32[]{:S(2)}) collective-permute-start(f32[32,9,1,128]{3,2,1,0:T(1,128)S(1)} %get-tuple-element.26), channel_id=1, source_target_pairs={{0,64},{64,128},{128,192},{192,256},{256,320},{320,384},{384,448},... | collective-permute-start | bytes 442376 | tf_op jit(solution)/shard_map/ppermute | solution.py:482
  56.9 6.8 %collective-permute-start.1 = (f32[32,9,1,128]{3,2,1,0:T(1,128)S(1)}, f32[32,9,1,128]{3,2,1,0:T(1,128)S(1)}, u32[]{:S(2)}, u32[]{:S(2)}) collective-permute-start(f32[32,9,1,128]{3,2,1,0:T(1,128)S(1)} %get-tuple-element.27), channel_id=1, source_target_pairs={{64,0},{128,64},{192,128},{256,192},{320,256},{384,320},{448,384},... | collective-permute-start | bytes 442376 | tf_op jit(solution)/shard_map/ppermute | solution.py:483
  64.0 5.2 %copy-start.11 = (f32[32,19,1,128]{3,2,1,0:T(1,128)}, f32[32,19,1,128]{3,2,1,0:T(1,128)S(1)}, u32[]{:S(2)}) copy-start(f32[32,19,1,128]{3,2,1,0:T(1,128)S(1)} %pad_maximum_fusion) | copy-start | bytes 933892
  64.0 4.4 %collective-permute-start.2 = (f32[32,19,1,128]{3,2,1,0:T(1,128)S(1)}, f32[32,19,1,128]{3,2,1,0:T(1,128)S(1)}, u32[]{:S(2)}, u32[]{:S(2)}) collective-permute-start(f32[32,19,1,128]{3,2,1,0:T(1,128)S(1)} %pad_maximum_fusion), channel_id=1, source_target_pairs={{0,1},{1,0},{2,3},{3,2},{4,5},{5,4},{6,7},{7,6},{8,9},{9,8},{10,11... | collective-permute-start | bytes 933896 | tf_op jit(solution)/shard_map/ppermute | solution.py:485
  68.4 0.7 copy-start.14
  74.6 8.0 %copy-start.1 = (f32[128,1152]{1,0:T(8,128)S(1)}, f32[128,1152]{1,0:T(8,128)}, u32[]{:S(2)}) copy-start(f32[128,1152]{1,0:T(8,128)} %constant.28.clone.wide.refs_2_.weights) | copy-start | bytes 1769476
  74.7 1.1 copy-start.2
  75.8 6.8 %copy-start.4 = (f32[1152,128]{1,0:T(8,128)S(1)}, f32[1152,128]{1,0:T(8,128)}, u32[]{:S(2)}) copy-start(f32[1152,128]{1,0:T(8,128)} %constant.31.clone.stokes_table) | copy-start | bytes 1769476
  75.8 12.9 %copy-start.8 = (s32[1,64]{1,0:T(1,128)S(1)}, s32[1,64]{1,0:T(1,128)}, u32[]{:S(2)}) copy-start(s32[1,64]{1,0:T(1,128)} %index_west.3) | copy-start | bytes 772
  75.8 12.9 %copy-start.9 = (s32[1,64]{1,0:T(1,128)S(1)}, s32[1,64]{1,0:T(1,128)}, u32[]{:S(2)}) copy-start(s32[1,64]{1,0:T(1,128)} %index_east.3) | copy-start | bytes 772
  77.3 7.0 %collective-permute-start.5 = (f32[9,64,128]{2,1,0:T(8,128)S(1)}, f32[9,64,128]{2,1,0:T(8,128)S(1)}, u32[]{:S(2)}, u32[]{:S(2)}) collective-permute-start(f32[9,64,128]{2,1,0:T(8,128)S(1)} %get-tuple-element.14.far), channel_id=1, source_target_pairs={{0,1},{1,2},{2,3},{3,4},{4,5},{5,6},{6,7},{7,8},{8,9},{9,10},{10,1... | collective-permute-start | bytes 884744 | tf_op jit(solution)/shard_map/ppermute | solution.py:519
  80.7 8.0 %collective-permute-start.6 = (f32[9,64,128]{2,1,0:T(8,128)S(1)}, f32[9,64,128]{2,1,0:T(8,128)S(1)}, u32[]{:S(2)}, u32[]{:S(2)}) collective-permute-start(f32[9,64,128]{2,1,0:T(8,128)S(1)} %get-tuple-element.13.near), channel_id=1, source_target_pairs={{1,0},{2,1},{3,2},{4,3},{5,4},{6,5},{7,6},{8,7},{9,8},{10,9},{11,1... | collective-permute-start | bytes 884744 | tf_op jit(solution)/shard_map/ppermute | solution.py:520
  84.2 15.4 %copy-start.15 = (s32[32]{0:T(128)S(1)}, s32[32]{0:T(128)}, u32[]{:S(2)}) copy-start(s32[32]{0:T(128)} %constant.33.clone) | copy-start | bytes 388
  90.9 28.7 %all-to-all-start.2 = ((f32[64,20,1,128]{3,2,1,0:T(1,128)}), f32[64,20,1,128]{3,2,1,0:T(1,128)S(1)}, u32[]{:S(2)}, u32[]{:S(2)}) async-start(f32[64,20,1,128]{3,2,1,0:T(1,128)} %bitcast.12), calls=%async_computation.2 | async-start | bytes 1310720 | tf_op jit(solution)/shard_map/all_to_all | solution.py:444

commit v5 on v4

--- a/solution.py
+++ b/solution.py
@@ -144,8 +144,12 @@
 def source_step(spec_ref, transfer, wind, damp, sea_row, out_ref):
     spectra = spec_ref[...]
     energy = jnp.sum(spectra * spectra, axis=0, keepdims=True) * (1.0 / COMPS)
-    transfer = transfer.get() if isinstance(transfer, Fetched) else transfer
-    redist = jnp.dot(transfer[...], spectra.astype(jnp.bfloat16), preferred_element_type=jnp.float32)
+    rounded = spectra.astype(jnp.bfloat16)
+    product = lambda block: jnp.dot(block[...], rounded, preferred_element_type=jnp.float32)
+    if isinstance(transfer, Fetched):
+        redist = jnp.concatenate([product(transfer.get(k)) for k in range(TILES)], axis=0)
+    else:
+        redist = product(transfer)
     turns = lax.broadcasted_iota(jnp.int32, (2 * NF, NF), 0)
     turns = jnp.where(turns >= NF, turns - NF, turns)
     pick = turns == lax.broadcasted_iota(jnp.int32, (2 * NF, NF), 1)
@@ -297,9 +301,14 @@
         (jnp.where(end, jnp.broadcast_to(index[...], (NROW, NROW)), along) == across).astype(jnp.float32).T
         for end, index in zip(at_end, (index_west, index_east))
     ]
-    for k in range(TILES):
-        west_halo[...] = exact(picks[0], from_west[k])
-        east_halo[...] = exact(picks[1], from_east[k])
+    halos = [
+        exact(pick, jnp.concatenate([source[k] for k in range(TILES)], axis=1))
+        for pick, source in zip(picks, (from_west, from_east))
+    ]
+    for k in range(TILES):
+        west_halo[k] = halos[0][:, 128 * k : 128 * k + 128]
+        east_halo[k] = halos[1][:, 128 * k : 128 * k + 128]
+    for k in range(TILES):
         lanes = pl.ds(128 * k, 128)
         into = [table[pl.ds(INFLOW[1] + n, 1), lanes] * flags[n] for n in range(2)]
         cells = [[ref.at[k][pl.ds(s, 8, stride=8), :] for s in range(8)] for ref in (near, far)]
@@ -308,7 +317,7 @@
             moved = []
             for s in range(8):
                 at = pl.ds(NROW * side + s, 8, stride=8)
-                beyond = halo[pl.ds(s, 8, stride=8), :]
+                beyond = halo.at[k][pl.ds(s, 8, stride=8), :]
                 mids = cells[side]
                 north = mids[s - 1] if s else down(mids[7])
                 south = mids[s + 1] if s < 7 else up(mids[0])
@@ -379,10 +388,10 @@
         total = jnp.zeros((NROW, 256), jnp.float32)
         for side in range(2):
             left = both[NROW * side : NROW * (side + 1)]
-            for n in range(3):
+            for n in range(2):
                 part = left.astype(jnp.bfloat16)
                 total = total + jnp.dot(part, spread[side], preferred_element_type=jnp.float32)
-                if n < 2:
+                if n == 0:
                     left = left - part.astype(jnp.float32)
         for n in range(2):
             i = 2 * pair + n
@@ -460,8 +469,8 @@
         rows_source,
         [flow, (NROW // 2 * EDGE, 128)],
         [full, (24, 128)],
-        [SM] + [FETCH] * 6,
-        [at, spec, transfer, u, sea, wind, damp],
+        [SM, FETCH, TILED] + [FETCH] * 4,
+        [at, spec, transfer.reshape(TILES, 128, COMPS), u, sea, wind, damp],
         340_000_000,
         4_000_000,
     )
@@ -521,7 +530,7 @@
     (sent,) = kernel(
         columns_move,
         [(64 * MSG, 128)],
-        [(NROW, 128), (NROW, 128), square, full],
+        [half, half, square, full],
         [SM] + [VM] * 10,
         [at, near, far, from_west, from_east, west_index, east_index, a_cols, b_cols, drift, table],
         10_000_000,

time: 124 us -> 125 us (level)
  transfers between devices with their start and end apart: 10 -> 10, of which waited for: 9 -> 8; matrix products, arithmetic and copies ran while one was open for 3% -> 3% of each run, Pallas kernels for 9% -> 8%
where the time goes in v5:
time: 125 us; the launch traced here: 124 us
  starting transfers between devices  53.1 us (42%)
  waiting for transfers between devices  40.7 us (33%)
  Pallas kernels  22.5 us (18%)
  local copies, waits for them, and re-layouts  6.51 us (5%)
    all_to_all x3, starting transfers between devices, exchange(): got = lax.all_to_all(sent, axes, split_axis=0, concat_axis=0, tiled=True)  29.2 us
    pallas_call x7, Pallas kernels, kernel(): pl.pallas_call(whole if late else body, out_shape=[jax.ShapeDtypeStruct(s...  22.5 us
    all_to_all x3, waiting for transfers between devices, exchange(): got = lax.all_to_all(sent, axes, split_axis=0, concat_axis=0, tiled=True)  20.8 us
    ppermute x1, starting transfers between devices, model(): north = lax.ppermute(rows, PLANE, step(PLANE, 1))  10.7 us
    ppermute x1, waiting for transfers between devices, model(): north = lax.ppermute(rows, PLANE, step(PLANE, 1))  6.53 us
    ppermute x1, waiting for transfers between devices, model(): from_east = lax.ppermute(near, EVERY, step(EVERY, -1))  4.33 us
    ppermute x1, waiting for transfers between devices, model(): east = lax.ppermute(own[:, TILES:2 * TILES], 'grid', step('grid', -1))  3.84 us
    unnamed x32, local copies, waits for them, and re-layouts  3.44 us
  transfers between devices with their start and end apart: 10, of which 8 were waited for; matrix products, arithmetic and copies ran while one was open for 3% of the time, Pallas kernels for 8%

profile of v5, /device:TPU:1, one launch (start us, length us, event | category | flops | bytes accessed | tf_op | source)
XLA Modules:
  0.0 123.9 jit_solution(14907025113701131318)
XLA Ops:
  0.6 5.2 %shard_map.158 = (f32[9,128,128]{2,1,0:T(8,128)}, f32[608,128]{1,0:T(8,128)}) custom-call(s32[1]{0:T(128)} %bitcast.refs_0_.place, f32[1152,128]{1,0:T(8,128)} %bitcast.32, bf16[9,128,1152]{2,1,0:T(8,128)(2,1)} %bitcast.19, f32[64,128]{1,0:T(8,128)} %bitcast.35, s32[64,128]{1,0:T(8,128)} %bitcast.23, f32[1,36]{1,0:T(1,128)} %bitcast.26, f32[1,36]{1,0:T(1,128)} %bitcast.28), custom_call_target="tpu_custom_call" | custom-call | flops 340000000 | bytes 4000000 | tf_op jit(solution)/shard_map/pallas_call | solution.py:434
  5.9 10.5 %all-to-all-start = ((f32[32,19,1,128]{3,2,1,0:T(1,128)}), f32[32,19,1,128]{3,2,1,0:T(1,128)S(1)}, u32[]{:S(2)}, u32[]{:S(2)}) async-start(f32[32,19,1,128]{3,2,1,0:T(1,128)} %bitcast.33), calls=%async_computation | async-start | bytes 622592 | tf_op jit(solution)/shard_map/all_to_all | solution.py:453
  16.4 10.7 %collective-permute-start.3 = (f32[9,128,128]{2,1,0:T(8,128)}, f32[9,128,128]{2,1,0:T(8,128)S(1)}, u32[]{:S(2)}, u32[]{:S(2)}) collective-permute-start(f32[9,128,128]{2,1,0:T(8,128)} %get-tuple-element.12.refs_4_), channel_id=1, source_target_pairs={{0,1},{1,2},{2,3},{3,4},{4,5},{5,6},{6,7},{7,8},{8,9},{9,10},{10,1... | collective-permute-start | bytes 1769480 | tf_op jit(solution)/shard_map/ppermute | solution.py:477
  27.1 1.9 %collective-permute-start.4 = (f32[9,128,128]{2,1,0:T(8,128)}, f32[9,128,128]{2,1,0:T(8,128)S(1)}, u32[]{:S(2)}, u32[]{:S(2)}) collective-permute-start(f32[9,128,128]{2,1,0:T(8,128)} %get-tuple-element.12.refs_4_), channel_id=1, source_target_pairs={{1,0},{2,1},{3,2},{4,3},{5,4},{6,5},{7,6},{8,7},{9,8},{10,9},{11,1... | collective-permute-start | bytes 1769480 | tf_op jit(solution)/shard_map/ppermute | solution.py:478
  29.0 6.5 %collective-permute-done.3.refs_5_ = f32[9,128,128]{2,1,0:T(8,128)S(1)} collective-permute-done((f32[9,128,128]{2,1,0:T(8,128)}, f32[9,128,128]{2,1,0:T(8,128)S(1)}, u32[]{:S(2)}, u32[]{:S(2)}) %collective-permute-start.3) | collective-permute-done | bytes 589856 | tf_op jit(solution)/shard_map/ppermute | solution.py:477
  35.5 0.0 copy-start.12
  35.5 2.9 %collective-permute-done.4.refs_6_ = f32[9,128,128]{2,1,0:T(8,128)S(1)} collective-permute-done((f32[9,128,128]{2,1,0:T(8,128)}, f32[9,128,128]{2,1,0:T(8,128)S(1)}, u32[]{:S(2)}, u32[]{:S(2)}) %collective-permute-start.4) | collective-permute-done | bytes 589856 | tf_op jit(solution)/shard_map/ppermute | solution.py:478
  38.5 0.0 copy-start.13
  38.5 0.0 copy-done.12
  38.5 0.8 copy-done.13
  39.3 5.5 %shard_map.160 = f32[1280,128]{1,0:T(8,128)} custom-call(f32[64,128]{1,0:T(8,128)} %bitcast.36, f32[64,128]{1,0:T(8,128)} %bitcast.37, f32[128,1152]{1,0:T(8,128)} %constant.28.clone.wide.refs_2_.weights, f32[40,1152]{1,0:T(8,128)} %constant.29.clone.refs_3_, f32[9,128,128]{2,1,0:T(8,128)} %get-tuple-element.12.refs_4_, f32[9,128,128]{2,1,0:T(8,128)} %copy-done.12, ...), custom_call_target="tpu_custom_call" | custom-call | flops 90000000 | bytes 5000000 | tf_op jit(solution)/shard_map/pallas_call | solution.py:434
  44.8 0.0 copy-start
  44.8 0.0 copy-start.3
  44.8 0.0 copy-start.5
  44.8 0.0 copy-start.6
  44.9 0.0 copy-start.7
  44.9 0.0 all-to-all-done
  44.9 0.0 copy-start.10
  44.9 0.7 copy-done.10
  45.6 10.3 %all-to-all-start.1 = ((f32[64,20,1,128]{3,2,1,0:T(1,128)}), f32[64,20,1,128]{3,2,1,0:T(1,128)S(1)}, u32[]{:S(2)}, u32[]{:S(2)}) async-start(f32[64,20,1,128]{3,2,1,0:T(1,128)} %bitcast.30), calls=%async_computation.1 | async-start | bytes 1310720 | tf_op jit(solution)/shard_map/all_to_all | solution.py:453
  55.9 1.0 fusion
  56.9 1.3 %collective-permute-start = (f32[32,9,1,128]{3,2,1,0:T(1,128)S(1)}, f32[32,9,1,128]{3,2,1,0:T(1,128)S(1)}, u32[]{:S(2)}, u32[]{:S(2)}) collective-permute-start(f32[32,9,1,128]{3,2,1,0:T(1,128)S(1)} %get-tuple-element.26), channel_id=1, source_target_pairs={{0,64},{64,128},{128,192},{192,256},{256,320},{320,384},{384,448},... | collective-permute-start | bytes 442376 | tf_op jit(solution)/shard_map/ppermute | solution.py:491
  58.2 1.3 %collective-permute-start.1 = (f32[32,9,1,128]{3,2,1,0:T(1,128)S(1)}, f32[32,9,1,128]{3,2,1,0:T(1,128)S(1)}, u32[]{:S(2)}, u32[]{:S(2)}) collective-permute-start(f32[32,9,1,128]{3,2,1,0:T(1,128)S(1)} %get-tuple-element.27), channel_id=1, source_target_pairs={{64,0},{128,64},{192,128},{256,192},{320,256},{384,320},{448,384},... | collective-permute-start | bytes 442376 | tf_op jit(solution)/shard_map/ppermute | solution.py:492
  59.5 0.7 slice.14
  60.3 1.0 collective-permute-done
  61.2 3.8 %collective-permute-done.1 = f32[32,9,1,128]{3,2,1,0:T(1,128)S(1)} collective-permute-done((f32[32,9,1,128]{3,2,1,0:T(1,128)S(1)}, f32[32,9,1,128]{3,2,1,0:T(1,128)S(1)}, u32[]{:S(2)}, u32[]{:S(2)}) %collective-permute-start.1) | collective-permute-done | bytes 147488 | tf_op jit(solution)/shard_map/ppermute | solution.py:492
  65.1 0.3 pad_maximum_fusion
  65.4 0.0 copy-start.11
  65.4 3.2 %collective-permute-start.2 = (f32[32,19,1,128]{3,2,1,0:T(1,128)S(1)}, f32[32,19,1,128]{3,2,1,0:T(1,128)S(1)}, u32[]{:S(2)}, u32[]{:S(2)}) collective-permute-start(f32[32,19,1,128]{3,2,1,0:T(1,128)S(1)} %pad_maximum_fusion), channel_id=1, source_target_pairs={{0,1},{1,0},{2,3},{3,2},{4,5},{5,4},{6,7},{7,6},{8,9},{9,8},{10,11... | collective-permute-start | bytes 933896 | tf_op jit(solution)/shard_map/ppermute | solution.py:494
  68.6 1.2 collective-permute-done.2
  69.8 0.0 copy-start.14
  69.8 0.7 copy-done.14
  70.5 0.0 copy-done.11
  70.5 3.4 %shard_map.159.inflow = f32[9,128,128]{2,1,0:T(8,128)} custom-call(s32[1]{0:T(128)} %bitcast.refs_0_.place, f32[128,1152]{1,0:T(8,128)} %constant.28.clone.wide.refs_2_.weights, f32[27,1152]{1,0:T(8,128)} %constant.30.clone.table, s32[1,64]{1,0:T(1,128)} %index_west.3, s32[1,64]{1,0:T(1,128)} %index_east.3, f32[608,128]{1,0:T(8,128)} %bitcast.31, ...), custom_call_target="tpu_custom_call" | custom-call | flops 60000000 | bytes 3000000 | tf_op jit(solution)/shard_map/pallas_call | solution.py:434
  74.0 2.0 %all-to-all-done.1 = f32[64,20,1,128]{3,2,1,0:T(1,128)S(1)} async-done(((f32[64,20,1,128]{3,2,1,0:T(1,128)}), f32[64,20,1,128]{3,2,1,0:T(1,128)S(1)}, u32[]{:S(2)}, u32[]{:S(2)}) %all-to-all-start.1) | async-done | bytes 655392 | tf_op jit(solution)/shard_map/all_to_all | solution.py:453
  76.0 0.0 copy-start.1
  76.0 0.0 copy-done
  76.0 0.0 copy-done.3
  76.0 0.0 copy-done.5
  76.0 0.0 copy-done.6
  76.0 0.0 copy-done.7
  76.0 0.0 copy-start.2
  76.0 1.1 copy-done.2
  77.2 0.0 copy-start.4
  77.2 0.0 copy-start.8
  77.2 0.0 copy-start.9
  77.2 1.5 %shard_map.161 = (f32[9,64,128]{2,1,0:T(8,128)S(1)}, f32[9,64,128]{2,1,0:T(8,128)S(1)}) custom-call(s32[1]{0:T(128)} %bitcast.refs_0_.place, s32[64,128]{1,0:T(8,128)S(1)} %bitcast.24, f32[1,36]{1,0:T(1,128)S(1)} %bitcast.27, f32[1,36]{1,0:T(1,128)S(1)} %bitcast.29, f32[27,1152]{1,0:T(8,128)S(1)} %copy-done.3, f32[9,128,128]{2,1,0:T(8,128)S(1)} %copy-done.2, ...), custom_call_target="tpu_custom_call" | custom-call | flops 400000000 | bytes 7000000 | tf_op jit(solution)/shard_map/pallas_call | solution.py:434
  78.7 3.3 %collective-permute-start.5 = (f32[9,64,128]{2,1,0:T(8,128)S(1)}, f32[9,64,128]{2,1,0:T(8,128)S(1)}, u32[]{:S(2)}, u32[]{:S(2)}) collective-permute-start(f32[9,64,128]{2,1,0:T(8,128)S(1)} %get-tuple-element.14.far), channel_id=1, source_target_pairs={{0,1},{1,2},{2,3},{3,4},{4,5},{5,6},{6,7},{7,8},{8,9},{9,10},{10,1... | collective-permute-start | bytes 884744 | tf_op jit(solution)/shard_map/ppermute | solution.py:528
  82.1 2.1 %collective-permute-start.6 = (f32[9,64,128]{2,1,0:T(8,128)S(1)}, f32[9,64,128]{2,1,0:T(8,128)S(1)}, u32[]{:S(2)}, u32[]{:S(2)}) collective-permute-start(f32[9,64,128]{2,1,0:T(8,128)S(1)} %get-tuple-element.13.near), channel_id=1, source_target_pairs={{1,0},{2,1},{3,2},{4,3},{5,4},{6,5},{7,6},{8,7},{9,8},{10,9},{11,1... | collective-permute-start | bytes 884744 | tf_op jit(solution)/shard_map/ppermute | solution.py:529
  84.2 0.0 copy-done.1
  84.2 0.0 copy-done.4
  84.2 1.6 %shard_map.162 = (f32[9,128,128]{2,1,0:T(8,128)S(1)}, f32[9,128,128]{2,1,0:T(8,128)S(1)}, f32[128,128]{1,0:T(8,128)S(1)}) custom-call(f32[1280,128]{1,0:T(8,128)S(1)} %bitcast.21, f32[9,64,128]{2,1,0:T(8,128)S(1)} %get-tuple-element.13.near, f32[9,64,128]{2,1,0:T(8,128)S(1)} %get-tuple-element.14.far, f32[128,1152]{1,0:T(8,128)S(1)} %copy-done.1, ...), custom_call_target="tpu_custom_call" | custom-call | flops 100000000 | bytes 4000000 | tf_op jit(solution)/shard_map/pallas_call | solution.py:434
  85.7 0.0 copy-start.15
  85.8 0.0 collective-permute-done.5.from_west
  85.8 4.3 %collective-permute-done.6.from_east = f32[9,64,128]{2,1,0:T(8,128)S(1)} collective-permute-done((f32[9,64,128]{2,1,0:T(8,128)S(1)}, f32[9,64,128]{2,1,0:T(8,128)S(1)}, u32[]{:S(2)}, u32[]{:S(2)}) %collective-permute-start.6) | collective-permute-done | bytes 294944 | tf_op jit(solution)/shard_map/ppermute | solution.py:529
  90.1 0.0 copy-done.8
  90.1 0.0 copy-done.9
  90.1 2.2 %shard_map.163 = f32[1280,128]{1,0:T(8,128)} custom-call(s32[1]{0:T(128)} %bitcast.refs_0_.place, f32[9,64,128]{2,1,0:T(8,128)S(1)} %get-tuple-element.13.near, f32[9,64,128]{2,1,0:T(8,128)S(1)} %get-tuple-element.14.far, f32[9,64,128]{2,1,0:T(8,128)S(1)} %collective-permute-done.5.from_west, f32[9,64,128]{2,1,0:T(8,128)S(1)} %collective-permute-done.6.from_east, ...), custom_call_target="tpu_custom_call" | custom-call | flops 10000000 | bytes 5000000 | tf_op jit(solution)/shard_map/pallas_call | solution.py:434
  92.3 8.4 %all-to-all-start.2 = ((f32[64,20,1,128]{3,2,1,0:T(1,128)}), f32[64,20,1,128]{3,2,1,0:T(1,128)S(1)}, u32[]{:S(2)}, u32[]{:S(2)}) async-start(f32[64,20,1,128]{3,2,1,0:T(1,128)} %bitcast.13), calls=%async_computation.2 | async-start | bytes 1310720 | tf_op jit(solution)/shard_map/all_to_all | solution.py:453
  100.8 0.0 copy-done.15
  100.8 0.6 dynamic_slice.6.ahead
  101.4 0.7 constant_dynamic-slice_fusion.scalars
  102.1 18.8 %all-to-all-done.2 = f32[64,20,1,128]{3,2,1,0:T(1,128)S(1)} async-done(((f32[64,20,1,128]{3,2,1,0:T(1,128)}), f32[64,20,1,128]{3,2,1,0:T(1,128)S(1)}, u32[]{:S(2)}, u32[]{:S(2)}) %all-to-all-start.2) | async-done | bytes 655392 | tf_op jit(solution)/shard_map/all_to_all | solution.py:453
  120.9 3.1 %shard_map.164 = (f32[1152,128]{1,0:T(8,128)}, f32[128,128]{1,0:T(8,128)}) custom-call(s32[1]{0:T(128)} %dynamic_slice.6.ahead, f32[1,144]{1,0:T(1,128)S(1)} %constant_dynamic-slice_fusion.scalars, f32[1280,128]{1,0:T(8,128)S(1)} %bitcast.22, s32[64,128]{1,0:T(8,128)S(1)} %bitcast.25), custom_call_target="tpu_custom_call" | custom-call | flops 100000000 | bytes 2000000 | tf_op jit(solution)/shard_map/pallas_call | solution.py:434
Async XLA Ops:
  5.9 39.0 %all-to-all-start = ((f32[32,19,1,128]{3,2,1,0:T(1,128)}), f32[32,19,1,128]{3,2,1,0:T(1,128)S(1)}, u32[]{:S(2)}, u32[]{:S(2)}) async-start(f32[32,19,1,128]{3,2,1,0:T(1,128)} %bitcast.33), calls=%async_computation | async-start | bytes 622592 | tf_op jit(solution)/shard_map/all_to_all | solution.py:453
  16.4 19.2 %collective-permute-start.3 = (f32[9,128,128]{2,1,0:T(8,128)}, f32[9,128,128]{2,1,0:T(8,128)S(1)}, u32[]{:S(2)}, u32[]{:S(2)}) collective-permute-start(f32[9,128,128]{2,1,0:T(8,128)} %get-tuple-element.12.refs_4_), channel_id=1, source_target_pairs={{0,1},{1,2},{2,3},{3,4},{4,5},{5,6},{6,7},{7,8},{8,9},{9,10},{10,1... | collective-permute-start | bytes 1769480 | tf_op jit(solution)/shard_map/ppermute | solution.py:477
  27.1 11.4 %collective-permute-start.4 = (f32[9,128,128]{2,1,0:T(8,128)}, f32[9,128,128]{2,1,0:T(8,128)S(1)}, u32[]{:S(2)}, u32[]{:S(2)}) collective-permute-start(f32[9,128,128]{2,1,0:T(8,128)} %get-tuple-element.12.refs_4_), channel_id=1, source_target_pairs={{1,0},{2,1},{3,2},{4,3},{5,4},{6,5},{7,6},{8,7},{9,8},{10,9},{11,1... | collective-permute-start | bytes 1769480 | tf_op jit(solution)/shard_map/ppermute | solution.py:478
  35.5 3.0 %copy-start.12 = (f32[9,128,128]{2,1,0:T(8,128)}, f32[9,128,128]{2,1,0:T(8,128)S(1)}, u32[]{:S(2)}) copy-start(f32[9,128,128]{2,1,0:T(8,128)S(1)} %collective-permute-done.3.refs_5_) | copy-start | bytes 1769476
  38.5 0.8 copy-start.13
  44.8 31.2 %copy-start = (bf16[1152,1152]{1,0:T(8,128)(2,1)S(1)}, bf16[1152,1152]{1,0:T(8,128)(2,1)}, u32[]{:S(2)}) copy-start(bf16[1152,1152]{1,0:T(8,128)(2,1)} %transfer.1) | copy-start | bytes 7962628
  44.8 31.2 %copy-start.3 = (f32[27,1152]{1,0:T(8,128)S(1)}, f32[27,1152]{1,0:T(8,128)}, u32[]{:S(2)}) copy-start(f32[27,1152]{1,0:T(8,128)} %constant.30.clone.table) | copy-start | bytes 373252
  44.8 31.2 %copy-start.5 = (s32[1,64,128]{2,1,0:T(8,128)S(1)}, s32[1,64,128]{2,1,0:T(8,128)}, u32[]{:S(2)}) copy-start(s32[1,64,128]{2,1,0:T(8,128)} %param.16) | copy-start | bytes 98308
  44.8 31.2 %copy-start.6 = (f32[36]{0:T(128)S(1)}, f32[36]{0:T(128)}, u32[]{:S(2)}) copy-start(f32[36]{0:T(128)} %param.22) | copy-start | bytes 436
  44.9 31.2 %copy-start.7 = (f32[36]{0:T(128)S(1)}, f32[36]{0:T(128)}, u32[]{:S(2)}) copy-start(f32[36]{0:T(128)} %param.23) | copy-start | bytes 436
  44.9 0.7 copy-start.10
  45.6 30.4 %all-to-all-start.1 = ((f32[64,20,1,128]{3,2,1,0:T(1,128)}), f32[64,20,1,128]{3,2,1,0:T(1,128)S(1)}, u32[]{:S(2)}, u32[]{:S(2)}) async-start(f32[64,20,1,128]{3,2,1,0:T(1,128)} %bitcast.30), calls=%async_computation.1 | async-start | bytes 1310720 | tf_op jit(solution)/shard_map/all_to_all | solution.py:453
  56.9 4.3 %collective-permute-start = (f32[32,9,1,128]{3,2,1,0:T(1,128)S(1)}, f32[32,9,1,128]{3,2,1,0:T(1,128)S(1)}, u32[]{:S(2)}, u32[]{:S(2)}) collective-permute-start(f32[32,9,1,128]{3,2,1,0:T(1,128)S(1)} %get-tuple-element.26), channel_id=1, source_target_pairs={{0,64},{64,128},{128,192},{192,256},{256,320},{320,384},{384,448},... | collective-permute-start | bytes 442376 | tf_op jit(solution)/shard_map/ppermute | solution.py:491
  58.2 6.8 %collective-permute-start.1 = (f32[32,9,1,128]{3,2,1,0:T(1,128)S(1)}, f32[32,9,1,128]{3,2,1,0:T(1,128)S(1)}, u32[]{:S(2)}, u32[]{:S(2)}) collective-permute-start(f32[32,9,1,128]{3,2,1,0:T(1,128)S(1)} %get-tuple-element.27), channel_id=1, source_target_pairs={{64,0},{128,64},{192,128},{256,192},{320,256},{384,320},{448,384},... | collective-permute-start | bytes 442376 | tf_op jit(solution)/shard_map/ppermute | solution.py:492
  65.4 5.2 %copy-start.11 = (f32[32,19,1,128]{3,2,1,0:T(1,128)}, f32[32,19,1,128]{3,2,1,0:T(1,128)S(1)}, u32[]{:S(2)}) copy-start(f32[32,19,1,128]{3,2,1,0:T(1,128)S(1)} %pad_maximum_fusion) | copy-start | bytes 933892
  65.4 4.4 %collective-permute-start.2 = (f32[32,19,1,128]{3,2,1,0:T(1,128)S(1)}, f32[32,19,1,128]{3,2,1,0:T(1,128)S(1)}, u32[]{:S(2)}, u32[]{:S(2)}) collective-permute-start(f32[32,19,1,128]{3,2,1,0:T(1,128)S(1)} %pad_maximum_fusion), channel_id=1, source_target_pairs={{0,1},{1,0},{2,3},{3,2},{4,5},{5,4},{6,7},{7,6},{8,9},{9,8},{10,11... | collective-permute-start | bytes 933896 | tf_op jit(solution)/shard_map/ppermute | solution.py:494
  69.8 0.7 copy-start.14
  76.0 8.2 %copy-start.1 = (f32[128,1152]{1,0:T(8,128)S(1)}, f32[128,1152]{1,0:T(8,128)}, u32[]{:S(2)}) copy-start(f32[128,1152]{1,0:T(8,128)} %constant.28.clone.wide.refs_2_.weights) | copy-start | bytes 1769476
  76.0 1.1 copy-start.2
  77.2 7.0 %copy-start.4 = (f32[1152,128]{1,0:T(8,128)S(1)}, f32[1152,128]{1,0:T(8,128)}, u32[]{:S(2)}) copy-start(f32[1152,128]{1,0:T(8,128)} %constant.31.clone.stokes_table) | copy-start | bytes 1769476
  77.2 12.9 %copy-start.8 = (s32[1,64]{1,0:T(1,128)S(1)}, s32[1,64]{1,0:T(1,128)}, u32[]{:S(2)}) copy-start(s32[1,64]{1,0:T(1,128)} %index_west.3) | copy-start | bytes 772
  77.2 12.9 %copy-start.9 = (s32[1,64]{1,0:T(1,128)S(1)}, s32[1,64]{1,0:T(1,128)}, u32[]{:S(2)}) copy-start(s32[1,64]{1,0:T(1,128)} %index_east.3) | copy-start | bytes 772
  78.7 7.1 %collective-permute-start.5 = (f32[9,64,128]{2,1,0:T(8,128)S(1)}, f32[9,64,128]{2,1,0:T(8,128)S(1)}, u32[]{:S(2)}, u32[]{:S(2)}) collective-permute-start(f32[9,64,128]{2,1,0:T(8,128)S(1)} %get-tuple-element.14.far), channel_id=1, source_target_pairs={{0,1},{1,2},{2,3},{3,4},{4,5},{5,6},{6,7},{7,8},{8,9},{9,10},{10,1... | collective-permute-start | bytes 884744 | tf_op jit(solution)/shard_map/ppermute | solution.py:528
  82.1 8.0 %collective-permute-start.6 = (f32[9,64,128]{2,1,0:T(8,128)S(1)}, f32[9,64,128]{2,1,0:T(8,128)S(1)}, u32[]{:S(2)}, u32[]{:S(2)}) collective-permute-start(f32[9,64,128]{2,1,0:T(8,128)S(1)} %get-tuple-element.13.near), channel_id=1, source_target_pairs={{1,0},{2,1},{3,2},{4,3},{5,4},{6,5},{7,6},{8,7},{9,8},{10,9},{11,1... | collective-permute-start | bytes 884744 | tf_op jit(solution)/shard_map/ppermute | solution.py:529
  85.7 15.0 %copy-start.15 = (s32[32]{0:T(128)S(1)}, s32[32]{0:T(128)}, u32[]{:S(2)}) copy-start(s32[32]{0:T(128)} %constant.33.clone) | copy-start | bytes 388
  92.3 28.5 %all-to-all-start.2 = ((f32[64,20,1,128]{3,2,1,0:T(1,128)}), f32[64,20,1,128]{3,2,1,0:T(1,128)S(1)}, u32[]{:S(2)}, u32[]{:S(2)}) async-start(f32[64,20,1,128]{3,2,1,0:T(1,128)} %bitcast.13), calls=%async_computation.2 | async-start | bytes 1310720 | tf_op jit(solution)/shard_map/all_to_all | solution.py:453
